TPU v7x, 32 devices: a whole 2x2x4 slice. The times are simulated.
32 devices in a mesh: lat: 4 (over y, core), lon: 8 (over z, x).
Axes of the slice: x: 2, y: 2, z: 4, core: 2. Of those that a mesh axis runs over, the one named last changes fastest.
Arguments:
- noisy: float32 [8, 512, 3072], P(None, 'lat', 'lon'), may hold values from -6 to 6
- coarse: float32 [8, 512, 3072], P(None, 'lat', 'lon'), may hold values from -6 to 6
- step_noise: float32 [8, 512, 3072], P(None, 'lat', 'lon'), may hold values from -6 to 6
- timestep: int32 [1], replicated, may hold values from 985 to 999
- w_time: float32 [128, 1408], replicated, may hold values from -0.5 to 0.5
- w_embed: bfloat16 [64, 64], replicated, may hold values from -0.75 to 0.75
- w_enc1: bfloat16 [576, 64], replicated, may hold values from -0.25 to 0.25
- w_down1: bfloat16 [256, 128], replicated, may hold values from -0.375 to 0.375
- w_enc2: bfloat16 [1152, 128], replicated, may hold values from -0.1875 to 0.1875
- w_down2: bfloat16 [512, 256], replicated, may hold values from -0.25 to 0.25
- w_enc3: bfloat16 [2304, 256], replicated, may hold values from -0.125 to 0.125
- w_down3: bfloat16 [1024, 512], replicated, may hold values from -0.1875 to 0.1875
- w_qkv: bfloat16 [512, 1536], replicated, may hold values from -3 to 3
- w_attn_out: bfloat16 [512, 512], replicated, may hold values from -0.25 to 0.25
- w_up3: bfloat16 [512, 1024], replicated, may hold values from -0.25 to 0.25
- w_dec3: bfloat16 [2304, 256], replicated, may hold values from -0.375 to 0.375
- w_up2: bfloat16 [256, 512], replicated, may hold values from -0.375 to 0.375
- w_dec2: bfloat16 [1152, 128], replicated, may hold values from -0.5 to 0.5
- w_up1: bfloat16 [128, 256], replicated, may hold values from -0.5 to 0.5
- w_dec1: bfloat16 [576, 64], replicated, may hold values from -0.75 to 0.75
- w_head: bfloat16 [64, 32], replicated, may hold values from -0.75 to 0.75
Outputs:
- denoised: float32 [8, 512, 3072], P(None, 'lat', 'lon')
All inputs are finite; a program needn't handle non-finite values.
Results may differ from a plain program's by a relative error of at most 0.025.
Values may be sent and summed in bfloat16 or wider, within the bound.
No kernel may reach another device: no remote copies, remote signals or barrier semaphores. Data moves between devices by JAX's collectives and lax.ppermute only.
A program may use at most 128 MiB of HBM per device.

v0:
```python
import functools
import math

import jax
import jax.numpy as jnp
from jax import lax
from jax.experimental import pallas as pl
from jax.experimental.pallas import tpu as pltpu
from jax.sharding import PartitionSpec as P

HEAD_DIM = 64
T_STEPS = 1000
BF = jnp.bfloat16
F32 = jnp.float32
EPS = 1e-06


def plan(step):
    frac = (step.astype(jnp.float32) / T_STEPS + 0.008) / 1.008
    return jnp.cos(frac * (math.pi / 2)) ** 2


def time_embed(timestep, w_time):
    half = w_time.shape[0] // 2
    freqs = jnp.exp(-math.log(10000.0) * jnp.arange(half, dtype=jnp.float32) / half)
    angle = timestep.astype(jnp.float32)[0] * freqs
    feats = jnp.concatenate([jnp.sin(angle), jnp.cos(angle)])[None]
    return jax.nn.silu(jnp.dot(feats, w_time, precision=lax.Precision.HIGHEST))[0]


def update_factors(timestep):
    current_alpha_product = plan(timestep[0])
    abar_prev = plan(timestep[0] - 1)
    beta = jnp.minimum(1.0 - current_alpha_product / abar_prev, 0.999)
    keep = 1.0 / jnp.sqrt(1.0 - beta)
    noise = beta / jnp.sqrt(1.0 - current_alpha_product) * keep
    sigma = jnp.sqrt(beta * (1.0 - abar_prev) / (1.0 - current_alpha_product))
    return jnp.stack([keep, noise, sigma])


def iota(shape, dim):
    return lax.broadcasted_iota(jnp.int32, shape, dim)


def dotf(a, b):
    return jnp.dot(a, b, preferred_element_type=F32)


def mean_matrix(chans):
    size = 256
    same = (iota((size, size), 0) & -chans) == (iota((size, size), 1) & -chans)
    return jnp.where(same, 1.0 / chans, 0.0).astype(BF)


def scaled(x, bias, mean):
    squares = (x * x).astype(BF)
    size = mean.shape[0]
    parts = [dotf(squares[:, i : i + size], mean) for i in range(0, x.shape[1], size)]
    return x * lax.rsqrt(jnp.concatenate(parts, axis=1) + EPS) + bias


def activate(x, bias, mean):
    half = 0.5 * scaled(x, bias, mean)
    return half + half * jnp.tanh(half)


def row_factor(index, low, high, flags):
    return jnp.where(index < low, flags[0], jnp.where(index >= high, flags[1], 1.0))


def put_taps1(ref, parity, k, u):
    size = u.shape[0]
    pairs = [u[:, p * 128 : (p + 1) * 128] for p in range(4)]
    first = iota((size, 128), 1) < 64
    after = pairs[1:] + [pltpu.roll(pairs[0], size - 1, 0)]
    before = [pltpu.roll(pairs[3], 1, 0)] + pairs[:3]
    for p in range(4):
        ref[parity, k, :, p * 256 : p * 256 + 128] = pairs[p].astype(BF)
        ref[parity, k, :, p * 256 + 128 : (p + 1) * 256] = jnp.where(first, after[p], before[p]).astype(BF)


def put_taps(ref, k, u, chans):
    size, lanes = u.shape
    ref[k, :, 0:chans] = pltpu.roll(u[:, lanes - chans :], 1, 0).astype(BF)
    ref[k, :, chans : chans + lanes] = u.astype(BF)
    ref[k, :, chans + lanes :] = pltpu.roll(u[:, :chans], size - 1, 0).astype(BF)


def fill_conv1(out_ref, w_ref):
    chans = w_ref.shape[1]
    twice = jnp.where((iota((chans, 128), 1) & 63) == iota((chans, 128), 0), 1.0, 0.0).astype(BF)
    wide = dotf(w_ref[...], twice)
    left = iota((chans, 128), 1) < 64
    zero = jnp.zeros((chans, 128), F32)
    for t in range(4):
        for ro in range(2):
            a = t - ro
            for j, dx in enumerate((0, 1, 2, -1)):
                halves = []
                for co in range(2):
                    b = dx - co + 1
                    good = 0 <= a < 3 and 0 <= b < 3
                    halves.append(wide[(a * 3 + b) * chans : (a * 3 + b + 1) * chans] if good else zero)
                value = jnp.where(left, halves[0], halves[1]).astype(BF)
                row = t * 256 + j * 64
                out_ref[row : row + 64, ro * 128 : (ro + 1) * 128] = value


def fill_conv2(out_ref, w_ref):
    zero = jnp.zeros((128, 128), BF)
    for a in range(3):
        part = w_ref[a * 384 : (a + 1) * 384, :]
        out_ref[a * 512 : a * 512 + 384, 0:128] = part
        out_ref[a * 512 + 384 : (a + 1) * 512, 0:128] = zero
        out_ref[a * 512 : a * 512 + 128, 128:256] = zero
        out_ref[a * 512 + 128 : (a + 1) * 512, 128:256] = part


def conv1(taps_ref, i, count, w_ref):
    size = taps_ref.shape[2]
    rows = [
        taps_ref[1, pl.ds(i, count)],
        taps_ref[0, pl.ds(i + 1, count)],
        taps_ref[1, pl.ds(i + 1, count)],
        taps_ref[0, pl.ds(i + 2, count)],
    ]
    lhs = [
        jnp.concatenate([r[:, :, p * 256 : (p + 1) * 256].reshape(count * size, 256) for r in rows], axis=1)
        for p in range(4)
    ]
    return dotf(jnp.concatenate(lhs, axis=0), w_ref[...])


def conv(taps_ref, o, count, reach, w_ref):
    size = taps_ref.shape[1]
    rows = [taps_ref[pl.ds(o + a, count)] for a in range(3)]
    lhs = [
        jnp.concatenate(
            [r[:, :, q * 256 : q * 256 + reach].reshape(count * size, reach) for r in rows], axis=1
        )
        for q in range(2)
    ]
    return dotf(jnp.concatenate(lhs, axis=0), w_ref[...])


def loop(count, body):
    def step(i, carry):
        body(i)
        return carry

    lax.fori_loop(0, count, step, 0)


def fill_embed(out_ref, w_ref):
    feats, chans = w_ref.shape
    twice = jnp.where((iota((chans, 128), 1) & 63) == iota((chans, 128), 0), 1.0, 0.0).astype(BF)
    wide = dotf(w_ref[...], twice).astype(BF)
    k = iota((512, feats), 0)
    source = ((k >> 3) & 15) * 4 + (k & 1) * 2 + ((k >> 7) & 1)
    pick = jnp.where(source == iota((512, feats), 1), 1.0, 0.0).astype(BF)
    wide = dotf(pick, wide)
    k = iota((512, 128), 0)
    right = iota((512, 128), 1) >= 64
    same_cell = right == ((k >> 8) == 1)
    for i in range(4):
        keep = same_cell & (((k & 7) >> 1) == i)
        out_ref[:, i * 128 : (i + 1) * 128] = jnp.where(keep, wide, 0.0).astype(BF)


def embed_rows(noisy_ref, coarse_ref, w_ref, turn_ref):
    cols = noisy_ref.shape[2]
    n = cols // 16
    out = []
    for o in range(2):
        block = jnp.concatenate(
            [noisy_ref[:, o * 8 : (o + 1) * 8, :].reshape(64, cols), coarse_ref[:, o * 8 : (o + 1) * 8, :].reshape(64, cols)],
            axis=0,
        )
        turn_ref[o] = block.T
        lhs = [
            jnp.concatenate([turn_ref[o, pl.ds(4 * p + s, n, stride=16), :] for s in range(4)], axis=1)
            for p in range(4)
        ]
        res = dotf(jnp.concatenate(lhs, axis=0).astype(BF), w_ref[...])
        for i in range(4):
            out.append(
                jnp.concatenate([res[p * n : (p + 1) * n, i * 128 : (i + 1) * 128] for p in range(4)], axis=1)
            )
    return out


def embed_edge_kernel(w_ref, noisy_ref, coarse_ref, pay_ref, wide_ref, turn_ref, strip_ref):
    @pl.when(pl.program_id(0) == 0)
    def _():
        fill_embed(wide_ref, w_ref)

    rows = embed_rows(noisy_ref, coarse_ref, wide_ref, turn_ref)
    n = rows[0].shape[0]
    pay_ref[0, 0 : 8 * n, :] = jnp.concatenate(rows, axis=0).astype(BF)
    for j in range(8):
        strip_ref[j : j + 1, :] = rows[j][0:1]
        strip_ref[8 + j : 9 + j, :] = rows[j][n - 1 : n]
    pay_ref[0, 8 * n :, :] = strip_ref[...].astype(BF)


def embed_mid_kernel(w_ref, noisy_ref, coarse_ref, mid_ref, left_ref, right_ref, wide_ref, turn_ref, strip_ref):
    @pl.when(pl.program_id(0) == 0)
    def _():
        fill_embed(wide_ref, w_ref)

    rows = embed_rows(noisy_ref, coarse_ref, wide_ref, turn_ref)
    n = rows[0].shape[0]
    mid_ref[...] = jnp.concatenate(rows, axis=0).astype(BF)
    k = pl.program_id(0)
    base = pl.multiple_of(k * 8, 8)
    strip_ref[0, pl.ds(base, 8), :] = jnp.concatenate([r[0:1] for r in rows], axis=0)
    strip_ref[1, pl.ds(base, 8), :] = jnp.concatenate([r[n - 1 : n] for r in rows], axis=0)

    @pl.when(k == pl.num_programs(0) - 1)
    def _():
        left_ref[...] = strip_ref[0].astype(BF)
        right_ref[...] = strip_ref[1].astype(BF)


def whole(shape):
    return pl.BlockSpec(shape, lambda *_: (0,) * len(shape))


def embed_edges(noisy, coarse, w_embed):
    nvars, rows, cols = noisy.shape
    n = cols // 16
    last = rows // 16 - 1
    field = pl.BlockSpec((nvars, 16, cols), lambda k: (0, k * last, 0))
    return pl.pallas_call(
        embed_edge_kernel,
        name="embed_edges",
        grid=(2,),
        in_specs=[whole(w_embed.shape), field, field],
        out_specs=pl.BlockSpec((1, 8 * n + 16, 512), lambda k: (k, 0, 0)),
        out_shape=jax.ShapeDtypeStruct((2, 8 * n + 16, 512), BF),
        scratch_shapes=[pltpu.VMEM((512, 512), BF), pltpu.VMEM((2, cols, 128), F32), pltpu.VMEM((16, 512), F32)],
    )(w_embed, noisy, coarse)


def embed_middle(noisy, coarse, w_embed):
    nvars, rows, cols = noisy.shape
    n = cols // 16
    steps = rows // 16 - 2
    field = pl.BlockSpec((nvars, 16, cols), lambda k: (0, k + 1, 0))
    return pl.pallas_call(
        embed_mid_kernel,
        name="embed_middle",
        grid=(steps,),
        in_specs=[whole(w_embed.shape), field, field],
        out_specs=[pl.BlockSpec((8 * n, 512), lambda k: (k, 0)), whole((8 * steps, 512)), whole((8 * steps, 512))],
        out_shape=[
            jax.ShapeDtypeStruct((8 * steps * n, 512), BF),
            jax.ShapeDtypeStruct((8 * steps, 512), BF),
            jax.ShapeDtypeStruct((8 * steps, 512), BF),
        ],
        scratch_shapes=[
            pltpu.VMEM((512, 512), BF),
            pltpu.VMEM((2, cols, 128), F32),
            pltpu.VMEM((2, 8 * steps, 512), F32),
        ],
    )(w_embed, noisy, coarse)


def encoder_kernel(
    flags, bias_ref, pay_ref, mid_ref, top_ref, bot_ref, lhalo_ref, rhalo_ref,
    w1_ref, wd1_ref, w2_ref, wd2_ref, w3_ref, wd3_ref,
    e1_ref, e2_ref, e3_ref, d3_ref,
    conv1_ref, conv2_ref, lf_ref, rf_ref, h1_ref, taps1_ref, d1_ref, taps2_ref, d2_ref, taps3_ref,
    *, n, size, rows1,
):
    fill_conv1(conv1_ref, w1_ref)
    fill_conv2(conv2_ref, w2_ref)
    lf_ref[...] = lhalo_ref[...].astype(F32)
    rf_ref[...] = rhalo_ref[...].astype(F32)
    mean1, mean2, mean3 = mean_matrix(64), mean_matrix(128), mean_matrix(256)
    tail = size - n
    place = iota((tail, 512), 0)
    rows2, rows3 = rows1 // 2, rows1 // 4

    def first(x, index):
        full = []
        for j in range(4):
            right = rf_ref[pl.ds(index + j, 1), :]
            left = lf_ref[pl.ds(index + j, 1), :]
            rim = jnp.where(place == 0, right, jnp.where(place == tail - 1, left, 0.0))
            full += [x[j * n : (j + 1) * n], rim]
        h = jnp.concatenate(full, axis=0)
        u = activate(h, bias_ref[0:1, :], mean1)
        k = index // 2
        for j in range(4):
            part = u[j * size : (j + 1) * size] * row_factor(index + j, 8, rows1 + 8, flags)
            h1_ref[j % 2, k + j // 2] = h[j * size : (j + 1) * size].astype(BF)
            put_taps1(taps1_ref, j % 2, k + j // 2, part)

    for j in range(2):
        part = slice(j * 4 * n, (j + 1) * 4 * n)
        first(top_ref[part, :].astype(F32), j * 4)
        first(pay_ref[0, part, :].astype(F32), 8 + j * 4)
        first(pay_ref[1, part, :].astype(F32), rows1 + j * 4)
        first(bot_ref[part, :].astype(F32), rows1 + 8 + j * 4)
    loop((rows1 - 16) // 4, lambda i: first(mid_ref[pl.ds(pl.multiple_of(i * 4 * n, 4 * n), 4 * n), :].astype(F32), 16 + i * 4))

    count = 2

    def second(c):
        i = c * count
        acc = conv1(taps1_ref, i, count, conv1_ref)
        flat = count * size
        merged = []
        for p in range(4):
            halves = []
            for ro in range(2):
                lanes = slice(p * 128, (p + 1) * 128)
                prior = h1_ref[ro, pl.ds(i + 1, count), :, lanes].reshape(flat, 128).astype(F32)
                e = (prior + acc[p * flat : (p + 1) * flat, ro * 128 : (ro + 1) * 128]).astype(BF)
                e1_ref[ro, pl.ds(i, count), :, lanes] = e.reshape(count, size, 128)
                halves.append(e)
            merged.append(jnp.concatenate(halves, axis=1))
        d = dotf(jnp.concatenate(merged, axis=0), wd1_ref[...]).astype(BF)
        d = jnp.concatenate([d[p * flat : (p + 1) * flat] for p in range(4)], axis=1)
        d1_ref[pl.ds(i, count)] = d.reshape(count, size, 512)
        u = activate(d.astype(F32), bias_ref[1:2, :], mean2)
        for j in range(count):
            put_taps(taps2_ref, i + j, u[j * size : (j + 1) * size] * row_factor(i + j, 3, rows2 + 3, flags), 128)

    loop((rows2 + 6) // count, second)

    count2 = 2

    def third(c):
        i = c * count2
        o = 2 * i
        acc = conv(taps2_ref, o, 2 * count2, 512, conv2_ref)
        flat = 2 * count2 * size
        merged = []
        for q in range(2):
            lanes = slice(q * 256, (q + 1) * 256)
            prior = d1_ref[pl.ds(o + 1, 2 * count2), :, lanes].reshape(flat, 256).astype(F32)
            e = (prior + acc[q * flat : (q + 1) * flat]).astype(BF).reshape(2 * count2, size, 256)
            e2_ref[pl.ds(o, 2 * count2), :, lanes] = e
            for j in range(count2):
                merged.append(jnp.concatenate([e[2 * j], e[2 * j + 1]], axis=1))
        d = dotf(jnp.concatenate(merged, axis=0), wd2_ref[...]).astype(BF)
        d = jnp.concatenate([d[: flat // 2], d[flat // 2 :]], axis=1)
        d2_ref[pl.ds(i, count2)] = d.reshape(count2, size, 512)
        u = activate(d.astype(F32), bias_ref[2:3, :], mean3)
        for j in range(count2):
            put_taps(taps3_ref, i + j, u[j * size : (j + 1) * size] * row_factor(i + j, 1, rows3 + 1, flags), 256)

    loop((rows3 + 2) // count2, third)

    def fourth(i):
        o = 4 * i
        acc = conv(taps3_ref, o, 4, 768, w3_ref)
        flat = 4 * size
        acc = jnp.concatenate([acc[:flat], acc[flat:]], axis=1)
        e = (d2_ref[pl.ds(o + 1, 4)].reshape(flat, 512).astype(F32) + acc).astype(BF).reshape(4, size, 512)
        e3_ref[pl.ds(o, 4)] = e
        merged = [jnp.concatenate([e[2 * j], e[2 * j + 1]], axis=1) for j in range(2)]
        d = dotf(jnp.concatenate(merged, axis=0), wd3_ref[...])
        for j in range(2):
            d3_ref[2 * i + j] = d[j * size : j * size + n].astype(BF)

    loop(rows3 // 4, fourth)


def encoder(flags, biases, pay, mid, top, bot, lhalo, rhalo, weights, n, size):
    rows1 = lhalo.shape[0] - 16
    k1, rows2, rows3 = rows1 // 2 + 8, rows1 // 2, rows1 // 4
    vmem = pltpu.VMEM
    return pl.pallas_call(
        functools.partial(encoder_kernel, n=n, size=size, rows1=rows1),
        name="encoder",
        in_specs=[pl.BlockSpec(memory_space=pltpu.SMEM)] + [pl.BlockSpec(memory_space=pltpu.VMEM)] * 13,
        out_specs=[pl.BlockSpec(memory_space=pltpu.VMEM)] * 4,
        out_shape=[
            jax.ShapeDtypeStruct((2, rows2 + 6, size, 512), BF),
            jax.ShapeDtypeStruct((rows2 + 4, size, 512), BF),
            jax.ShapeDtypeStruct((rows3, size, 512), BF),
            jax.ShapeDtypeStruct((rows3 // 2, n, 512), BF),
        ],
        scratch_shapes=[
            vmem((1024, 256), BF),
            vmem((1536, 256), BF),
            vmem((rows1 + 16, 512), F32),
            vmem((rows1 + 16, 512), F32),
            vmem((2, k1, size, 512), BF),
            vmem((2, k1, size, 1024), BF),
            vmem((rows2 + 6, size, 512), BF),
            vmem((rows2 + 6, size, 768), BF),
            vmem((rows3 + 2, size, 512), BF),
            vmem((rows3 + 2, size, 1024), BF),
        ],
    )(flags, biases, pay, mid, top, bot, lhalo, rhalo, *weights)


def attention_kernel(
    x_ref, bias_ref, e3_ref, lhalo_ref, rhalo_ref, wqkv_ref, wout_ref, out_ref, full_ref, mixed_ref, a4_ref, *, n, size
):
    tail = size - n
    place = iota((tail, 512), 0)
    rows, length, width = x_ref.shape
    lf = lhalo_ref[...].astype(F32)
    rf = rhalo_ref[...].astype(F32)
    for r in range(e3_ref.shape[0]):
        rim = jnp.where(place == 0, rf[r : r + 1], jnp.where(place == tail - 1, lf[r : r + 1], 0.0))
        full_ref[r] = jnp.concatenate([e3_ref[r, 0:n, :].astype(F32), rim], axis=0).astype(BF)

    scale = HEAD_DIM**-0.5
    for row in range(rows):
        x = x_ref[row].astype(F32)
        mean = jnp.mean(x * x, axis=1, keepdims=True)
        u = (x * lax.rsqrt(mean + EPS) + bias_ref[3:4, :]).astype(BF)
        qkv = dotf(u, wqkv_ref[...]).astype(BF)
        left = iota((length, 128), 1) < 64
        for h in range(width // 128):
            q = qkv[:, h * 128 : (h + 1) * 128].astype(F32) * scale
            k = qkv[:, width + h * 128 : width + (h + 1) * 128]
            v = qkv[:, 2 * width + h * 128 : 2 * width + (h + 1) * 128]
            outs = []
            for side in range(2):
                mine = left if side == 0 else jnp.logical_not(left)
                qs = jnp.where(mine, q, 0.0).astype(BF)
                s = lax.dot_general(qs, k, (((1,), (1,)), ((), ())), preferred_element_type=F32)
                e = jnp.exp(s - jnp.max(s, axis=1, keepdims=True))
                total = jnp.sum(e, axis=1, keepdims=True)
                outs.append(dotf(e.astype(BF), v) / total)
            mixed_ref[:, h * 128 : (h + 1) * 128] = jnp.where(left, outs[0], outs[1]).astype(BF)
        a4_ref[...] = x + dotf(mixed_ref[...], wout_ref[...])
        for t in range(length // n):
            after = (t * n + n) % length
            before = (t * n - 1) % length
            rim = jnp.where(
                place == 0,
                a4_ref[after : after + 1, :],
                jnp.where(place == tail - 1, a4_ref[before : before + 1, :], 0.0),
            )
            out_ref[t, row] = jnp.concatenate([a4_ref[t * n : (t + 1) * n, :], rim], axis=0).astype(BF)


def attention(x, biases, e3, lhalo, rhalo, w_qkv, w_out, n, size):
    rows, length, width = x.shape
    return pl.pallas_call(
        functools.partial(attention_kernel, n=n, size=size),
        name="attention",
        out_shape=[
            jax.ShapeDtypeStruct((length // n, rows, size, width), BF),
            jax.ShapeDtypeStruct((e3.shape[0], size, width), BF),
        ],
        scratch_shapes=[pltpu.VMEM((length, width), BF), pltpu.VMEM((length, width), F32)],
    )(x, biases, e3, lhalo, rhalo, w_qkv, w_out)


def fill_head(out_ref, w_ref):
    chans, outs = w_ref.shape
    col = iota((outs, 512), 1)
    source = ((col >> 3) & 7) * 4 + (col & 1) * 2 + ((col >> 7) & 1)
    pick = jnp.where(source == iota((outs, 512), 0), 1.0, 0.0).astype(BF)
    wide = dotf(w_ref[...], pick)
    col = iota((chans, 512), 1)
    for o in range(2):
        for i in range(4):
            for c in range(2):
                keep = (((col >> 6) & 1) == o) & (((col & 7) >> 1) == i) & ((col >> 8) == c)
                row = o * 512 + i * 128 + c * 64
                out_ref[row : row + 64, :] = jnp.where(keep, wide, 0.0).astype(BF)


def decoder_kernel(
    flags, factors, bias_ref, a4_ref, e3_ref, top_ref, bot_ref, e2_ref, e1_ref,
    wu3_ref, w3_ref, wu2_ref, w2_ref, wu1_ref, w1_ref, wh_ref, noisy_ref, noise_ref,
    out_ref,
    conv1_ref, conv2_ref, head_ref, h3_ref, taps3_ref, h2_ref, taps2_ref, h1_ref, taps1_ref, turn_ref,
    *, n, size, rows1,
):
    rows2, rows3 = rows1 // 2, rows1 // 4
    rows4 = rows1 // 8
    step = pl.program_id(0)

    def prepare():
        fill_conv1(conv1_ref, w1_ref)
        fill_conv2(conv2_ref, w2_ref)
        fill_head(head_ref, wh_ref)
        mean1, mean2, mean3 = mean_matrix(64), mean_matrix(128), mean_matrix(256)

        def third(a, e, index):
            count = a.shape[0]
            spread = dotf(a.reshape(count * size, 512), wu3_ref[...])
            for j in range(count):
                for ro in range(2):
                    part = spread[j * size : (j + 1) * size, ro * 512 : (ro + 1) * 512]
                    h = (part + e[2 * j + ro].astype(F32)).astype(BF)
                    row = 2 * (index + j) + ro
                    h3_ref[row] = h
                    u = activate(h.astype(F32), bias_ref[4:5, :], mean3)
                    put_taps(taps3_ref, row, u * row_factor(row, 2, rows3 + 2, flags), 256)

        third(top_ref[0:1], top_ref[1:3], 0)
        third(bot_ref[0:1], bot_ref[1:3], rows4 + 1)
        loop(rows4 // 2, lambda i: third(a4_ref[pl.ds(2 * i, 2)], e3_ref[pl.ds(4 * i, 4)], 1 + 2 * i))

        count3 = 2

        def second(c):
            o = c * count3
            acc = conv(taps3_ref, o, count3, 768, w3_ref)
            flat = count3 * size
            g = []
            for q in range(2):
                prior = h3_ref[pl.ds(o + 1, count3), :, q * 256 : (q + 1) * 256].reshape(flat, 256).astype(F32)
                g.append((prior + acc[q * flat : (q + 1) * flat]).astype(BF))
            spread = dotf(jnp.concatenate(g, axis=0), wu2_ref[...])
            for j in range(count3):
                for ro in range(2):
                    part = [
                        spread[q * flat + j * size : q * flat + (j + 1) * size, ro * 256 : (ro + 1) * 256]
                        for q in range(2)
                    ]
                    row = 2 * (o + j) + ro
                    h = (jnp.concatenate(part, axis=1) + e2_ref[row].astype(F32)).astype(BF)
                    h2_ref[row] = h
                    u = activate(h.astype(F32), bias_ref[5:6, :], mean2)
                    put_taps(taps2_ref, row, u * row_factor(row, 2, rows2 + 2, flags), 128)

        loop((rows3 + 2) // count3, second)

        count2 = 2

        def first(c):
            o = c * count2
            acc = conv(taps2_ref, o, count2, 512, conv2_ref)
            flat = count2 * size
            g = []
            for q in range(2):
                prior = h2_ref[pl.ds(o + 1, count2), :, q * 256 : (q + 1) * 256].reshape(flat, 256).astype(F32)
                both = (prior + acc[q * flat : (q + 1) * flat]).astype(BF)
                g += [both[:, :128], both[:, 128:]]
            spread = dotf(jnp.concatenate(g, axis=0), wu1_ref[...])
            for j in range(count2):
                for ro in range(2):
                    part = [
                        spread[p * flat + j * size : p * flat + (j + 1) * size, ro * 128 : (ro + 1) * 128]
                        for p in range(4)
                    ]
                    h = (jnp.concatenate(part, axis=1) + e1_ref[ro, o + j + 2].astype(F32)).astype(BF)
                    h1_ref[ro, o + j] = h
                    u = activate(h.astype(F32), bias_ref[6:7, :], mean1)
                    row = 2 * (o + j) + ro
                    put_taps1(taps1_ref, ro, o + j, u * row_factor(row, 2, rows1 + 2, flags))

        loop((rows2 + 2) // count2, first)

    pl.when(step == 0)(prepare)

    i = step * 4
    acc = conv1(taps1_ref, i, 4, conv1_ref)
    flat = 4 * size
    octets = []
    g = []
    for p in range(4):
        halves = []
        for ro in range(2):
            prior = h1_ref[ro, pl.ds(i + 1, 4), :, p * 128 : (p + 1) * 128].reshape(flat, 128).astype(F32)
            halves.append((prior + acc[p * flat : (p + 1) * flat, ro * 128 : (ro + 1) * 128]).astype(BF))
        both = jnp.concatenate(halves, axis=1)
        g.append(jnp.concatenate([both[j * size : (j + 1) * size] for j in range(4)], axis=1))
    spread = dotf(jnp.concatenate(g, axis=0), head_ref[...])
    for p in range(4):
        for s in range(4):
            turn_ref[pl.ds(4 * p + s, n, stride=16), :] = spread[p * size : p * size + n, s * 128 : (s + 1) * 128]
    eps = turn_ref[...].T
    nvars, _, cols = noisy_ref.shape
    for o in range(2):
        part = eps[o * 64 : (o + 1) * 64].reshape(nvars, 8, cols)
        rows = slice(o * 8, (o + 1) * 8)
        out_ref[:, rows, :] = factors[0] * noisy_ref[:, rows, :] - factors[1] * part + factors[2] * noise_ref[:, rows, :]


def decoder(flags, factors, biases, a4, e3, top, bot, e2, e1, weights, noisy, step_noise, n, size):
    nvars, lat, cols = noisy.shape
    rows1 = lat // 2
    rows2, rows3 = rows1 // 2, rows1 // 4
    field = pl.BlockSpec((nvars, 16, cols), lambda k: (0, k, 0))
    smem = pl.BlockSpec(memory_space=pltpu.SMEM)
    vmem = pltpu.VMEM
    return pl.pallas_call(
        functools.partial(decoder_kernel, n=n, size=size, rows1=rows1),
        name="decoder",
        grid=(rows1 // 8,),
        in_specs=[smem, smem] + [pl.BlockSpec(memory_space=pltpu.VMEM)] * 14 + [field, field],
        out_specs=field,
        out_shape=jax.ShapeDtypeStruct(noisy.shape, F32),
        scratch_shapes=[
            vmem((1024, 256), BF),
            vmem((1536, 256), BF),
            vmem((1024, 512), BF),
            vmem((rows3 + 4, size, 512), BF),
            vmem((rows3 + 4, size, 1024), BF),
            vmem((rows2 + 4, size, 512), BF),
            vmem((rows2 + 4, size, 768), BF),
            vmem((2, rows2 + 2, size, 512), BF),
            vmem((2, rows2 + 2, size, 1024), BF),
            vmem((cols, 128), F32),
        ],
    )(flags, factors, biases, a4, e3, top, bot, e2, e1, *weights, noisy, step_noise)


def shift(array, axis, by, closed):
    count = lax.axis_size(axis)
    if closed:
        pairs = [(i, (i + by) % count) for i in range(count)]
    else:
        pairs = [(i, i + by) for i in range(count) if 0 <= i + by < count]
    return lax.ppermute(array, axis, pairs)


def body(
    noisy, coarse, step_noise, timestep, w_time, w_embed, w_enc1, w_down1, w_enc2, w_down2, w_enc3, w_down3,
    w_qkv, w_attn_out, w_up3, w_dec3, w_up2, w_dec2, w_up1, w_dec1, w_head,
):
    nvars, lat, cols = noisy.shape
    n = cols // 16
    size = -(-(n + 2) // 16) * 16
    rows1 = lat // 2
    rows4 = lat // 16
    groups = lax.axis_size("lon")
    lat_at, lat_count = lax.axis_index("lat"), lax.axis_size("lat")
    flags = jnp.stack([lat_at > 0, lat_at < lat_count - 1]).astype(F32)

    pay = embed_edges(noisy, coarse, w_embed)
    from_top = shift(pay[1], "lat", 1, False)
    from_bot = shift(pay[0], "lat", -1, False)
    mid, mid_left, mid_right = embed_middle(noisy, coarse, w_embed)

    temb = time_embed(timestep, w_time)
    factors = update_factors(timestep)
    widths = [w_enc1.shape[1], w_enc2.shape[1], w_enc3.shape[1], w_qkv.shape[0], w_dec3.shape[1], w_dec2.shape[1], w_dec1.shape[1]]
    starts = [sum(widths[:i]) for i in range(7)]
    biases = jnp.stack([jnp.tile(temb[s : s + w], 512 // w) for s, w in zip(starts, widths)])

    cut = 8 * n
    left = jnp.concatenate([from_top[cut : cut + 8], pay[0, cut : cut + 8], mid_left, pay[1, cut : cut + 8], from_bot[cut : cut + 8]])
    right = jnp.concatenate([from_top[cut + 8 :], pay[0, cut + 8 :], mid_right, pay[1, cut + 8 :], from_bot[cut + 8 :]])
    rhalo = shift(left, "lon", -1, True)
    lhalo = shift(right, "lon", 1, True)

    e1, e2, e3, d3 = encoder(
        flags, biases, pay, mid, from_top, from_bot, lhalo, rhalo,
        (w_enc1, w_down1, w_enc2, w_down2, w_enc3, w_down3), n, size,
    )

    rhalo3 = shift(e3[:, 0], "lon", -1, True)
    lhalo3 = shift(e3[:, n - 1], "lon", 1, True)

    copies = max(1, groups // rows4)
    each = max(1, rows4 // groups)
    sent = jnp.repeat(d3, copies, axis=0) if copies > 1 else d3
    got = lax.all_to_all(sent.reshape(groups, each * n, 512), "lon", split_axis=0, concat_axis=0, tiled=True)
    got = got.reshape(groups, each, n, 512)
    got = got.transpose(1, 0, 2, 3).reshape(each, groups * n, 512) if each > 1 else got.reshape(1, groups * n, 512)
    out, e3 = attention(got, biases, e3, lhalo3, rhalo3, w_qkv, w_attn_out, n, size)
    a4 = lax.all_to_all(out.reshape(groups, each * size, 512), "lon", split_axis=0, concat_axis=0, tiled=True)
    a4 = a4.reshape(groups * each, size, 512)
    if copies > 1:
        a4 = a4.reshape(rows4, copies, size, 512)[:, 0]

    top = shift(jnp.concatenate([a4[-1:], e3[-2:]]), "lat", 1, False)
    bot = shift(jnp.concatenate([a4[:1], e3[:2]]), "lat", -1, False)
    return decoder(
        flags, factors, biases, a4, e3, top, bot, e2, e1,
        (w_up3, w_dec3, w_up2, w_dec2, w_up1, w_dec1, w_head), noisy, step_noise, n, size,
    )


def solution(mesh):
    field = P(None, "lat", "lon")
    return jax.shard_map(
        body, mesh=mesh, in_specs=(field, field, field) + (P(),) * 18, out_specs=field, check_vma=False
    )
```

profile of v0, /device:TPU:1, one launch (start us, length us, event | category | flops | bytes accessed | tf_op | source)
XLA Modules:
  0.0 142.4 jit_solution(18345051634250992110)
XLA Ops:
  0.0 3.1 %embed_edges.1.pay_ref = bf16[2,208,512]{2,1,0:T(8,128)(2,1)} custom-call(bf16[64,64]{1,0:T(8,128)(2,1)} %w_ref.3, f32[8,128,384]{2,1,0:T(8,128)} %noisy_ref.5, f32[8,128,384]{2,1,0:T(8,128)} %coarse_ref.3), custom_call_target="tpu_custom_call" | custom-call | tf_op jit(solution)/shard_map/embed_edges/pallas_call | solution.py:234
  3.1 1.1 slice_bitcast_fusion
  4.2 4.5 %collective-permute-start = (bf16[208,512]{1,0:T(8,128)(2,1)S(1)}, bf16[208,512]{1,0:T(8,128)(2,1)S(1)}, u32[]{:S(2)}, u32[]{:S(2)}) collective-permute-start(bf16[208,512]{1,0:T(8,128)(2,1)S(1)} %get-tuple-element.32), channel_id=1, source_target_pairs={{0,8},{8,16},{16,24},{1,9},{9,17},{17,25},{2,10},{10,18},{18,26},{... | collective-permute-start | bytes 638984 | tf_op jit(solution)/shard_map/ppermute | solution.py:619
  8.7 1.9 %collective-permute-start.1 = (bf16[208,512]{1,0:T(8,128)(2,1)S(1)}, bf16[208,512]{1,0:T(8,128)(2,1)S(1)}, u32[]{:S(2)}, u32[]{:S(2)}) collective-permute-start(bf16[208,512]{1,0:T(8,128)(2,1)S(1)} %get-tuple-element.31), channel_id=1, source_target_pairs={{8,0},{16,8},{24,16},{9,1},{17,9},{25,17},{10,2},{18,10},{26,18},{... | collective-permute-start | bytes 638984 | tf_op jit(solution)/shard_map/ppermute | solution.py:619
  12.1 6.3 %embed_middle.1 = (bf16[1152,512]{1,0:T(8,128)(2,1)}, bf16[48,512]{1,0:T(8,128)(2,1)}, bf16[48,512]{1,0:T(8,128)(2,1)}) custom-call(bf16[64,64]{1,0:T(8,128)(2,1)} %w_ref.3, f32[8,128,384]{2,1,0:T(8,128)} %noisy_ref.5, f32[8,128,384]{2,1,0:T(8,128)} %coarse_ref.3), custom_call_target="tpu_custom_call" | custom-call | tf_op jit(solution)/shard_map/embed_middle/pallas_call | solution.py:250
  20.9 0.8 constant_dynamic-update-slice_fusion.2
  22.5 1.3 collective-permute-start.2
  23.7 3.1 %collective-permute-start.3 = (bf16[80,512]{1,0:T(8,128)(2,1)S(1)}, bf16[80,512]{1,0:T(8,128)(2,1)S(1)}, u32[]{:S(2)}, u32[]{:S(2)}) collective-permute-start(bf16[80,512]{1,0:T(8,128)(2,1)S(1)} %get-tuple-element.35), channel_id=1, source_target_pairs={{0,7},{1,0},{2,1},{3,2},{4,3},{5,4},{6,5},{7,6},{8,15},{9,8},{10,9... | collective-permute-start | bytes 245768 | tf_op jit(solution)/shard_map/ppermute | solution.py:619
  27.5 1.1 collective-permute-done.2.lhalo_ref
  29.3 31.1 %encoder.1 = (bf16[2,38,32,512]{3,2,1,0:T(8,128)(2,1)}, bf16[36,32,512]{2,1,0:T(8,128)(2,1)}, bf16[16,32,512]{2,1,0:T(8,128)(2,1)}, bf16[8,24,512]{2,1,0:T(8,128)(2,1)}) custom-call(f32[2]{0:T(128)} %add_convert_fusion.flags, f32[7,512]{1,0:T(8,128)} %stack.31.bias_ref, bf16[2,208,512]{2,1,0:T(8,128)(2,1)} %embed_edges.1.pay_ref, ...), custom_call_target="tpu_custom_call" | custom-call | tf_op jit(solution)/shard_map/encoder/pallas_call | solution.py:376
  60.4 5.4 %all-to-all-start = ((bf16[8,24,512]{2,1,0:T(8,128)(2,1)}), bf16[8,24,512]{2,1,0:T(8,128)(2,1)S(1)}, u32[]{:S(2)}, u32[]{:S(2)}) async-start(bf16[8,24,512]{2,1,0:T(8,128)(2,1)} %get-tuple-element.17), calls=%async_computation | async-start | bytes 393216 | tf_op jit(solution)/shard_map/all_to_all | solution.py:663
  65.9 1.3 copy.23
  67.2 1.5 %collective-permute-start.4 = (bf16[16,512]{1,0:T(8,128)(2,1)S(1)}, bf16[16,512]{1,0:T(8,128)(2,1)S(1)}, u32[]{:S(2)}, u32[]{:S(2)}) collective-permute-start(bf16[16,512]{1,0:T(8,128)(2,1)S(1)} %get-tuple-element.26), channel_id=1, source_target_pairs={{0,1},{1,2},{2,3},{3,4},{4,5},{5,6},{6,7},{7,0},{8,9},{9,10},{10,1... | collective-permute-start | bytes 49160 | tf_op jit(solution)/shard_map/ppermute | solution.py:619
  68.7 2.8 %collective-permute-start.5 = (bf16[16,512]{1,0:T(8,128)(2,1)S(1)}, bf16[16,512]{1,0:T(8,128)(2,1)S(1)}, u32[]{:S(2)}, u32[]{:S(2)}) collective-permute-start(bf16[16,512]{1,0:T(8,128)(2,1)S(1)} %get-tuple-element.25), channel_id=1, source_target_pairs={{0,7},{1,0},{2,1},{3,2},{4,3},{5,4},{6,5},{7,6},{8,15},{9,8},{10,9... | collective-permute-start | bytes 49160 | tf_op jit(solution)/shard_map/ppermute | solution.py:619
  71.5 3.5 %collective-permute-done.4.lhalo_ref = bf16[16,512]{1,0:T(8,128)(2,1)S(1)} collective-permute-done((bf16[16,512]{1,0:T(8,128)(2,1)S(1)}, bf16[16,512]{1,0:T(8,128)(2,1)S(1)}, u32[]{:S(2)}, u32[]{:S(2)}) %collective-permute-start.4) | collective-permute-done | bytes 16416 | tf_op jit(solution)/shard_map/ppermute | solution.py:619
  75.7 4.1 %attention.1 = (bf16[8,1,32,512]{3,2,1,0:T(8,128)(2,1)}, bf16[16,32,512]{2,1,0:T(8,128)(2,1)}) custom-call(bf16[1,192,512]{2,1,0:T(8,128)(2,1)} %bitcast.59, f32[7,512]{1,0:T(8,128)} %stack.31.bias_ref, bf16[16,32,512]{2,1,0:T(8,128)(2,1)} %get-tuple-element.18.e3_ref, bf16[16,512]{1,0:T(8,128)(2,1)} %copy-done.11, bf16[16,512]{1,0:T(8,128)(2,1)} %copy-done.12, ...), custom_call_target="tpu_custom_call" | custom-call | tf_op jit(solution)/shard_map/attention/pallas_call | solution.py:448
  79.8 3.4 %all-to-all-start.1 = ((bf16[8,32,512]{2,1,0:T(8,128)(2,1)}), bf16[8,32,512]{2,1,0:T(8,128)(2,1)S(1)}, u32[]{:S(2)}, u32[]{:S(2)}) async-start(bf16[8,32,512]{2,1,0:T(8,128)(2,1)} %bitcast.60), calls=%async_computation.1 | async-start | bytes 524288 | tf_op jit(solution)/shard_map/all_to_all | solution.py:667
  83.6 0.8 copy.25.w1_ref
  85.1 0.9 fusion.5
  86.0 4.6 %all-to-all-done.1.a4_ref = bf16[8,32,512]{2,1,0:T(8,128)(2,1)S(1)} async-done(((bf16[8,32,512]{2,1,0:T(8,128)(2,1)}), bf16[8,32,512]{2,1,0:T(8,128)(2,1)S(1)}, u32[]{:S(2)}, u32[]{:S(2)}) %all-to-all-start.1) | async-done | bytes 262176 | tf_op jit(solution)/shard_map/all_to_all | solution.py:667
  90.6 7.4 %collective-permute-start.6 = (bf16[3,32,512]{2,1,0:T(8,128)(2,1)S(1)}, bf16[3,32,512]{2,1,0:T(8,128)(2,1)S(1)}, u32[]{:S(2)}, u32[]{:S(2)}) collective-permute-start(bf16[3,32,512]{2,1,0:T(8,128)(2,1)S(1)} %pad_maximum_fusion), channel_id=1, source_target_pairs={{0,8},{8,16},{16,24},{1,9},{9,17},{17,25},{2,10},{10,18},{18,26},{... | collective-permute-start | bytes 294920 | tf_op jit(solution)/shard_map/ppermute | solution.py:619
  98.1 1.9 %collective-permute-start.7 = (bf16[3,32,512]{2,1,0:T(8,128)(2,1)S(1)}, bf16[3,32,512]{2,1,0:T(8,128)(2,1)S(1)}, u32[]{:S(2)}, u32[]{:S(2)}) collective-permute-start(bf16[3,32,512]{2,1,0:T(8,128)(2,1)S(1)} %pad_maximum_fusion.1), channel_id=1, source_target_pairs={{8,0},{16,8},{24,16},{9,1},{17,9},{25,17},{10,2},{18,10},{26,18},{... | collective-permute-start | bytes 294920 | tf_op jit(solution)/shard_map/ppermute | solution.py:619
  100.6 3.4 %collective-permute-done.7.bot_ref = bf16[3,32,512]{2,1,0:T(8,128)(2,1)S(1)} collective-permute-done((bf16[3,32,512]{2,1,0:T(8,128)(2,1)S(1)}, bf16[3,32,512]{2,1,0:T(8,128)(2,1)S(1)}, u32[]{:S(2)}, u32[]{:S(2)}) %collective-permute-start.7) | collective-permute-done | bytes 98336 | tf_op jit(solution)/shard_map/ppermute | solution.py:619
  104.6 37.8 %decoder.1 = f32[8,128,384]{2,1,0:T(8,128)} custom-call(f32[2]{0:T(128)} %add_convert_fusion.flags, f32[3]{0:T(128)} %pad_maximum_fusion.2.factors, f32[7,512]{1,0:T(8,128)} %stack.31.bias_ref, bf16[8,32,512]{2,1,0:T(8,128)(2,1)} %copy-done.1, bf16[16,32,512]{2,1,0:T(8,128)(2,1)} %get-tuple-element.20.e3_ref, bf16[3,32,512]{2,1,0:T(8,128)(2,1)} %copy-done.5, ...), custom_call_target="tpu_custom_call" | custom-call | tf_op jit(solution)/shard_map/decoder/pallas_call | solution.py:591
  (65 shorter events, 8.0 us)
Async XLA Ops:
  0.0 11.4 %copy-start = (f32[128,1408]{1,0:T(8,128)S(1)}, f32[128,1408]{1,0:T(8,128)}, u32[]{:S(2)}) copy-start(f32[128,1408]{1,0:T(8,128)} %param.25) | copy-start | bytes 2162692
  4.2 16.0 %collective-permute-start = (bf16[208,512]{1,0:T(8,128)(2,1)S(1)}, bf16[208,512]{1,0:T(8,128)(2,1)S(1)}, u32[]{:S(2)}, u32[]{:S(2)}) collective-permute-start(bf16[208,512]{1,0:T(8,128)(2,1)S(1)} %get-tuple-element.32), channel_id=1, source_target_pairs={{0,8},{8,16},{16,24},{1,9},{9,17},{17,25},{2,10},{10,18},{18,26},{... | collective-permute-start | bytes 638984 | tf_op jit(solution)/shard_map/ppermute | solution.py:619
  8.7 13.7 %collective-permute-start.1 = (bf16[208,512]{1,0:T(8,128)(2,1)S(1)}, bf16[208,512]{1,0:T(8,128)(2,1)S(1)}, u32[]{:S(2)}, u32[]{:S(2)}) collective-permute-start(bf16[208,512]{1,0:T(8,128)(2,1)S(1)} %get-tuple-element.31), channel_id=1, source_target_pairs={{8,0},{16,8},{24,16},{9,1},{17,9},{25,17},{10,2},{18,10},{26,18},{... | collective-permute-start | bytes 638984 | tf_op jit(solution)/shard_map/ppermute | solution.py:619
  12.1 6.5 %copy-start.7 = (bf16[576,64]{0,1:T(8,128)(2,1)S(1)}, bf16[576,64]{0,1:T(8,128)(2,1)}, u32[]{:S(2)}) copy-start(bf16[576,64]{0,1:T(8,128)(2,1)} %param.27) | copy-start | bytes 221188
  20.1 8.5 %copy-start.3 = (bf16[208,512]{1,0:T(8,128)(2,1)}, bf16[208,512]{1,0:T(8,128)(2,1)S(1)}, u32[]{:S(2)}) copy-start(bf16[208,512]{1,0:T(8,128)(2,1)S(1)} %collective-permute-done.top_ref) | copy-start | bytes 638980
  22.5 6.2 %copy-start.4 = (bf16[208,512]{1,0:T(8,128)(2,1)}, bf16[208,512]{1,0:T(8,128)(2,1)S(1)}, u32[]{:S(2)}) copy-start(bf16[208,512]{1,0:T(8,128)(2,1)S(1)} %collective-permute-done.1.bot_ref) | copy-start | bytes 638980
  22.5 6.2 %collective-permute-start.2 = (bf16[80,512]{1,0:T(8,128)(2,1)S(1)}, bf16[80,512]{1,0:T(8,128)(2,1)S(1)}, u32[]{:S(2)}, u32[]{:S(2)}) collective-permute-start(bf16[80,512]{1,0:T(8,128)(2,1)S(1)} %get-tuple-element.36), channel_id=1, source_target_pairs={{0,1},{1,2},{2,3},{3,4},{4,5},{5,6},{6,7},{7,0},{8,9},{9,10},{10,1... | collective-permute-start | bytes 245768 | tf_op jit(solution)/shard_map/ppermute | solution.py:619
  23.7 4.9 %collective-permute-start.3 = (bf16[80,512]{1,0:T(8,128)(2,1)S(1)}, bf16[80,512]{1,0:T(8,128)(2,1)S(1)}, u32[]{:S(2)}, u32[]{:S(2)}) collective-permute-start(bf16[80,512]{1,0:T(8,128)(2,1)S(1)} %get-tuple-element.35), channel_id=1, source_target_pairs={{0,7},{1,0},{2,1},{3,2},{4,3},{5,4},{6,5},{7,6},{8,15},{9,8},{10,9... | collective-permute-start | bytes 245768 | tf_op jit(solution)/shard_map/ppermute | solution.py:619
  28.6 0.6 copy-start.9
  28.6 0.7 copy-start.10
  60.4 14.6 %all-to-all-start = ((bf16[8,24,512]{2,1,0:T(8,128)(2,1)}), bf16[8,24,512]{2,1,0:T(8,128)(2,1)S(1)}, u32[]{:S(2)}, u32[]{:S(2)}) async-start(bf16[8,24,512]{2,1,0:T(8,128)(2,1)} %get-tuple-element.17), calls=%async_computation | async-start | bytes 393216 | tf_op jit(solution)/shard_map/all_to_all | solution.py:663
  67.2 7.8 %collective-permute-start.4 = (bf16[16,512]{1,0:T(8,128)(2,1)S(1)}, bf16[16,512]{1,0:T(8,128)(2,1)S(1)}, u32[]{:S(2)}, u32[]{:S(2)}) collective-permute-start(bf16[16,512]{1,0:T(8,128)(2,1)S(1)} %get-tuple-element.26), channel_id=1, source_target_pairs={{0,1},{1,2},{2,3},{3,4},{4,5},{5,6},{6,7},{7,0},{8,9},{9,10},{10,1... | collective-permute-start | bytes 49160 | tf_op jit(solution)/shard_map/ppermute | solution.py:619
  68.7 6.3 %collective-permute-start.5 = (bf16[16,512]{1,0:T(8,128)(2,1)S(1)}, bf16[16,512]{1,0:T(8,128)(2,1)S(1)}, u32[]{:S(2)}, u32[]{:S(2)}) collective-permute-start(bf16[16,512]{1,0:T(8,128)(2,1)S(1)} %get-tuple-element.25), channel_id=1, source_target_pairs={{0,7},{1,0},{2,1},{3,2},{4,3},{5,4},{6,5},{7,6},{8,15},{9,8},{10,9... | collective-permute-start | bytes 49160 | tf_op jit(solution)/shard_map/ppermute | solution.py:619
  75.0 0.6 copy-start.11
  75.0 0.6 copy-start.12
  75.0 0.7 copy-start.2
  75.7 7.9 %copy-start.8 = (bf16[576,64]{0,1:T(8,128)(2,1)S(1)}, bf16[576,64]{0,1:T(8,128)(2,1)}, u32[]{:S(2)}) copy-start(bf16[576,64]{0,1:T(8,128)(2,1)} %param.40) | copy-start | bytes 221188
  75.7 8.7 %copy-start.13 = (bf16[64,32]{0,1:T(8,128)(2,1)S(1)}, bf16[64,32]{0,1:T(8,128)(2,1)}, u32[]{:S(2)}) copy-start(bf16[64,32]{0,1:T(8,128)(2,1)} %param.41) | copy-start | bytes 12292
  79.8 10.8 %all-to-all-start.1 = ((bf16[8,32,512]{2,1,0:T(8,128)(2,1)}), bf16[8,32,512]{2,1,0:T(8,128)(2,1)S(1)}, u32[]{:S(2)}, u32[]{:S(2)}) async-start(bf16[8,32,512]{2,1,0:T(8,128)(2,1)} %bitcast.60), calls=%async_computation.1 | async-start | bytes 524288 | tf_op jit(solution)/shard_map/all_to_all | solution.py:667
  90.6 13.4 %copy-start.1 = (bf16[8,32,512]{2,1,0:T(8,128)(2,1)}, bf16[8,32,512]{2,1,0:T(8,128)(2,1)S(1)}, u32[]{:S(2)}) copy-start(bf16[8,32,512]{2,1,0:T(8,128)(2,1)S(1)} %all-to-all-done.1.a4_ref) | copy-start | bytes 786436
  90.6 10.0 %collective-permute-start.6 = (bf16[3,32,512]{2,1,0:T(8,128)(2,1)S(1)}, bf16[3,32,512]{2,1,0:T(8,128)(2,1)S(1)}, u32[]{:S(2)}, u32[]{:S(2)}) collective-permute-start(bf16[3,32,512]{2,1,0:T(8,128)(2,1)S(1)} %pad_maximum_fusion), channel_id=1, source_target_pairs={{0,8},{8,16},{16,24},{1,9},{9,17},{17,25},{2,10},{10,18},{18,26},{... | collective-permute-start | bytes 294920 | tf_op jit(solution)/shard_map/ppermute | solution.py:619
  98.1 5.9 %collective-permute-start.7 = (bf16[3,32,512]{2,1,0:T(8,128)(2,1)S(1)}, bf16[3,32,512]{2,1,0:T(8,128)(2,1)S(1)}, u32[]{:S(2)}, u32[]{:S(2)}) collective-permute-start(bf16[3,32,512]{2,1,0:T(8,128)(2,1)S(1)} %pad_maximum_fusion.1), channel_id=1, source_target_pairs={{8,0},{16,8},{24,16},{9,1},{17,9},{25,17},{10,2},{18,10},{26,18},{... | collective-permute-start | bytes 294920 | tf_op jit(solution)/shard_map/ppermute | solution.py:619
  100.6 3.4 %copy-start.5 = (bf16[3,32,512]{2,1,0:T(8,128)(2,1)}, bf16[3,32,512]{2,1,0:T(8,128)(2,1)S(1)}, u32[]{:S(2)}) copy-start(bf16[3,32,512]{2,1,0:T(8,128)(2,1)S(1)} %collective-permute-done.6.top_ref) | copy-start | bytes 294916
  104.0 0.6 copy-start.6
where the time goes:
time: 143 us; the launch traced here: 142 us
  Pallas kernels  82.4 us (58%)
  starting transfers between devices  33.3 us (23%)
  waiting for transfers between devices  12.7 us (9%)
  local copies, waits for them, and re-layouts  11 us (8%)
    pallas_call x1, Pallas kernels, decoder(): pl.pallas_call(functools.partial(decoder_kernel, n=n, size=size, rows1=ro...  37.8 us
    pallas_call x1, Pallas kernels, encoder(): pl.pallas_call(functools.partial(encoder_kernel, n=n, size=size, rows1=ro...  31.1 us
    ppermute x8, starting transfers between devices, shift(): return lax.ppermute(array, axis, pairs)  24.4 us
    ppermute x8, waiting for transfers between devices, shift(): return lax.ppermute(array, axis, pairs)  8.05 us
    unnamed x39, local copies, waits for them, and re-layouts  6.62 us
    pallas_call x1, Pallas kernels, embed_middle(): pl.pallas_call(embed_mid_kernel, name='embed_middle', grid=(steps,), in_s...  6.35 us
    all_to_all x1, starting transfers between devices, body(): lax.all_to_all(sent.reshape(groups, each * n, 512), 'lon', split_axis=0,...  5.45 us
    all_to_all x1, waiting for transfers between devices, body(): lax.all_to_all(out.reshape(groups, each * size, 512), 'lon', split_axis=0...  4.63 us
  transfers between devices with their start and end apart: 10, of which 4 were waited for; matrix products, arithmetic and copies ran while one was open for 7% of the time, Pallas kernels for 4%

commit v1 on v0

v1 whole, which is shorter than its diff:
```python
import functools
import math

import jax
import jax.numpy as jnp
from jax import lax
from jax.experimental import pallas as pl
from jax.experimental.pallas import tpu as pltpu
from jax.sharding import PartitionSpec as P

HEAD_DIM = 64
T_STEPS = 1000
BF = jnp.bfloat16
F32 = jnp.float32
EPS = 1e-06


def plan(step):
    frac = (step.astype(jnp.float32) / T_STEPS + 0.008) / 1.008
    return jnp.cos(frac * (math.pi / 2)) ** 2


def time_embed(timestep, w_time):
    half = w_time.shape[0] // 2
    freqs = jnp.exp(-math.log(10000.0) * jnp.arange(half, dtype=jnp.float32) / half)
    angle = timestep.astype(jnp.float32)[0] * freqs
    feats = jnp.concatenate([jnp.sin(angle), jnp.cos(angle)])[None]
    return jax.nn.silu(jnp.dot(feats, w_time, precision=lax.Precision.HIGHEST))[0]


def update_factors(timestep):
    current_alpha_product = plan(timestep[0])
    abar_prev = plan(timestep[0] - 1)
    beta = jnp.minimum(1.0 - current_alpha_product / abar_prev, 0.999)
    keep = 1.0 / jnp.sqrt(1.0 - beta)
    noise = beta / jnp.sqrt(1.0 - current_alpha_product) * keep
    sigma = jnp.sqrt(beta * (1.0 - abar_prev) / (1.0 - current_alpha_product))
    return jnp.stack([keep, noise, sigma])


def iota(shape, dim):
    return lax.broadcasted_iota(jnp.int32, shape, dim)


def dotf(a, b):
    return jnp.dot(a, b, preferred_element_type=F32)


def mean_matrix(chans):
    size = 256
    same = (iota((size, size), 0) & -chans) == (iota((size, size), 1) & -chans)
    return jnp.where(same, 1.0 / chans, 0.0).astype(BF)


def scaled(x, bias, mean):
    squares = (x * x).astype(BF)
    size = mean.shape[0]
    parts = [dotf(squares[:, i : i + size], mean) for i in range(0, x.shape[1], size)]
    return x * lax.rsqrt(jnp.concatenate(parts, axis=1) + EPS) + bias


def activate(x, bias, mean):
    half = 0.5 * scaled(x, bias, mean)
    return half + half * jnp.tanh(half)


def row_factor(index, low, high, flags):
    return jnp.where(index < low, flags[0], jnp.where(index >= high, flags[1], 1.0))


def put_taps1(ref, parity, k, u):
    size = u.shape[0]
    pairs = [u[:, p * 128 : (p + 1) * 128] for p in range(4)]
    first = iota((size, 128), 1) < 64
    after = pairs[1:] + [pltpu.roll(pairs[0], size - 1, 0)]
    before = [pltpu.roll(pairs[3], 1, 0)] + pairs[:3]
    for p in range(4):
        ref[parity, k, :, p * 256 : p * 256 + 128] = pairs[p].astype(BF)
        ref[parity, k, :, p * 256 + 128 : (p + 1) * 256] = jnp.where(first, after[p], before[p]).astype(BF)


def put_taps(ref, k, u, chans):
    size, lanes = u.shape
    ref[k, :, 0:chans] = pltpu.roll(u[:, lanes - chans :], 1, 0).astype(BF)
    ref[k, :, chans : chans + lanes] = u.astype(BF)
    ref[k, :, chans + lanes :] = pltpu.roll(u[:, :chans], size - 1, 0).astype(BF)


def fill_conv1(out_ref, w_ref):
    chans = w_ref.shape[1]
    twice = jnp.where((iota((chans, 128), 1) & 63) == iota((chans, 128), 0), 1.0, 0.0).astype(BF)
    wide = dotf(w_ref[...], twice)
    left = iota((chans, 128), 1) < 64
    zero = jnp.zeros((chans, 128), F32)
    for t in range(4):
        for ro in range(2):
            a = t - ro
            for j, dx in enumerate((0, 1, 2, -1)):
                halves = []
                for co in range(2):
                    b = dx - co + 1
                    good = 0 <= a < 3 and 0 <= b < 3
                    halves.append(wide[(a * 3 + b) * chans : (a * 3 + b + 1) * chans] if good else zero)
                value = jnp.where(left, halves[0], halves[1]).astype(BF)
                row = t * 256 + j * 64
                out_ref[row : row + 64, ro * 128 : (ro + 1) * 128] = value


def fill_conv2(out_ref, w_ref):
    zero = jnp.zeros((128, 128), BF)
    for a in range(3):
        part = w_ref[a * 384 : (a + 1) * 384, :]
        out_ref[a * 512 : a * 512 + 384, 0:128] = part
        out_ref[a * 512 + 384 : (a + 1) * 512, 0:128] = zero
        out_ref[a * 512 : a * 512 + 128, 128:256] = zero
        out_ref[a * 512 + 128 : (a + 1) * 512, 128:256] = part


def conv1(taps_ref, i, count, w_ref):
    size = taps_ref.shape[2]
    rows = [
        taps_ref[1, pl.ds(i, count)],
        taps_ref[0, pl.ds(i + 1, count)],
        taps_ref[1, pl.ds(i + 1, count)],
        taps_ref[0, pl.ds(i + 2, count)],
    ]
    lhs = [
        jnp.concatenate([r[:, :, p * 256 : (p + 1) * 256].reshape(count * size, 256) for r in rows], axis=1)
        for p in range(4)
    ]
    return dotf(jnp.concatenate(lhs, axis=0), w_ref[...])


def conv(taps_ref, o, count, reach, w_ref):
    size = taps_ref.shape[1]
    rows = [taps_ref[pl.ds(o + a, count)] for a in range(3)]
    lhs = [
        jnp.concatenate(
            [r[:, :, q * 256 : q * 256 + reach].reshape(count * size, reach) for r in rows], axis=1
        )
        for q in range(2)
    ]
    return dotf(jnp.concatenate(lhs, axis=0), w_ref[...])


def loop(count, body):
    def step(i, carry):
        body(i)
        return carry

    lax.fori_loop(0, count, step, 0)


def divisor(total, most):
    return max(d for d in range(1, most + 1) if total % d == 0)


def loop_chunks(total, chunk, body):
    chunk = min(chunk, total)
    steps = -(-total // chunk)
    loop(steps, lambda c: body(jnp.minimum(c * chunk, total - chunk), chunk))


def fill_embed(out_ref, w_ref):
    feats, chans = w_ref.shape
    twice = jnp.where((iota((chans, 128), 1) & 63) == iota((chans, 128), 0), 1.0, 0.0).astype(BF)
    wide = dotf(w_ref[...], twice).astype(BF)
    k = iota((512, feats), 0)
    source = ((k >> 3) & 15) * 4 + (k & 1) * 2 + ((k >> 7) & 1)
    pick = jnp.where(source == iota((512, feats), 1), 1.0, 0.0).astype(BF)
    wide = dotf(pick, wide)
    k = iota((512, 128), 0)
    right = iota((512, 128), 1) >= 64
    same_cell = right == ((k >> 8) == 1)
    for i in range(4):
        keep = same_cell & (((k & 7) >> 1) == i)
        out_ref[:, i * 128 : (i + 1) * 128] = jnp.where(keep, wide, 0.0).astype(BF)


def embed_rows(noisy_ref, coarse_ref, w_ref, turn_ref):
    cols = noisy_ref.shape[2]
    n = cols // 16
    out = []
    for o in range(2):
        block = jnp.concatenate(
            [noisy_ref[:, o * 8 : (o + 1) * 8, :].reshape(64, cols), coarse_ref[:, o * 8 : (o + 1) * 8, :].reshape(64, cols)],
            axis=0,
        )
        turn_ref[o] = block.T
        lhs = [
            jnp.concatenate([turn_ref[o, pl.ds(4 * p + s, n, stride=16), :] for s in range(4)], axis=1)
            for p in range(4)
        ]
        res = dotf(jnp.concatenate(lhs, axis=0).astype(BF), w_ref[...])
        for i in range(4):
            out.append(
                jnp.concatenate([res[p * n : (p + 1) * n, i * 128 : (i + 1) * 128] for p in range(4)], axis=1)
            )
    return out


def strips_kernel(w_ref, nl_ref, cl_ref, nr_ref, cr_ref, wide_ref, left_ref, right_ref, turn_ref, strip_ref):
    fill_embed(wide_ref, w_ref)
    octets = nl_ref.shape[1] // 8
    first = iota((64, 128), 1) < 64
    for o in range(octets):
        rows = slice(o * 8, (o + 1) * 8)
        block = jnp.concatenate(
            [
                jnp.where(first, a[:, rows, :].reshape(64, 128), b[:, rows, :].reshape(64, 128))
                for a, b in ((nl_ref, nr_ref), (cl_ref, cr_ref))
            ],
            axis=0,
        ).T
        turn_ref[0, o * 16 : (o + 1) * 16, :] = block[:16]
        turn_ref[1, o * 16 : (o + 1) * 16, :] = block[112:]
    lhs = [
        jnp.concatenate([turn_ref[side, pl.ds(4 * p + s, octets, stride=16), :] for s in range(4)], axis=1)
        for side in range(2)
        for p in range(4)
    ]
    res = dotf(jnp.concatenate(lhs, axis=0).astype(BF), wide_ref[...])
    for side, out_ref in ((0, left_ref), (1, right_ref)):
        for p in range(4):
            at = (side * 4 + p) * octets
            for i in range(4):
                strip_ref[p, pl.ds(i, octets, stride=4), :] = res[at : at + octets, i * 128 : (i + 1) * 128]
        for p in range(4):
            out_ref[:, p * 128 : (p + 1) * 128] = strip_ref[p].astype(BF)


def embed_mid_kernel(wide_ref, noisy_ref, coarse_ref, mid_ref, turn_ref):
    mid_ref[...] = jnp.concatenate(embed_rows(noisy_ref, coarse_ref, wide_ref, turn_ref), axis=0).astype(BF)


def embed_edge_kernel(wide_ref, left_ref, right_ref, noisy_ref, coarse_ref, top_ref, bot_ref, turn_ref):
    rows = embed_rows(noisy_ref, coarse_ref, wide_ref, turn_ref)
    n = rows[0].shape[0]
    count = left_ref.shape[0]
    for k, ref in ((0, top_ref), (1, bot_ref)):

        @pl.when(pl.program_id(0) == k)
        def _(k=k, ref=ref):
            ref[0 : 8 * n, :] = jnp.concatenate(rows, axis=0).astype(BF)
            at = slice(0, 16) if k == 0 else slice(count - 16, count)
            pick = slice(0, 8) if k == 0 else slice(8, 16)
            rims = [r[at, :].astype(F32)[pick] for r in (left_ref, right_ref)]
            ref[8 * n :, :] = jnp.concatenate(rims, axis=0).astype(BF)


def near(array):
    return pltpu.with_memory_space_constraint(array, pltpu.VMEM)


ANYWHERE = pl.BlockSpec(memory_space=pl.ANY)


class Fetch:
    def __init__(self, sems, **pairs):
        self.copies = {name: pltpu.make_async_copy(src, dst, sems.at[i]) for i, (name, (src, dst)) in enumerate(pairs.items())}
        for copy in self.copies.values():
            copy.start()

    def wait(self, *names):
        for name in names:
            self.copies[name].wait()


def whole(shape):
    return pl.BlockSpec(shape, lambda *_: (0,) * len(shape))


def embed_strips(noisy, coarse, w_embed):
    nvars, rows, cols = noisy.shape
    sides = [pl.BlockSpec((nvars, rows, 128), lambda k: (0, 0, 0)), pl.BlockSpec((nvars, rows, 128), lambda k: (0, 0, cols // 128 - 1))]
    strip = jax.ShapeDtypeStruct((rows // 2, 512), BF)
    return pl.pallas_call(
        strips_kernel,
        name="embed_strips",
        grid=(1,),
        in_specs=[whole(w_embed.shape), sides[0], sides[0], sides[1], sides[1]],
        out_specs=[whole((512, 512)), whole(strip.shape), whole(strip.shape)],
        out_shape=[jax.ShapeDtypeStruct((512, 512), BF), strip, strip],
        scratch_shapes=[pltpu.VMEM((2, rows * 2, 128), F32), pltpu.VMEM((4, rows // 2, 128), F32)],
    )(w_embed, noisy, coarse, noisy, coarse)


def embed_edges(noisy, coarse, wide, left, right):
    nvars, rows, cols = noisy.shape
    n = cols // 16
    last = rows // 16 - 1
    field = pl.BlockSpec((nvars, 16, cols), lambda k: (0, k * last, 0))
    pay = jax.ShapeDtypeStruct((8 * n + 16, 512), BF)
    return pl.pallas_call(
        embed_edge_kernel,
        name="embed_edges",
        grid=(2,),
        in_specs=[whole(wide.shape), whole(left.shape), whole(right.shape), field, field],
        out_specs=[whole(pay.shape)] * 2,
        out_shape=[pay, pay],
        scratch_shapes=[pltpu.VMEM((2, cols, 128), F32)],
    )(wide, near(left), near(right), noisy, coarse)


def embed_middle(noisy, coarse, wide):
    nvars, rows, cols = noisy.shape
    n = cols // 16
    steps = rows // 16 - 2
    field = pl.BlockSpec((nvars, 16, cols), lambda k: (0, k + 1, 0))
    return pl.pallas_call(
        embed_mid_kernel,
        name="embed_middle",
        grid=(steps,),
        in_specs=[whole(wide.shape), field, field],
        out_specs=pl.BlockSpec((8 * n, 512), lambda k: (k, 0)),
        out_shape=jax.ShapeDtypeStruct((8 * steps * n, 512), BF),
        scratch_shapes=[pltpu.VMEM((2, cols, 128), F32)],
    )(wide, noisy, coarse)


def full_rows(x, left, right, n, size):
    tail = size - n
    place = iota((tail, 512), 0)
    full = []
    for j in range(x.shape[0] // n):
        rim = jnp.where(place == 0, right[j], jnp.where(place == tail - 1, left[j], 0.0))
        full += [x[j * n : (j + 1) * n], rim]
    return jnp.concatenate(full, axis=0)


def level1(h_ref, taps_ref, k, h, bias, mean, factor=None):
    size = h_ref.shape[2]
    u = activate(h, bias, mean)
    for j in range(h.shape[0] // size):
        part = u[j * size : (j + 1) * size]
        h_ref[j % 2, k + j // 2] = h[j * size : (j + 1) * size].astype(BF)
        put_taps1(taps_ref, j % 2, k + j // 2, part if factor is None else part * factor)


def enc_conv1(taps_ref, h_ref, i, count, conv_ref, wd_ref, store):
    size = taps_ref.shape[2]
    acc = conv1(taps_ref, i, count, conv_ref)
    flat = count * size
    merged = []
    for p in range(4):
        halves = []
        for ro in range(2):
            lanes = slice(p * 128, (p + 1) * 128)
            prior = h_ref[ro, pl.ds(i + 1, count), :, lanes].reshape(flat, 128).astype(F32)
            e = (prior + acc[p * flat : (p + 1) * flat, ro * 128 : (ro + 1) * 128]).astype(BF)
            store(ro, lanes, e.reshape(count, size, 128))
            halves.append(e)
        merged.append(jnp.concatenate(halves, axis=1))
    d = dotf(jnp.concatenate(merged, axis=0), wd_ref[...]).astype(BF)
    return jnp.concatenate([d[p * flat : (p + 1) * flat] for p in range(4)], axis=1)


def encoder_own_kernel(
    bias_ref, mid_ref, top_ref, bot_ref, lhalo_ref, rhalo_ref, w1_ref, wd1_ref, w2_ref,
    e1_out, d1_out, taps2_out, edge_h_out, edge_taps_out, conv1_out, conv2_out,
    lf_ref, rf_ref, h1_ref, taps1_ref, e1_ref, d1_ref, taps2_ref, conv1_ref, conv2_ref, sem, sems,
    *, n, size,
):
    fill_conv1(conv1_ref, w1_ref)
    fill_conv2(conv2_ref, w2_ref)
    weights_out = Fetch(sems, conv1=(conv1_ref, conv1_out), conv2=(conv2_ref, conv2_out))
    lf_ref[...] = lhalo_ref[...].astype(F32)
    rf_ref[...] = rhalo_ref[...].astype(F32)
    mean1, mean2 = mean_matrix(64), mean_matrix(128)
    rows1 = lhalo_ref.shape[0]

    def first(x, row):
        left = [lf_ref[pl.ds(row + j, 1), :] for j in range(4)]
        right = [rf_ref[pl.ds(row + j, 1), :] for j in range(4)]
        k = row // 2
        level1(h1_ref, taps1_ref, k, full_rows(x.astype(F32), left, right, n, size), bias_ref[0:1, :], mean1)

    for j in range(2):
        part = slice(j * 4 * n, (j + 1) * 4 * n)
        first(top_ref[part, :], j * 4)
        first(bot_ref[part, :], rows1 - 8 + j * 4)
    loop((rows1 - 16) // 4, lambda i: first(mid_ref[pl.ds(pl.multiple_of(i * 4 * n, 4 * n), 4 * n), :], 8 + i * 4))

    edges = []
    for side, k in ((0, 0), (1, rows1 // 2 - 2)):
        for t, (source, out) in enumerate(((h1_ref, edge_h_out), (taps1_ref, edge_taps_out))):
            for ro in range(2):
                copy = pltpu.make_async_copy(
                    source.at[ro, pl.ds(k, 2)], out.at[ro, pl.ds(2 * side, 2)], sems.at[2 + 4 * side + 2 * t + ro]
                )
                copy.start()
                edges.append(copy)

    def second(i, count):
        def store(ro, lanes, e):
            e1_ref[ro, pl.ds(i, count), :, lanes] = e

        d = enc_conv1(taps1_ref, h1_ref, i, count, conv1_ref, wd1_ref, store)
        d1_ref[pl.ds(i, count)] = d.reshape(count, size, 512)
        u = activate(d.astype(F32), bias_ref[1:2, :], mean2)
        for j in range(count):
            put_taps(taps2_ref, i + j, u[j * size : (j + 1) * size], 128)
        for copy in leave(i):
            copy.start()

    chunk = divisor(rows1 // 2 - 2, 6)
    steps = (rows1 // 2 - 2) // chunk

    def leave(i):
        part = pl.ds(i, chunk)
        slot = i // chunk
        return [
            pltpu.make_async_copy(e1_ref.at[0, part], e1_out.at[0, part], sem.at[slot, 0]),
            pltpu.make_async_copy(e1_ref.at[1, part], e1_out.at[1, part], sem.at[slot, 1]),
            pltpu.make_async_copy(d1_ref.at[part], d1_out.at[part], sem.at[slot, 2]),
            pltpu.make_async_copy(taps2_ref.at[part], taps2_out.at[part], sem.at[slot, 3]),
        ]

    loop(steps, lambda c: second(c * chunk, chunk))
    weights_out.wait("conv1", "conv2")
    for copy in edges:
        copy.wait()
    for c in range(steps):
        for copy in leave(c * chunk):
            copy.wait()


def encoder_own(biases, mid, top, bot, lhalo, rhalo, w1, wd1, w2, n, size):
    rows1 = lhalo.shape[0]
    inner = rows1 // 2 - 2
    vmem = pltpu.VMEM
    inside = pl.BlockSpec(memory_space=pltpu.VMEM)
    return pl.pallas_call(
        functools.partial(encoder_own_kernel, n=n, size=size),
        name="encoder_own",
        in_specs=[inside] * 9,
        out_specs=[ANYWHERE] * 7,
        out_shape=[
            jax.ShapeDtypeStruct((2, inner, size, 512), BF),
            jax.ShapeDtypeStruct((inner, size, 512), BF),
            jax.ShapeDtypeStruct((inner, size, 768), BF),
            jax.ShapeDtypeStruct((2, 4, size, 512), BF),
            jax.ShapeDtypeStruct((2, 4, size, 1024), BF),
            jax.ShapeDtypeStruct((1024, 256), BF),
            jax.ShapeDtypeStruct((1536, 256), BF),
        ],
        scratch_shapes=[
            vmem((rows1, 512), F32),
            vmem((rows1, 512), F32),
            vmem((2, rows1 // 2, size, 512), BF),
            vmem((2, rows1 // 2, size, 1024), BF),
            vmem((2, inner, size, 512), BF),
            vmem((inner, size, 512), BF),
            vmem((inner, size, 768), BF),
            vmem((1024, 256), BF),
            vmem((1536, 256), BF),
            pltpu.SemaphoreType.DMA((inner // divisor(inner, 6), 4)),
            pltpu.SemaphoreType.DMA((10,)),
        ],
    )(biases, mid, top, bot, near(lhalo), near(rhalo), w1, wd1, w2)


def encoder_kernel(
    flags, before, bias_ref, top_ref, bot_ref, wd1_ref,
    edge_h_ref, edge_taps_ref, conv1_in, conv2_in, d1_own_ref, taps2_own_ref, wd2_in, w3_in, wd3_in,
    e1_ref, e2_out, e3_out, send_ref,
    h1_ref, taps1_ref, d1_ref, taps2_ref, d2_ref, taps3_ref, d3_ref, edge_ref,
    conv1_ref, conv2_ref, wd2_ref, w3_ref, wd3_ref, e2_ref, e3_ref, sems, sems2, sems3,
    *, n, size, rows1, sent,
):
    rows2, rows3 = rows1 // 2, rows1 // 4
    inner = rows2 - 2
    fetch = Fetch(
        sems,
        **{
            f"{name}{side}{ro}": (
                source.at[ro, pl.ds(2 * side, 2)],
                target.at[ro, pl.ds(4 if side == 0 else 6, 2)],
            )
            for name, source, target in (("h", edge_h_ref, h1_ref), ("t", edge_taps_ref, taps1_ref))
            for side in range(2)
            for ro in range(2)
        },
        conv1=(conv1_in, conv1_ref),
        conv2=(conv2_in, conv2_ref),
        d1=(d1_own_ref, d1_ref.at[pl.ds(4, inner)]),
        taps2=(taps2_own_ref, taps2_ref.at[pl.ds(4, inner)]),
        wd2=(wd2_in, wd2_ref),
        w3=(w3_in, w3_ref),
        wd3=(wd3_in, wd3_ref),
    )
    mean1, mean2, mean3 = mean_matrix(64), mean_matrix(128), mean_matrix(256)

    for side, ref in ((0, top_ref), (1, bot_ref)):
        base = 6 * side
        rims = ref[8 * n :, :].astype(F32)
        x = ref[0 : 8 * n, :].astype(F32)
        left = [rims[j : j + 1] for j in range(8)]
        right = [rims[8 + j : 9 + j] for j in range(8)]
        at = base if side == 0 else base + 2
        level1(h1_ref, taps1_ref, at, full_rows(x, left, right, n, size), bias_ref[0:1, :], mean1, flags[side])

    fetch.wait("conv1", *(f"{name}{side}{ro}" for name in "ht" for side in range(2) for ro in range(2)))
    for side in range(2):

        def store(ro, lanes, e, side=side):
            keep = slice(2, 4) if side == 0 else slice(0, 2)
            e1_ref[ro, 2 * side : 2 * side + 2, :, lanes] = e[keep]

        d = enc_conv1(taps1_ref, h1_ref, 6 * side, 4, conv1_ref, wd1_ref, store)
        at = 0 if side == 0 else rows2 + 2
        d1_ref[at : at + 4] = d.reshape(4, size, 512)
        u = activate(d.astype(F32), bias_ref[1:2, :], mean2)
        for j in range(4):
            inside = j == 3 if side == 0 else j == 0
            part = u[j * size : (j + 1) * size]
            put_taps(taps2_ref, at + j, part if inside else part * flags[side], 128)

    fetch.wait("conv2", "d1", "taps2", "wd2")
    chunk2, chunk3 = divisor(rows3 + 2, 6), divisor(rows3 // 2, 4)

    def leave2(i):
        part = pl.ds(2 * i, 2 * chunk2)
        return pltpu.make_async_copy(e2_ref.at[part], e2_out.at[part], sems2.at[i // chunk2])

    def leave3(i):
        part = pl.ds(2 * i, 2 * chunk3)
        return pltpu.make_async_copy(e3_ref.at[part], e3_out.at[part], sems3.at[i // chunk3])

    def third(i, count2):
        o = 2 * i
        acc = conv(taps2_ref, o, 2 * count2, 512, conv2_ref)
        flat = 2 * count2 * size
        merged = []
        for q in range(2):
            lanes = slice(q * 256, (q + 1) * 256)
            prior = d1_ref[pl.ds(o + 1, 2 * count2), :, lanes].reshape(flat, 256).astype(F32)
            e = (prior + acc[q * flat : (q + 1) * flat]).astype(BF).reshape(2 * count2, size, 256)
            e2_ref[pl.ds(o, 2 * count2), :, lanes] = e
            for j in range(count2):
                merged.append(jnp.concatenate([e[2 * j], e[2 * j + 1]], axis=1))
        d = dotf(jnp.concatenate(merged, axis=0), wd2_ref[...]).astype(BF)
        d = jnp.concatenate([d[: flat // 2], d[flat // 2 :]], axis=1)
        d2_ref[pl.ds(i, count2)] = d.reshape(count2, size, 512)
        u = activate(d.astype(F32), bias_ref[2:3, :], mean3)
        for j in range(count2):
            put_taps(taps3_ref, i + j, u[j * size : (j + 1) * size] * row_factor(i + j, 1, rows3 + 1, flags), 256)
        leave2(i).start()

    loop((rows3 + 2) // chunk2, lambda c: third(c * chunk2, chunk2))
    fetch.wait("w3", "wd3")

    def fourth(i, count3):
        o = 2 * i
        acc = conv(taps3_ref, o, 2 * count3, 768, w3_ref)
        flat = 2 * count3 * size
        acc = jnp.concatenate([acc[:flat], acc[flat:]], axis=1)
        e = (d2_ref[pl.ds(o + 1, 2 * count3)].reshape(flat, 512).astype(F32) + acc).astype(BF)
        wide = e.astype(F32)
        for j in range(2 * count3):
            edge_ref[0, pl.ds(o + j, 1), :] = wide[j * size : j * size + 1]
            edge_ref[1, pl.ds(o + j, 1), :] = wide[j * size + n - 1 : j * size + n]
        e = e.reshape(2 * count3, size, 512)
        e3_ref[pl.ds(o, 2 * count3)] = e
        merged = [jnp.concatenate([e[2 * j], e[2 * j + 1]], axis=1) for j in range(count3)]
        d = dotf(jnp.concatenate(merged, axis=0), wd3_ref[...])
        for j in range(count3):
            d3_ref[i + j] = d[j * size : j * size + n].astype(BF)
        leave3(i).start()

    loop(rows3 // 2 // chunk3, lambda c: fourth(c * chunk3, chunk3))

    left = edge_ref[0].astype(BF)
    right = edge_ref[1].astype(BF)
    groups, each, copies = sent
    for d in range(groups):
        send_ref[d, 0:rows3, :] = jnp.where(before[0] == d, left, right)
        for e in range(each):
            row = d * each + e if copies == 1 else d // copies
            send_ref[d, rows3 + e * n : rows3 + (e + 1) * n, :] = d3_ref[row]
    for c in range((rows3 + 2) // chunk2):
        leave2(c * chunk2).wait()
    for c in range(rows3 // 2 // chunk3):
        leave3(c * chunk3).wait()


def encoder(flags, before, biases, top, bot, edge_h, edge_taps, weights, d1, taps2, n, size, rows1, sent):
    rows2, rows3 = rows1 // 2, rows1 // 4
    vmem = pltpu.VMEM
    smem = pl.BlockSpec(memory_space=pltpu.SMEM)
    inside = pl.BlockSpec(memory_space=pltpu.VMEM)
    conv1_w, wd1, conv2_w, wd2, w3, wd3 = weights
    return pl.pallas_call(
        functools.partial(encoder_kernel, n=n, size=size, rows1=rows1, sent=sent),
        name="encoder",
        in_specs=[smem] * 2 + [inside] * 4 + [ANYWHERE] * 9,
        out_specs=[inside, ANYWHERE, ANYWHERE, inside],
        out_shape=[
            jax.ShapeDtypeStruct((2, 4, size, 512), BF),
            jax.ShapeDtypeStruct((rows2 + 4, size, 512), BF),
            jax.ShapeDtypeStruct((rows3, size, 512), BF),
            jax.ShapeDtypeStruct((sent[0], rows3 + sent[1] * n, 512), BF),
        ],
        scratch_shapes=[
            vmem((2, 12, size, 512), BF),
            vmem((2, 12, size, 1024), BF),
            vmem((rows2 + 6, size, 512), BF),
            vmem((rows2 + 6, size, 768), BF),
            vmem((rows3 + 2, size, 512), BF),
            vmem((rows3 + 2, size, 1024), BF),
            vmem((rows3 // 2, n, 512), BF),
            vmem((2, rows3, 512), F32),
            vmem(conv1_w.shape, BF),
            vmem(conv2_w.shape, BF),
            vmem(wd2.shape, BF),
            vmem(w3.shape, BF),
            vmem(wd3.shape, BF),
            vmem((rows2 + 4, size, 512), BF),
            vmem((rows3, size, 512), BF),
            pltpu.SemaphoreType.DMA((15,)),
            pltpu.SemaphoreType.DMA(((rows3 + 2) // divisor(rows3 + 2, 6),)),
            pltpu.SemaphoreType.DMA((rows3 // 2 // divisor(rows3 // 2, 4),)),
        ],
    )(
        flags, before, biases, near(top), near(bot), wd1,
        edge_h, edge_taps, conv1_w, conv2_w, d1, taps2, wd2, w3, wd3,
    )


def attention_kernel(
    sides, x_ref, bias_ref, wqkv_ref, e3_in, wout_in, out_ref, full_ref, mixed_ref, a4_ref, e3_ref, wout_ref, sems,
    *, n, size, each,
):
    fetch = Fetch(sems, e3=(e3_in, e3_ref), wout=(wout_in, wout_ref))
    tail = size - n
    place = iota((tail, 512), 0)
    groups, _, width = x_ref.shape
    length = groups * n
    edge = e3_ref.shape[0]
    scale = HEAD_DIM**-0.5
    for row in range(each):
        at = edge + row * n
        x = jnp.concatenate([x_ref[g, at : at + n, :].astype(F32) for g in range(groups)], axis=0)
        mean = jnp.mean(x * x, axis=1, keepdims=True)
        u = (x * lax.rsqrt(mean + EPS) + bias_ref[3:4, :]).astype(BF)
        qkv = dotf(u, wqkv_ref[...]).astype(BF)
        left = iota((length, 128), 1) < 64
        for h in range(width // 128):
            q = qkv[:, h * 128 : (h + 1) * 128].astype(F32) * scale
            k = qkv[:, width + h * 128 : width + (h + 1) * 128]
            v = qkv[:, 2 * width + h * 128 : 2 * width + (h + 1) * 128]
            outs = []
            for side in range(2):
                mine = left if side == 0 else jnp.logical_not(left)
                qs = jnp.where(mine, q, 0.0).astype(BF)
                s = lax.dot_general(qs, k, (((1,), (1,)), ((), ())), preferred_element_type=F32)
                e = jnp.exp(s - jnp.max(s, axis=1, keepdims=True))
                total = jnp.sum(e, axis=1, keepdims=True)
                outs.append(dotf(e.astype(BF), v) / total)
            mixed_ref[:, h * 128 : (h + 1) * 128] = jnp.where(left, outs[0], outs[1]).astype(BF)
        if row == 0:
            fetch.wait("e3", "wout")
        a4_ref[...] = x + dotf(mixed_ref[...], wout_ref[...])
        for t in range(length // n):
            after = (t * n + n) % length
            before = (t * n - 1) % length
            rim = jnp.where(
                place == 0,
                a4_ref[after : after + 1, :],
                jnp.where(place == tail - 1, a4_ref[before : before + 1, :], 0.0),
            )
            out_ref[t, row] = jnp.concatenate([a4_ref[t * n : (t + 1) * n, :], rim], axis=0).astype(BF)

    lf = x_ref[sides[0], 0:edge, :].astype(F32)
    rf = x_ref[sides[1], 0:edge, :].astype(F32)
    for r in range(edge):
        rim = jnp.where(place == 0, rf[r : r + 1], jnp.where(place == tail - 1, lf[r : r + 1], 0.0))
        full_ref[r] = jnp.concatenate([e3_ref[r, 0:n, :].astype(F32), rim], axis=0).astype(BF)


def attention(sides, x, biases, e3, w_qkv, w_out, n, size, each):
    groups, _, width = x.shape
    length = groups * n
    return pl.pallas_call(
        functools.partial(attention_kernel, n=n, size=size, each=each),
        name="attention",
        in_specs=[pl.BlockSpec(memory_space=pltpu.SMEM)] + [pl.BlockSpec(memory_space=pltpu.VMEM)] * 3 + [ANYWHERE] * 2,
        out_shape=[
            jax.ShapeDtypeStruct((groups, each, size, width), BF),
            jax.ShapeDtypeStruct((e3.shape[0], size, width), BF),
        ],
        scratch_shapes=[
            pltpu.VMEM((length, width), BF),
            pltpu.VMEM((length, width), F32),
            pltpu.VMEM(e3.shape, BF),
            pltpu.VMEM(w_out.shape, BF),
            pltpu.SemaphoreType.DMA((2,)),
        ],
    )(sides, near(x), biases, w_qkv, e3, w_out)


def fill_head(out_ref, w_ref):
    chans, outs = w_ref.shape
    col = iota((outs, 512), 1)
    source = ((col >> 3) & 7) * 4 + (col & 1) * 2 + ((col >> 7) & 1)
    pick = jnp.where(source == iota((outs, 512), 0), 1.0, 0.0).astype(BF)
    wide = dotf(w_ref[...], pick)
    col = iota((chans, 512), 1)
    for o in range(2):
        for i in range(4):
            for c in range(2):
                keep = (((col >> 6) & 1) == o) & (((col & 7) >> 1) == i) & ((col >> 8) == c)
                row = o * 512 + i * 128 + c * 64
                out_ref[row : row + 64, :] = jnp.where(keep, wide, 0.0).astype(BF)


def prepare_kernel(w1_ref, w2_ref, wh_ref, conv1_ref, conv2_ref, head_ref):
    fill_conv1(conv1_ref, w1_ref)
    fill_conv2(conv2_ref, w2_ref)
    fill_head(head_ref, wh_ref)


def prepare(w1, w2, wh):
    shapes = [(1024, 256), (1536, 256), (1024, 512)]
    return pl.pallas_call(
        prepare_kernel, name="prepare", out_shape=[jax.ShapeDtypeStruct(x, BF) for x in shapes]
    )(w1, w2, wh)


def up3(a, e, put, wu_ref, bias, mean, size, factor=None):
    spread = dotf(a.reshape(-1, 512), wu_ref[...])
    for j in range(a.shape[0]):
        for ro in range(2):
            part = spread[j * size : (j + 1) * size, ro * 512 : (ro + 1) * 512]
            h = (part + e[2 * j + ro].astype(F32)).astype(BF)
            u = activate(h.astype(F32), bias, mean)
            put(2 * j + ro, h, u if factor is None else u * factor)


def conv_rows(rows, reach, w_ref):
    count, size, _ = rows[0].shape
    lhs = [
        jnp.concatenate(
            [r[:, :, q * 256 : q * 256 + reach].reshape(count * size, reach) for r in rows], axis=1
        )
        for q in range(2)
    ]
    return dotf(jnp.concatenate(lhs, axis=0), w_ref[...])


def up2(prior, acc, e, put, wu_ref, bias, mean, size):
    count = prior.shape[0]
    flat = count * size
    g = []
    for q in range(2):
        mine = prior[:, :, q * 256 : (q + 1) * 256].reshape(flat, 256).astype(F32)
        g.append((mine + acc[q * flat : (q + 1) * flat]).astype(BF))
    spread = dotf(jnp.concatenate(g, axis=0), wu_ref[...])
    for j in range(count):
        for ro in range(2):
            part = [
                spread[q * flat + j * size : q * flat + (j + 1) * size, ro * 256 : (ro + 1) * 256] for q in range(2)
            ]
            h = (jnp.concatenate(part, axis=1) + e(2 * j + ro).astype(F32)).astype(BF)
            put(2 * j + ro, h, activate(h.astype(F32), bias, mean))


def up1(prior, acc, e, put, wu_ref, bias, mean, size):
    count = prior.shape[0]
    flat = count * size
    g = []
    for q in range(2):
        mine = prior[:, :, q * 256 : (q + 1) * 256].reshape(flat, 256).astype(F32)
        both = (mine + acc[q * flat : (q + 1) * flat]).astype(BF)
        g += [both[:, :128], both[:, 128:]]
    spread = dotf(jnp.concatenate(g, axis=0), wu_ref[...])
    for j in range(count):
        for ro in range(2):
            part = [
                spread[p * flat + j * size : p * flat + (j + 1) * size, ro * 128 : (ro + 1) * 128] for p in range(4)
            ]
            h = (jnp.concatenate(part, axis=1) + e(j, ro).astype(F32)).astype(BF)
            put(j, ro, h, activate(h.astype(F32), bias, mean))


def decoder_own_kernel(
    bias_ref, a4_ref, e3_ref, wu3_ref, w3_in, wu2_in, e2_in,
    h2_out, taps2_out, edge_h_out, edge_taps_out,
    h3_ref, taps3_ref, w3_ref, wu2_ref, e2_ref, h2_ref, taps2_ref, sems, sems2,
    *, size,
):
    rows4, rows3 = a4_ref.shape[0], e3_ref.shape[0]
    fetch = Fetch(
        sems, w3=(w3_in, w3_ref), wu2=(wu2_in, wu2_ref), e2=(e2_in.at[pl.ds(4, 2 * rows3 - 4)], e2_ref)
    )
    mean2, mean3 = mean_matrix(128), mean_matrix(256)

    def third(i, count):
        def put(j, h, u):
            h3_ref[2 * i + j] = h
            put_taps(taps3_ref, 2 * i + j, u, 256)

        up3(a4_ref[pl.ds(i, count)], e3_ref[pl.ds(2 * i, 2 * count)], put, wu3_ref, bias_ref[4:5, :], mean3, size)

    loop_chunks(rows4, 4, third)

    edges = []
    for side, at in ((0, 0), (1, rows3 - 2)):
        edges.append(
            pltpu.make_async_copy(taps3_ref.at[pl.ds(at, 2)], edge_taps_out.at[pl.ds(2 * side, 2)], sems.at[3 + side])
        )
        edges.append(
            pltpu.make_async_copy(h3_ref.at[pl.ds(at + side, 1)], edge_h_out.at[pl.ds(side, 1)], sems.at[5 + side])
        )
    for copy in edges:
        copy.start()
    chunk = divisor(rows3 - 2, 7)

    def leave(o):
        part = pl.ds(2 * o, 2 * chunk)
        return [
            pltpu.make_async_copy(h2_ref.at[part], h2_out.at[part], sems2.at[o // chunk, 0]),
            pltpu.make_async_copy(taps2_ref.at[part], taps2_out.at[part], sems2.at[o // chunk, 1]),
        ]

    def second(o, count):
        def put(j, h, u):
            h2_ref[2 * o + j] = h
            put_taps(taps2_ref, 2 * o + j, u, 128)

        acc = conv(taps3_ref, o, count, 768, w3_ref)
        up2(h3_ref[pl.ds(o + 1, count)], acc, lambda j: e2_ref[2 * o + j], put, wu2_ref, bias_ref[5:6, :], mean2, size)

        for copy in leave(o):
            copy.start()

    fetch.wait("w3", "wu2", "e2")
    loop((rows3 - 2) // chunk, lambda c: second(c * chunk, chunk))
    for copy in edges:
        copy.wait()
    for c in range((rows3 - 2) // chunk):
        for copy in leave(c * chunk):
            copy.wait()


def decoder_own(biases, a4, e3, e2, wu3, w3, wu2, size):
    rows3 = e3.shape[0]
    inner = 2 * (rows3 - 2)
    out = pltpu.VMEM
    inside = pl.BlockSpec(memory_space=pltpu.VMEM)
    return pl.pallas_call(
        functools.partial(decoder_own_kernel, size=size),
        name="decoder_own",
        in_specs=[inside] * 4 + [ANYWHERE] * 3,
        out_specs=[ANYWHERE] * 4,
        out_shape=[
            jax.ShapeDtypeStruct((inner, size, 512), BF),
            jax.ShapeDtypeStruct((inner, size, 768), BF),
            jax.ShapeDtypeStruct((2, size, 512), BF),
            jax.ShapeDtypeStruct((4, size, 1024), BF),
        ],
        scratch_shapes=[
            out((rows3, size, 512), BF),
            out((rows3, size, 1024), BF),
            out(w3.shape, BF),
            out(wu2.shape, BF),
            out((2 * rows3 - 4, size, 512), BF),
            out((inner, size, 512), BF),
            out((inner, size, 768), BF),
            pltpu.SemaphoreType.DMA((7,)),
            pltpu.SemaphoreType.DMA(((rows3 - 2) // divisor(rows3 - 2, 7), 2)),
        ],
    )(biases, near(a4), e3, wu3, w3, wu2, e2)


def decoder_kernel(
    flags, factors, bias_ref, top_ref, bot_ref, edge_h_ref, edge_taps_ref, wu1_ref, wu3_ref,
    h2_own_ref, taps2_own_ref, e2_in, w3_in, wu2_in, e1_edge_in, conv2_in, e1_own_in, conv1_in, head_in, noisy_ref, noise_ref,
    out_ref,
    h3_ref, taps3_ref, h2_ref, taps2_ref, h1_ref, taps1_ref, turn_ref,
    e2_ref, w3_ref, wu2_ref, e1_edge_ref, conv2_ref, e1_own_ref, conv1_ref, head_ref, sems,
    *, n, size, rows1,
):
    rows2 = rows1 // 2
    inner = rows2 - 4
    step = pl.program_id(0)

    def prepare():
        fetch = Fetch(
            sems,
            w3=(w3_in, w3_ref),
            e2a=(e2_in.at[pl.ds(0, 4)], e2_ref.at[pl.ds(0, 4)]),
            e2b=(e2_in.at[pl.ds(rows2, 4)], e2_ref.at[pl.ds(4, 4)]),
            wu2=(wu2_in, wu2_ref),
            h2=(h2_own_ref, h2_ref.at[pl.ds(4, inner)]),
            taps2=(taps2_own_ref, taps2_ref.at[pl.ds(4, inner)]),
            conv2=(conv2_in, conv2_ref),
            e1_edge=(e1_edge_in, e1_edge_ref),
            e1_own=(e1_own_in, e1_own_ref),
            conv1=(conv1_in, conv1_ref),
            head=(head_in, head_ref),
        )
        mean1, mean2, mean3 = mean_matrix(64), mean_matrix(128), mean_matrix(256)
        bias3, bias2, bias1 = bias_ref[4:5, :], bias_ref[5:6, :], bias_ref[6:7, :]

        for side, ref in ((0, top_ref), (1, bot_ref)):
            at = 0 if side == 0 else 6

            def put3(j, h, u, at=at, side=side):
                if j == 1 - side:
                    h3_ref[3 * side] = h
                put_taps(taps3_ref, at + j, u, 256)

            up3(ref[0:1], ref[1:3], put3, wu3_ref, bias3, mean3, size, flags[side])
            own = 2 if side == 0 else 4
            taps3_ref[own : own + 2] = edge_taps_ref[2 * side : 2 * side + 2]
            h3_ref[1 + side] = edge_h_ref[side]

        rows = [jnp.concatenate([taps3_ref[a : a + 2], taps3_ref[4 + a : 6 + a]], axis=0) for a in range(3)]

        def place2(j):
            return j if j < 4 else rows2 + j - 4

        def put2(j, h, u):
            if j < 2:
                u = u * flags[0]
            if j >= 6:
                u = u * flags[1]
            h2_ref[place2(j)] = h
            put_taps(taps2_ref, place2(j), u, 128)

        fetch.wait("w3", "wu2", "e2a", "e2b")
        up2(h3_ref[...], conv_rows(rows, 768, w3_ref), lambda j: e2_ref[j], put2, wu2_ref, bias2, mean2, size)
        fetch.wait("h2", "taps2", "conv2", "e1_edge")

        rows = [jnp.concatenate([taps2_ref[a : a + 2], taps2_ref[rows2 + a : rows2 + a + 2]], axis=0) for a in range(3)]
        prior = jnp.concatenate([h2_ref[1:3], h2_ref[rows2 + 1 : rows2 + 3]], axis=0)

        def put1(j, ro, h, u):
            k = j if j < 2 else rows2 + j - 2
            if j == 0:
                u = u * flags[0]
            if j == 3:
                u = u * flags[1]
            h1_ref[ro, k] = h
            put_taps1(taps1_ref, ro, k, u)

        acc = conv_rows(rows, 512, conv2_ref)
        up1(prior, acc, lambda j, ro: e1_edge_ref[ro, j], put1, wu1_ref, bias1, mean1, size)

        def first(i, count):
            o = i + 2

            def put(j, ro, h, u):
                h1_ref[ro, o + j] = h
                put_taps1(taps1_ref, ro, o + j, u)

            acc = conv(taps2_ref, o, count, 512, conv2_ref)
            up1(h2_ref[pl.ds(o + 1, count)], acc, lambda j, ro: e1_own_ref[ro, i + j], put, wu1_ref, bias1, mean1, size)

        fetch.wait("e1_own")
        loop_chunks(rows2 - 2, 6, first)
        fetch.wait("conv1", "head")

    pl.when(step == 0)(prepare)

    i = step * 4
    acc = conv1(taps1_ref, i, 4, conv1_ref)
    flat = 4 * size
    g = []
    for p in range(4):
        halves = []
        for ro in range(2):
            prior = h1_ref[ro, pl.ds(i + 1, 4), :, p * 128 : (p + 1) * 128].reshape(flat, 128).astype(F32)
            halves.append((prior + acc[p * flat : (p + 1) * flat, ro * 128 : (ro + 1) * 128]).astype(BF))
        both = jnp.concatenate(halves, axis=1)
        g.append(jnp.concatenate([both[j * size : (j + 1) * size] for j in range(4)], axis=1))
    spread = dotf(jnp.concatenate(g, axis=0), head_ref[...])
    for p in range(4):
        for s in range(4):
            turn_ref[pl.ds(4 * p + s, n, stride=16), :] = spread[p * size : p * size + n, s * 128 : (s + 1) * 128]
    eps = turn_ref[...].T
    nvars, _, cols = noisy_ref.shape
    for o in range(2):
        part = eps[o * 64 : (o + 1) * 64].reshape(nvars, 8, cols)
        rows = slice(o * 8, (o + 1) * 8)
        out_ref[:, rows, :] = factors[0] * noisy_ref[:, rows, :] - factors[1] * part + factors[2] * noise_ref[:, rows, :]


def decoder(flags, factors, biases, top, bot, edge_h, edge_taps, e2, e1_own, e1_edge, weights, h2, taps2, noisy, step_noise, n, size):
    nvars, lat, cols = noisy.shape
    rows1 = lat // 2
    rows2 = rows1 // 2
    field = pl.BlockSpec((nvars, 16, cols), lambda k: (0, k, 0))
    smem = pl.BlockSpec(memory_space=pltpu.SMEM)
    inside = pl.BlockSpec(memory_space=pltpu.VMEM)
    vmem = pltpu.VMEM
    wu3, w3, wu2, conv2_w, wu1, conv1_w, head_w = weights
    late = [w3, wu2, e1_edge, conv2_w, e1_own, conv1_w, head_w]
    return pl.pallas_call(
        functools.partial(decoder_kernel, n=n, size=size, rows1=rows1),
        name="decoder",
        grid=(rows1 // 8,),
        in_specs=[smem, smem] + [inside] * 7 + [ANYWHERE] * 10 + [field, field],
        out_specs=field,
        out_shape=jax.ShapeDtypeStruct(noisy.shape, F32),
        scratch_shapes=[
            vmem((4, size, 512), BF),
            vmem((8, size, 1024), BF),
            vmem((rows2 + 4, size, 512), BF),
            vmem((rows2 + 4, size, 768), BF),
            vmem((2, rows2 + 2, size, 512), BF),
            vmem((2, rows2 + 2, size, 1024), BF),
            vmem((cols, 128), F32),
            vmem((8, size, 512), BF),
        ]
        + [vmem(x.shape, BF) for x in late]
        + [pltpu.SemaphoreType.DMA((11,))],
    )(
        flags, factors, biases, near(top), near(bot), edge_h, edge_taps, wu1, wu3,
        h2, taps2, e2, *late, noisy, step_noise,
    )


def shift(array, axis, by, closed):
    count = lax.axis_size(axis)
    if closed:
        pairs = [(i, (i + by) % count) for i in range(count)]
    else:
        pairs = [(i, i + by) for i in range(count) if 0 <= i + by < count]
    return lax.ppermute(array, axis, pairs)


def body(
    noisy, coarse, step_noise, timestep, w_time, w_embed, w_enc1, w_down1, w_enc2, w_down2, w_enc3, w_down3,
    w_qkv, w_attn_out, w_up3, w_dec3, w_up2, w_dec2, w_up1, w_dec1, w_head,
):
    nvars, lat, cols = noisy.shape
    n = cols // 16
    size = -(-(n + 2) // 16) * 16
    rows1 = lat // 2
    rows4 = lat // 16
    groups = lax.axis_size("lon")
    lat_at, lat_count = lax.axis_index("lat"), lax.axis_size("lat")
    flags = jnp.stack([lat_at > 0, lat_at < lat_count - 1]).astype(F32)

    wide, left, right = embed_strips(noisy, coarse, w_embed)
    rhalo = shift(left, "lon", -1, True)
    lhalo = shift(right, "lon", 1, True)
    mid = embed_middle(noisy, coarse, wide)

    temb = time_embed(timestep, w_time)
    factors = update_factors(timestep)
    widths = [w_enc1.shape[1], w_enc2.shape[1], w_enc3.shape[1], w_qkv.shape[0], w_dec3.shape[1], w_dec2.shape[1], w_dec1.shape[1]]
    starts = [sum(widths[:i]) for i in range(7)]
    biases = jnp.stack([jnp.tile(temb[s : s + w], 512 // w) for s, w in zip(starts, widths)])

    top, bot = embed_edges(noisy, coarse, wide, lhalo, rhalo)
    from_top = shift(bot, "lat", 1, False)
    from_bot = shift(top, "lat", -1, False)
    e1_own, d1, taps2, edge_h, edge_taps, conv1_w, conv2_w = encoder_own(
        biases, mid, top, bot, lhalo, rhalo, w_enc1, w_down1, w_enc2, n, size
    )

    copies = max(1, groups // rows4)
    each = max(1, rows4 // groups)
    lon_at = lax.axis_index("lon")
    sides = jnp.stack([(lon_at - 1) % groups, (lon_at + 1) % groups]).astype(jnp.int32)
    e1_edge, e2, e3, sent = encoder(
        flags, sides, biases, from_top, from_bot, edge_h, edge_taps,
        (conv1_w, w_down1, conv2_w, w_down2, w_enc3, w_down3), d1, taps2, n, size, rows1, (groups, each, copies),
    )
    got = lax.all_to_all(sent, "lon", split_axis=0, concat_axis=0, tiled=True)
    out, e3 = attention(sides, got, biases, e3, w_qkv, w_attn_out, n, size, each)
    a4 = lax.all_to_all(out.reshape(groups, each * size, 512), "lon", split_axis=0, concat_axis=0, tiled=True)
    a4 = a4.reshape(groups * each, size, 512)
    if copies > 1:
        a4 = a4.reshape(rows4, copies, size, 512)[:, 0]

    top = shift(jnp.concatenate([a4[-1:], e3[-2:]]), "lat", 1, False)
    bot = shift(jnp.concatenate([a4[:1], e3[:2]]), "lat", -1, False)
    h2, taps2, edge_h, edge_taps = decoder_own(biases, a4, e3, e2, w_up3, w_dec3, w_up2, size)
    conv1_w, conv2_w, head_w = prepare(w_dec1, w_dec2, w_head)
    return decoder(
        flags, factors, biases, top, bot, edge_h, edge_taps, e2, e1_own, e1_edge,
        (w_up3, w_dec3, w_up2, conv2_w, w_up1, conv1_w, head_w), h2, taps2, noisy, step_noise, n, size,
    )


def solution(mesh):
    field = P(None, "lat", "lon")
    return jax.shard_map(
        body, mesh=mesh, in_specs=(field, field, field) + (P(),) * 18, out_specs=field, check_vma=False
    )
```

time: 143 us -> 121 us (0.85)
  starting transfers between devices: 33.3 us -> 20.3 us
  blocking collectives: 0 us -> 12.7 us
  waiting for transfers between devices: 12.7 us -> 3.69 us
  Pallas kernels: 82.4 us -> 75 us
  local copies, waits for them, and re-layouts: 11 us -> 4.26 us
    pallas_call x1 -> x5, Pallas kernels: 4.07 us -> 30.1 us  [the longest x1 11.8 us: encoder_own(): pl.pallas_call(functools.partial(encoder_own_kernel, n=n, size=size), nam...]
    pallas_call x1, Pallas kernels: 31.1 us -> 12.1 us  [encoder(): pl.pallas_call(functools.partial(encoder_kernel, n=n, size=size, rows1=ro...]
    pallas_call x1, Pallas kernels: 37.8 us -> 23.8 us  [decoder(): pl.pallas_call(functools.partial(decoder_kernel, n=n, size=size, rows1=ro...]
    all_to_all x0 -> x1, blocking collectives: none -> 12.7 us  [body(): got = lax.all_to_all(sent, 'lon', split_axis=0, concat_axis=0, tiled=True)]
    ppermute x8 -> x6, waiting for transfers between devices: 8.05 us -> 0.02 us  [shift(): return lax.ppermute(array, axis, pairs)]
    ppermute x8 -> x6, starting transfers between devices: 24.4 us -> 16.9 us  [shift(): return lax.ppermute(array, axis, pairs)]
    all_to_all x1 -> x0, starting transfers between devices: 5.45 us -> none  [body(): lax.all_to_all(sent.reshape(groups, each * n, 512), 'lon', split_axis=0,...]
    unnamed x39 -> x15, local copies, waits for them, and re-layouts: 6.62 us -> 2.28 us
  transfers between devices with their start and end apart: 10 -> 7, of which waited for: 4 -> 1; matrix products, arithmetic and copies ran while one was open for 7% -> 5% of each run, Pallas kernels for 4% -> 25%
where the time goes in v1:
time: 121 us; the launch traced here: 120 us
  Pallas kernels  75 us (62%)
  starting transfers between devices  20.3 us (17%)
  blocking collectives  12.7 us (10%)
  local copies, waits for them, and re-layouts  4.26 us (4%)
  waiting for transfers between devices  3.69 us (3%)
  other arithmetic  1.83 us (2%)
  between operations  1.37 us (1%)
    pallas_call x1, Pallas kernels, decoder(): pl.pallas_call(functools.partial(decoder_kernel, n=n, size=size, rows1=ro...  23.8 us
    ppermute x6, starting transfers between devices, shift(): return lax.ppermute(array, axis, pairs)  16.9 us
    all_to_all x1, blocking collectives, body(): got = lax.all_to_all(sent, 'lon', split_axis=0, concat_axis=0, tiled=True)  12.7 us
    pallas_call x1, Pallas kernels, encoder(): pl.pallas_call(functools.partial(encoder_kernel, n=n, size=size, rows1=ro...  12.1 us
    pallas_call x1, Pallas kernels, encoder_own(): pl.pallas_call(functools.partial(encoder_own_kernel, n=n, size=size), nam...  11.8 us
    pallas_call x1, Pallas kernels, decoder_own(): pl.pallas_call(functools.partial(decoder_own_kernel, size=size), name='de...  8.63 us
    pallas_call x1, Pallas kernels, embed_middle(): pl.pallas_call(embed_mid_kernel, name='embed_middle', grid=(steps,), in_s...  6.11 us
    pallas_call x1, Pallas kernels, attention(): pl.pallas_call(functools.partial(attention_kernel, n=n, size=size, each=e...  3.86 us
  transfers between devices with their start and end apart: 7, of which 1 were waited for; matrix products, arithmetic and copies ran while one was open for 5% of the time, Pallas kernels for 25%

profile of v1, /device:TPU:1, one launch (start us, length us, event | category | flops | bytes accessed | tf_op | source)
XLA Modules:
  0.0 119.7 jit_solution(6586221543946838925)
XLA Ops:
  0.0 3.0 %embed_strips.1 = (bf16[512,512]{1,0:T(8,128)(2,1)}, bf16[64,512]{1,0:T(8,128)(2,1)}, bf16[64,512]{1,0:T(8,128)(2,1)}) custom-call(bf16[64,64]{1,0:T(8,128)(2,1)} %w_ref.1, f32[8,128,384]{2,1,0:T(8,128)} %noisy_ref.5, f32[8,128,384]{2,1,0:T(8,128)} %coarse_ref.3, f32[8,128,384]{2,1,0:T(8,128)} %noisy_ref.5, f32[8,128,384]{2,1,0:T(8,128)} %coarse_ref.3), custom_call_target="tpu_custom_call" | custom-call | tf_op jit(solution)/shard_map/embed_strips/pallas_call | solution.py:277
  3.0 2.0 %collective-permute-start = (bf16[64,512]{1,0:T(8,128)(2,1)}, bf16[64,512]{1,0:T(8,128)(2,1)S(1)}, u32[]{:S(2)}, u32[]{:S(2)}) collective-permute-start(bf16[64,512]{1,0:T(8,128)(2,1)} %get-tuple-element.31), channel_id=1, source_target_pairs={{0,1},{1,2},{2,3},{3,4},{4,5},{5,6},{6,7},{7,0},{8,9},{9,10},{10,1... | collective-permute-start | bytes 196616 | tf_op jit(solution)/shard_map/ppermute | solution.py:1031
  5.0 3.0 %collective-permute-start.1 = (bf16[64,512]{1,0:T(8,128)(2,1)}, bf16[64,512]{1,0:T(8,128)(2,1)S(1)}, u32[]{:S(2)}, u32[]{:S(2)}) collective-permute-start(bf16[64,512]{1,0:T(8,128)(2,1)} %get-tuple-element.32), channel_id=1, source_target_pairs={{0,7},{1,0},{2,1},{3,2},{4,3},{5,4},{6,5},{7,6},{8,15},{9,8},{10,9... | collective-permute-start | bytes 196616 | tf_op jit(solution)/shard_map/ppermute | solution.py:1031
  9.8 6.1 %embed_middle.1.mid_ref = bf16[1152,512]{1,0:T(8,128)(2,1)} custom-call(bf16[512,512]{1,0:T(8,128)(2,1)} %get-tuple-element.30.wide_ref, f32[8,128,384]{2,1,0:T(8,128)} %noisy_ref.5, f32[8,128,384]{2,1,0:T(8,128)} %coarse_ref.3), custom_call_target="tpu_custom_call" | custom-call | tf_op jit(solution)/shard_map/embed_middle/pallas_call | solution.py:310
  15.9 0.8 copy.22.w1_ref
  16.7 0.6 stack.40.bias_ref
  17.3 2.9 %embed_edges.1 = (bf16[208,512]{1,0:T(8,128)(2,1)}, bf16[208,512]{1,0:T(8,128)(2,1)}) custom-call(bf16[512,512]{1,0:T(8,128)(2,1)} %get-tuple-element.30.wide_ref, bf16[64,512]{1,0:T(8,128)(2,1)S(1)} %collective-permute-done.left_ref.lhalo_ref, bf16[64,512]{1,0:T(8,128)(2,1)S(1)} %collective-permute-done.1.right_ref.rhalo_ref, f32[8,128,384]{2,1,0:T(8,128)} %noisy_ref.5, ...), custom_call_target="tpu_custom_call" | custom-call | tf_op jit(solution)/shard_map/embed_edges/pallas_call | solution.py:294
  20.2 4.2 %collective-permute-start.2 = (bf16[208,512]{1,0:T(8,128)(2,1)}, bf16[208,512]{1,0:T(8,128)(2,1)S(1)}, u32[]{:S(2)}, u32[]{:S(2)}) collective-permute-start(bf16[208,512]{1,0:T(8,128)(2,1)} %get-tuple-element.33.bot_ref), channel_id=1, source_target_pairs={{0,8},{8,16},{16,24},{1,9},{9,17},{17,25},{2,10},{10,18},{18,26},{... | collective-permute-start | bytes 638984 | tf_op jit(solution)/shard_map/ppermute | solution.py:1031
  24.4 1.9 %collective-permute-start.3 = (bf16[208,512]{1,0:T(8,128)(2,1)}, bf16[208,512]{1,0:T(8,128)(2,1)S(1)}, u32[]{:S(2)}, u32[]{:S(2)}) collective-permute-start(bf16[208,512]{1,0:T(8,128)(2,1)} %get-tuple-element.34.top_ref), channel_id=1, source_target_pairs={{8,0},{16,8},{24,16},{9,1},{17,9},{25,17},{10,2},{18,10},{26,18},{... | collective-permute-start | bytes 638984 | tf_op jit(solution)/shard_map/ppermute | solution.py:1031
  26.9 0.6 add_convert_fusion.flags
  27.5 11.8 %encoder_own.1 = (bf16[2,30,32,512]{3,2,1,0:T(8,128)(2,1)}, bf16[30,32,512]{2,1,0:T(8,128)(2,1)}, bf16[30,32,768]{2,1,0:T(8,128)(2,1)}, bf16[2,4,32,512]{3,2,1,0...) custom-call(f32[7,512]{1,0:T(8,128)} %stack.40.bias_ref, ...), custom_call_target="tpu_custom_call" | custom-call | tf_op jit(solution)/shard_map/encoder_own/pallas_call | solution.py:433
  39.3 12.1 %encoder.1 = (bf16[2,4,32,512]{3,2,1,0:T(8,128)(2,1)}, bf16[36,32,512]{2,1,0:T(8,128)(2,1)}, bf16[16,32,512]{2,1,0:T(8,128)(2,1)}, bf16[8,40,512]{2,1,0:T(8,128)(2,1)}) custom-call(f32[2]{0:T(128)} %add_convert_fusion.flags, s32[2]{0:T(128)} %pad_add_fusion.before.sides, f32[7,512]{1,0:T(8,128)} %stack.40.bias_ref, ...), custom_call_target="tpu_custom_call" | custom-call | tf_op jit(solution)/shard_map/encoder/pallas_call | solution.py:593
  51.4 12.7 %all_to_all.10.x_ref = bf16[8,40,512]{2,1,0:T(8,128)(2,1)S(1)} all-to-all(bf16[8,40,512]{2,1,0:T(8,128)(2,1)} %get-tuple-element.41), channel_id=1, replica_groups=mesh['lat'=4,'lon'=8] {'lon'}, dimensions={0} | all-to-all | bytes 655360 | tf_op jit(solution)/shard_map/all_to_all | solution.py:1073
  64.0 3.9 %attention.1 = (bf16[8,1,32,512]{3,2,1,0:T(8,128)(2,1)}, bf16[16,32,512]{2,1,0:T(8,128)(2,1)}) custom-call(s32[2]{0:T(128)} %pad_add_fusion.before.sides, bf16[8,40,512]{2,1,0:T(8,128)(2,1)S(1)} %all_to_all.10.x_ref, f32[7,512]{1,0:T(8,128)} %stack.40.bias_ref, bf16[512,1536]{1,0:T(8,128)(2,1)} %wqkv_ref.1, bf16[16,32,512]{2,1,0:T(8,128)(2,1)} %get-tuple-element.42.e3_in, ...), custom_call_target="tpu_custom_call" | custom-call | tf_op jit(solution)/shard_map/attention/pallas_call | solution.py:684
  67.9 3.4 %all-to-all-start.1 = ((bf16[8,32,512]{2,1,0:T(8,128)(2,1)}), bf16[8,32,512]{2,1,0:T(8,128)(2,1)S(1)}, u32[]{:S(2)}, u32[]{:S(2)}) async-start(bf16[8,32,512]{2,1,0:T(8,128)(2,1)} %bitcast.36), calls=%async_computation.1 | async-start | bytes 524288 | tf_op jit(solution)/shard_map/all_to_all | solution.py:1075
  71.7 0.8 copy.23.w1_ref
  72.5 0.7 copy.24.wh_ref
  73.2 2.9 %prepare.1 = (bf16[1024,256]{1,0:T(8,128)(2,1)}, bf16[1536,256]{1,0:T(8,128)(2,1)}, bf16[1024,512]{1,0:T(8,128)(2,1)}) custom-call(bf16[576,64]{1,0:T(8,128)(2,1)} %copy.23.w1_ref, bf16[1152,128]{1,0:T(8,128)(2,1)} %w2_ref.3, bf16[64,32]{1,0:T(8,128)(2,1)} %copy.24.wh_ref), custom_call_target="tpu_custom_call" | custom-call | tf_op jit(solution)/shard_map/prepare/pallas_call | solution.py:725
  76.1 0.9 fusion.5
  77.0 3.7 %all-to-all-done.1.a4_ref = bf16[8,32,512]{2,1,0:T(8,128)(2,1)S(1)} async-done(((bf16[8,32,512]{2,1,0:T(8,128)(2,1)}), bf16[8,32,512]{2,1,0:T(8,128)(2,1)S(1)}, u32[]{:S(2)}, u32[]{:S(2)}) %all-to-all-start.1) | async-done | bytes 262176 | tf_op jit(solution)/shard_map/all_to_all | solution.py:1075
  80.7 2.4 %collective-permute-start.5 = (bf16[3,32,512]{2,1,0:T(8,128)(2,1)S(1)}, bf16[3,32,512]{2,1,0:T(8,128)(2,1)S(1)}, u32[]{:S(2)}, u32[]{:S(2)}) collective-permute-start(bf16[3,32,512]{2,1,0:T(8,128)(2,1)S(1)} %pad_maximum_fusion.1), channel_id=1, source_target_pairs={{8,0},{16,8},{24,16},{9,1},{17,9},{25,17},{10,2},{18,10},{26,18},{... | collective-permute-start | bytes 294920 | tf_op jit(solution)/shard_map/ppermute | solution.py:1031
  83.0 3.4 %collective-permute-start.4 = (bf16[3,32,512]{2,1,0:T(8,128)(2,1)S(1)}, bf16[3,32,512]{2,1,0:T(8,128)(2,1)S(1)}, u32[]{:S(2)}, u32[]{:S(2)}) collective-permute-start(bf16[3,32,512]{2,1,0:T(8,128)(2,1)S(1)} %pad_maximum_fusion), channel_id=1, source_target_pairs={{0,8},{8,16},{16,24},{1,9},{9,17},{17,25},{2,10},{10,18},{18,26},{... | collective-permute-start | bytes 294920 | tf_op jit(solution)/shard_map/ppermute | solution.py:1031
  87.0 8.6 %decoder_own.1 = (bf16[28,32,512]{2,1,0:T(8,128)(2,1)}, bf16[28,32,768]{2,1,0:T(8,128)(2,1)}, bf16[2,32,512]{2,1,0:T(8,128)(2,1)}, bf16[4,32,1024]{2,1,0:T(8,128)(2,1)}) custom-call(f32[7,512]{1,0:T(8,128)} %stack.40.bias_ref, bf16[8,32,512]{2,1,0:T(8,128)(2,1)S(1)} %all-to-all-done.1.a4_ref, bf16[16,32,512]{2,1,0:T(8,128)(2,1)} %get-tuple-element.44.e3_ref, ...), custom_call_target="tpu_custom_call" | custom-call | tf_op jit(solution)/shard_map/decoder_own/pallas_call | solution.py:851
  95.7 23.8 %decoder.1 = f32[8,128,384]{2,1,0:T(8,128)} custom-call(f32[2]{0:T(128)} %add_convert_fusion.flags, f32[3]{0:T(128)} %pad_maximum_fusion.2.factors, f32[7,512]{1,0:T(8,128)} %stack.40.bias_ref, bf16[3,32,512]{2,1,0:T(8,128)(2,1)S(1)} %collective-permute-done.4.top_ref, bf16[3,32,512]{2,1,0:T(8,128)(2,1)S(1)} %collective-permute-done.5.bot_ref, ...), custom_call_target="tpu_custom_call" | custom-call | tf_op jit(solution)/shard_map/decoder/pallas_call | solution.py:1000
  (37 shorter events, 2.2 us)
Async XLA Ops:
  0.0 8.8 %copy-start = (f32[128,1408]{1,0:T(8,128)S(1)}, f32[128,1408]{1,0:T(8,128)}, u32[]{:S(2)}) copy-start(f32[128,1408]{1,0:T(8,128)} %param.25) | copy-start | bytes 2162692
  3.0 14.3 %collective-permute-start = (bf16[64,512]{1,0:T(8,128)(2,1)}, bf16[64,512]{1,0:T(8,128)(2,1)S(1)}, u32[]{:S(2)}, u32[]{:S(2)}) collective-permute-start(bf16[64,512]{1,0:T(8,128)(2,1)} %get-tuple-element.31), channel_id=1, source_target_pairs={{0,1},{1,2},{2,3},{3,4},{4,5},{5,6},{6,7},{7,0},{8,9},{9,10},{10,1... | collective-permute-start | bytes 196616 | tf_op jit(solution)/shard_map/ppermute | solution.py:1031
  5.0 12.3 %collective-permute-start.1 = (bf16[64,512]{1,0:T(8,128)(2,1)}, bf16[64,512]{1,0:T(8,128)(2,1)S(1)}, u32[]{:S(2)}, u32[]{:S(2)}) collective-permute-start(bf16[64,512]{1,0:T(8,128)(2,1)} %get-tuple-element.32), channel_id=1, source_target_pairs={{0,7},{1,0},{2,1},{3,2},{4,3},{5,4},{6,5},{7,6},{8,15},{9,8},{10,9... | collective-permute-start | bytes 196616 | tf_op jit(solution)/shard_map/ppermute | solution.py:1031
  9.8 6.1 %copy-start.1 = (bf16[576,64]{0,1:T(8,128)(2,1)S(1)}, bf16[576,64]{0,1:T(8,128)(2,1)}, u32[]{:S(2)}) copy-start(bf16[576,64]{0,1:T(8,128)(2,1)} %param.27) | copy-start | bytes 221188
  20.2 19.0 %collective-permute-start.2 = (bf16[208,512]{1,0:T(8,128)(2,1)}, bf16[208,512]{1,0:T(8,128)(2,1)S(1)}, u32[]{:S(2)}, u32[]{:S(2)}) collective-permute-start(bf16[208,512]{1,0:T(8,128)(2,1)} %get-tuple-element.33.bot_ref), channel_id=1, source_target_pairs={{0,8},{8,16},{16,24},{1,9},{9,17},{17,25},{2,10},{10,18},{18,26},{... | collective-permute-start | bytes 638984 | tf_op jit(solution)/shard_map/ppermute | solution.py:1031
  24.4 14.9 %collective-permute-start.3 = (bf16[208,512]{1,0:T(8,128)(2,1)}, bf16[208,512]{1,0:T(8,128)(2,1)S(1)}, u32[]{:S(2)}, u32[]{:S(2)}) collective-permute-start(bf16[208,512]{1,0:T(8,128)(2,1)} %get-tuple-element.34.top_ref), channel_id=1, source_target_pairs={{8,0},{16,8},{24,16},{9,1},{17,9},{25,17},{10,2},{18,10},{26,18},{... | collective-permute-start | bytes 638984 | tf_op jit(solution)/shard_map/ppermute | solution.py:1031
  64.0 7.7 %copy-start.2 = (bf16[576,64]{0,1:T(8,128)(2,1)S(1)}, bf16[576,64]{0,1:T(8,128)(2,1)}, u32[]{:S(2)}) copy-start(bf16[576,64]{0,1:T(8,128)(2,1)} %param.40) | copy-start | bytes 221188
  64.0 8.5 %copy-start.3 = (bf16[64,32]{0,1:T(8,128)(2,1)S(1)}, bf16[64,32]{0,1:T(8,128)(2,1)}, u32[]{:S(2)}) copy-start(bf16[64,32]{0,1:T(8,128)(2,1)} %param.41) | copy-start | bytes 12292
  67.9 12.7 %all-to-all-start.1 = ((bf16[8,32,512]{2,1,0:T(8,128)(2,1)}), bf16[8,32,512]{2,1,0:T(8,128)(2,1)S(1)}, u32[]{:S(2)}, u32[]{:S(2)}) async-start(bf16[8,32,512]{2,1,0:T(8,128)(2,1)} %bitcast.36), calls=%async_computation.1 | async-start | bytes 524288 | tf_op jit(solution)/shard_map/all_to_all | solution.py:1075
  80.7 15.0 %collective-permute-start.5 = (bf16[3,32,512]{2,1,0:T(8,128)(2,1)S(1)}, bf16[3,32,512]{2,1,0:T(8,128)(2,1)S(1)}, u32[]{:S(2)}, u32[]{:S(2)}) collective-permute-start(bf16[3,32,512]{2,1,0:T(8,128)(2,1)S(1)} %pad_maximum_fusion.1), channel_id=1, source_target_pairs={{8,0},{16,8},{24,16},{9,1},{17,9},{25,17},{10,2},{18,10},{26,18},{... | collective-permute-start | bytes 294920 | tf_op jit(solution)/shard_map/ppermute | solution.py:1031
  83.0 12.6 %collective-permute-start.4 = (bf16[3,32,512]{2,1,0:T(8,128)(2,1)S(1)}, bf16[3,32,512]{2,1,0:T(8,128)(2,1)S(1)}, u32[]{:S(2)}, u32[]{:S(2)}) collective-permute-start(bf16[3,32,512]{2,1,0:T(8,128)(2,1)S(1)} %pad_maximum_fusion), channel_id=1, source_target_pairs={{0,8},{8,16},{16,24},{1,9},{9,17},{17,25},{2,10},{10,18},{18,26},{... | collective-permute-start | bytes 294920 | tf_op jit(solution)/shard_map/ppermute | solution.py:1031

commit v2 on v1

--- a/solution.py
+++ b/solution.py
@@ -46,21 +46,26 @@
     return jnp.dot(a, b, preferred_element_type=F32)
 
 
+def dot_tn(a, b):
+    return lax.dot_general(a, b, (((0,), (0,)), ((), ())), preferred_element_type=F32)
+
+
+def ends(count_of_lat):
+    at = lax.axis_index("lat")
+    return [jnp.where(at > 0, 1.0, 0.0), jnp.where(at < count_of_lat - 1, 1.0, 0.0)]
+
+
 def mean_matrix(chans):
     size = 256
     same = (iota((size, size), 0) & -chans) == (iota((size, size), 1) & -chans)
-    return jnp.where(same, 1.0 / chans, 0.0).astype(BF)
-
-
-def scaled(x, bias, mean):
+    return jnp.where(same, 4.0 / chans, 0.0).astype(BF)
+
+
+def activate(x, bias, mean):
     squares = (x * x).astype(BF)
     size = mean.shape[0]
     parts = [dotf(squares[:, i : i + size], mean) for i in range(0, x.shape[1], size)]
-    return x * lax.rsqrt(jnp.concatenate(parts, axis=1) + EPS) + bias
-
-
-def activate(x, bias, mean):
-    half = 0.5 * scaled(x, bias, mean)
+    half = x * lax.rsqrt(jnp.concatenate(parts, axis=1) + 4 * EPS) + bias
     return half + half * jnp.tanh(half)
 
 
@@ -75,21 +80,30 @@
     after = pairs[1:] + [pltpu.roll(pairs[0], size - 1, 0)]
     before = [pltpu.roll(pairs[3], 1, 0)] + pairs[:3]
     for p in range(4):
-        ref[parity, k, :, p * 256 : p * 256 + 128] = pairs[p].astype(BF)
-        ref[parity, k, :, p * 256 + 128 : (p + 1) * 256] = jnp.where(first, after[p], before[p]).astype(BF)
+        ref[parity, k, 2 * p] = pairs[p].astype(BF)
+        ref[parity, k, 2 * p + 1] = jnp.where(first, after[p], before[p]).astype(BF)
 
 
 def put_taps(ref, k, u, chans):
     size, lanes = u.shape
-    ref[k, :, 0:chans] = pltpu.roll(u[:, lanes - chans :], 1, 0).astype(BF)
-    ref[k, :, chans : chans + lanes] = u.astype(BF)
-    ref[k, :, chans + lanes :] = pltpu.roll(u[:, :chans], size - 1, 0).astype(BF)
+    parts = [u[:, i : i + 128] for i in range(0, lanes, 128)]
+    edge = chans // 128
+    around = (
+        [pltpu.roll(x, 1, 0) for x in parts[-edge:]] + parts + [pltpu.roll(x, size - 1, 0) for x in parts[:edge]]
+    )
+    for i, part in enumerate(around):
+        ref[k, i] = part.astype(BF)
+
+
+def lanes_of(rows, first, last):
+    count, _, size, _ = rows.shape
+    return [rows[:, b].reshape(count * size, 128) for b in range(first, last)]
 
 
 def fill_conv1(out_ref, w_ref):
-    chans = w_ref.shape[1]
+    chans = w_ref.shape[0]
     twice = jnp.where((iota((chans, 128), 1) & 63) == iota((chans, 128), 0), 1.0, 0.0).astype(BF)
-    wide = dotf(w_ref[...], twice)
+    wide = dot_tn(w_ref[...], twice)
     left = iota((chans, 128), 1) < 64
     zero = jnp.zeros((chans, 128), F32)
     for t in range(4):
@@ -117,30 +131,25 @@
 
 
 def conv1(taps_ref, i, count, w_ref):
-    size = taps_ref.shape[2]
     rows = [
         taps_ref[1, pl.ds(i, count)],
         taps_ref[0, pl.ds(i + 1, count)],
         taps_ref[1, pl.ds(i + 1, count)],
         taps_ref[0, pl.ds(i + 2, count)],
     ]
+    lhs = [jnp.concatenate([x for r in rows for x in lanes_of(r, 2 * p, 2 * p + 2)], axis=1) for p in range(4)]
+    return dotf(jnp.concatenate(lhs, axis=0), w_ref[...])
+
+
+def conv_rows(rows, reach, w_ref):
     lhs = [
-        jnp.concatenate([r[:, :, p * 256 : (p + 1) * 256].reshape(count * size, 256) for r in rows], axis=1)
-        for p in range(4)
+        jnp.concatenate([x for r in rows for x in lanes_of(r, 2 * q, 2 * q + reach // 128)], axis=1) for q in range(2)
     ]
     return dotf(jnp.concatenate(lhs, axis=0), w_ref[...])
 
 
 def conv(taps_ref, o, count, reach, w_ref):
-    size = taps_ref.shape[1]
-    rows = [taps_ref[pl.ds(o + a, count)] for a in range(3)]
-    lhs = [
-        jnp.concatenate(
-            [r[:, :, q * 256 : q * 256 + reach].reshape(count * size, reach) for r in rows], axis=1
-        )
-        for q in range(2)
-    ]
-    return dotf(jnp.concatenate(lhs, axis=0), w_ref[...])
+    return conv_rows([taps_ref[pl.ds(o + a, count)] for a in range(3)], reach, w_ref)
 
 
 def loop(count, body):
@@ -338,7 +347,7 @@
 
 
 def enc_conv1(taps_ref, h_ref, i, count, conv_ref, wd_ref, store):
-    size = taps_ref.shape[2]
+    size = taps_ref.shape[3]
     acc = conv1(taps_ref, i, count, conv_ref)
     flat = count * size
     merged = []
@@ -375,12 +384,48 @@
         k = row // 2
         level1(h1_ref, taps1_ref, k, full_rows(x.astype(F32), left, right, n, size), bias_ref[0:1, :], mean1)
 
-    for j in range(2):
-        part = slice(j * 4 * n, (j + 1) * 4 * n)
-        first(top_ref[part, :], j * 4)
-        first(bot_ref[part, :], rows1 - 8 + j * 4)
-    loop((rows1 - 16) // 4, lambda i: first(mid_ref[pl.ds(pl.multiple_of(i * 4 * n, 4 * n), 4 * n), :], 8 + i * 4))
-
+    def first_at(row):
+        if row < 8:
+            first(top_ref[row * n : (row + 4) * n, :], row)
+        elif row < rows1 - 8:
+            first(mid_ref[(row - 8) * n : (row - 4) * n, :], row)
+        else:
+            at = row - rows1 + 8
+            first(bot_ref[at * n : (at + 4) * n, :], row)
+
+    def second(i, count):
+        def store(ro, lanes, e):
+            e1_ref[ro, pl.ds(i, count), :, lanes] = e
+
+        d = enc_conv1(taps1_ref, h1_ref, i, count, conv1_ref, wd1_ref, store)
+        d1_ref[pl.ds(i, count)] = d.reshape(count, size, 512)
+        u = activate(d.astype(F32), bias_ref[1:2, :], mean2)
+        for j in range(count):
+            put_taps(taps2_ref, i + j, u[j * size : (j + 1) * size], 128)
+        for copy in leave(i):
+            copy.start()
+
+    chunk = divisor(rows1 // 2 - 2, 6)
+    steps = (rows1 // 2 - 2) // chunk
+
+    def leave(i):
+        part = pl.ds(i, chunk)
+        slot = i // chunk
+        return [
+            pltpu.make_async_copy(e1_ref.at[0, part], e1_out.at[0, part], sem.at[slot, 0]),
+            pltpu.make_async_copy(e1_ref.at[1, part], e1_out.at[1, part], sem.at[slot, 1]),
+            pltpu.make_async_copy(d1_ref.at[part], d1_out.at[part], sem.at[slot, 2]),
+            pltpu.make_async_copy(taps2_ref.at[part], taps2_out.at[part], sem.at[slot, 3]),
+        ]
+
+    done = 0
+    for c in range(steps + 1):
+        need = rows1 if c == steps else min(rows1, -(-(2 * chunk * (c + 1) + 3) // 4) * 4)
+        while done < need:
+            first_at(done)
+            done += 4
+        if c:
+            second((c - 1) * chunk, chunk)
     edges = []
     for side, k in ((0, 0), (1, rows1 // 2 - 2)):
         for t, (source, out) in enumerate(((h1_ref, edge_h_out), (taps1_ref, edge_taps_out))):
@@ -390,33 +435,6 @@
                 )
                 copy.start()
                 edges.append(copy)
-
-    def second(i, count):
-        def store(ro, lanes, e):
-            e1_ref[ro, pl.ds(i, count), :, lanes] = e
-
-        d = enc_conv1(taps1_ref, h1_ref, i, count, conv1_ref, wd1_ref, store)
-        d1_ref[pl.ds(i, count)] = d.reshape(count, size, 512)
-        u = activate(d.astype(F32), bias_ref[1:2, :], mean2)
-        for j in range(count):
-            put_taps(taps2_ref, i + j, u[j * size : (j + 1) * size], 128)
-        for copy in leave(i):
-            copy.start()
-
-    chunk = divisor(rows1 // 2 - 2, 6)
-    steps = (rows1 // 2 - 2) // chunk
-
-    def leave(i):
-        part = pl.ds(i, chunk)
-        slot = i // chunk
-        return [
-            pltpu.make_async_copy(e1_ref.at[0, part], e1_out.at[0, part], sem.at[slot, 0]),
-            pltpu.make_async_copy(e1_ref.at[1, part], e1_out.at[1, part], sem.at[slot, 1]),
-            pltpu.make_async_copy(d1_ref.at[part], d1_out.at[part], sem.at[slot, 2]),
-            pltpu.make_async_copy(taps2_ref.at[part], taps2_out.at[part], sem.at[slot, 3]),
-        ]
-
-    loop(steps, lambda c: second(c * chunk, chunk))
     weights_out.wait("conv1", "conv2")
     for copy in edges:
         copy.wait()
@@ -438,9 +456,9 @@
         out_shape=[
             jax.ShapeDtypeStruct((2, inner, size, 512), BF),
             jax.ShapeDtypeStruct((inner, size, 512), BF),
-            jax.ShapeDtypeStruct((inner, size, 768), BF),
+            jax.ShapeDtypeStruct((inner, 6, size, 128), BF),
             jax.ShapeDtypeStruct((2, 4, size, 512), BF),
-            jax.ShapeDtypeStruct((2, 4, size, 1024), BF),
+            jax.ShapeDtypeStruct((2, 4, 8, size, 128), BF),
             jax.ShapeDtypeStruct((1024, 256), BF),
             jax.ShapeDtypeStruct((1536, 256), BF),
         ],
@@ -448,26 +466,27 @@
             vmem((rows1, 512), F32),
             vmem((rows1, 512), F32),
             vmem((2, rows1 // 2, size, 512), BF),
-            vmem((2, rows1 // 2, size, 1024), BF),
+            vmem((2, rows1 // 2, 8, size, 128), BF),
             vmem((2, inner, size, 512), BF),
             vmem((inner, size, 512), BF),
-            vmem((inner, size, 768), BF),
+            vmem((inner, 6, size, 128), BF),
             vmem((1024, 256), BF),
             vmem((1536, 256), BF),
             pltpu.SemaphoreType.DMA((inner // divisor(inner, 6), 4)),
             pltpu.SemaphoreType.DMA((10,)),
         ],
-    )(biases, mid, top, bot, near(lhalo), near(rhalo), w1, wd1, w2)
+    )(biases, mid, top, bot, near(lhalo), near(rhalo), w1.T, wd1, w2)
 
 
 def encoder_kernel(
-    flags, before, bias_ref, top_ref, bot_ref, wd1_ref,
+    bias_ref, top_ref, bot_ref, wd1_ref,
     edge_h_ref, edge_taps_ref, conv1_in, conv2_in, d1_own_ref, taps2_own_ref, wd2_in, w3_in, wd3_in,
     e1_ref, e2_out, e3_out, send_ref,
     h1_ref, taps1_ref, d1_ref, taps2_ref, d2_ref, taps3_ref, d3_ref, edge_ref,
     conv1_ref, conv2_ref, wd2_ref, w3_ref, wd3_ref, e2_ref, e3_ref, sems, sems2, sems3,
-    *, n, size, rows1, sent,
+    *, n, size, rows1, sent, lat,
 ):
+    flags = ends(lat)
     rows2, rows3 = rows1 // 2, rows1 // 4
     inner = rows2 - 2
     fetch = Fetch(
@@ -573,8 +592,9 @@
     left = edge_ref[0].astype(BF)
     right = edge_ref[1].astype(BF)
     groups, each, copies = sent
+    before = lax.rem(lax.axis_index("lon") + groups - 1, groups)
     for d in range(groups):
-        send_ref[d, 0:rows3, :] = jnp.where(before[0] == d, left, right)
+        send_ref[d, 0:rows3, :] = jnp.where(before == d, left, right)
         for e in range(each):
             row = d * each + e if copies == 1 else d // copies
             send_ref[d, rows3 + e * n : rows3 + (e + 1) * n, :] = d3_ref[row]
@@ -584,16 +604,15 @@
         leave3(c * chunk3).wait()
 
 
-def encoder(flags, before, biases, top, bot, edge_h, edge_taps, weights, d1, taps2, n, size, rows1, sent):
+def encoder(lat_count, biases, top, bot, edge_h, edge_taps, weights, d1, taps2, n, size, rows1, sent):
     rows2, rows3 = rows1 // 2, rows1 // 4
     vmem = pltpu.VMEM
-    smem = pl.BlockSpec(memory_space=pltpu.SMEM)
     inside = pl.BlockSpec(memory_space=pltpu.VMEM)
     conv1_w, wd1, conv2_w, wd2, w3, wd3 = weights
     return pl.pallas_call(
-        functools.partial(encoder_kernel, n=n, size=size, rows1=rows1, sent=sent),
+        functools.partial(encoder_kernel, n=n, size=size, rows1=rows1, sent=sent, lat=lat_count),
         name="encoder",
-        in_specs=[smem] * 2 + [inside] * 4 + [ANYWHERE] * 9,
+        in_specs=[inside] * 4 + [ANYWHERE] * 9,
         out_specs=[inside, ANYWHERE, ANYWHERE, inside],
         out_shape=[
             jax.ShapeDtypeStruct((2, 4, size, 512), BF),
@@ -603,11 +622,11 @@
         ],
         scratch_shapes=[
             vmem((2, 12, size, 512), BF),
-            vmem((2, 12, size, 1024), BF),
+            vmem((2, 12, 8, size, 128), BF),
             vmem((rows2 + 6, size, 512), BF),
-            vmem((rows2 + 6, size, 768), BF),
+            vmem((rows2 + 6, 6, size, 128), BF),
             vmem((rows3 + 2, size, 512), BF),
-            vmem((rows3 + 2, size, 1024), BF),
+            vmem((rows3 + 2, 8, size, 128), BF),
             vmem((rows3 // 2, n, 512), BF),
             vmem((2, rows3, 512), F32),
             vmem(conv1_w.shape, BF),
@@ -622,13 +641,13 @@
             pltpu.SemaphoreType.DMA((rows3 // 2 // divisor(rows3 // 2, 4),)),
         ],
     )(
-        flags, before, biases, near(top), near(bot), wd1,
+        biases, near(top), near(bot), wd1,
         edge_h, edge_taps, conv1_w, conv2_w, d1, taps2, wd2, w3, wd3,
     )
 
 
 def attention_kernel(
-    sides, x_ref, bias_ref, wqkv_ref, e3_in, wout_in, out_ref, full_ref, mixed_ref, a4_ref, e3_ref, wout_ref, sems,
+    x_ref, bias_ref, wqkv_ref, e3_in, wout_in, out_ref, full_ref, mixed_ref, a4_ref, e3_ref, wout_ref, sems,
     *, n, size, each,
 ):
     fetch = Fetch(sems, e3=(e3_in, e3_ref), wout=(wout_in, wout_ref))
@@ -671,20 +690,21 @@
             )
             out_ref[t, row] = jnp.concatenate([a4_ref[t * n : (t + 1) * n, :], rim], axis=0).astype(BF)
 
-    lf = x_ref[sides[0], 0:edge, :].astype(F32)
-    rf = x_ref[sides[1], 0:edge, :].astype(F32)
+    here = lax.axis_index("lon")
+    lf = x_ref[lax.rem(here + groups - 1, groups), 0:edge, :].astype(F32)
+    rf = x_ref[lax.rem(here + 1, groups), 0:edge, :].astype(F32)
     for r in range(edge):
         rim = jnp.where(place == 0, rf[r : r + 1], jnp.where(place == tail - 1, lf[r : r + 1], 0.0))
         full_ref[r] = jnp.concatenate([e3_ref[r, 0:n, :].astype(F32), rim], axis=0).astype(BF)
 
 
-def attention(sides, x, biases, e3, w_qkv, w_out, n, size, each):
+def attention(x, biases, e3, w_qkv, w_out, n, size, each):
     groups, _, width = x.shape
     length = groups * n
     return pl.pallas_call(
         functools.partial(attention_kernel, n=n, size=size, each=each),
         name="attention",
-        in_specs=[pl.BlockSpec(memory_space=pltpu.SMEM)] + [pl.BlockSpec(memory_space=pltpu.VMEM)] * 3 + [ANYWHERE] * 2,
+        in_specs=[pl.BlockSpec(memory_space=pltpu.VMEM)] * 3 + [ANYWHERE] * 2,
         out_shape=[
             jax.ShapeDtypeStruct((groups, each, size, width), BF),
             jax.ShapeDtypeStruct((e3.shape[0], size, width), BF),
@@ -696,15 +716,15 @@
             pltpu.VMEM(w_out.shape, BF),
             pltpu.SemaphoreType.DMA((2,)),
         ],
-    )(sides, near(x), biases, w_qkv, e3, w_out)
+    )(near(x), biases, w_qkv, e3, w_out)
 
 
 def fill_head(out_ref, w_ref):
-    chans, outs = w_ref.shape
+    outs, chans = w_ref.shape
     col = iota((outs, 512), 1)
     source = ((col >> 3) & 7) * 4 + (col & 1) * 2 + ((col >> 7) & 1)
     pick = jnp.where(source == iota((outs, 512), 0), 1.0, 0.0).astype(BF)
-    wide = dotf(w_ref[...], pick)
+    wide = dot_tn(w_ref[...], pick)
     col = iota((chans, 512), 1)
     for o in range(2):
         for i in range(4):
@@ -712,19 +732,6 @@
                 keep = (((col >> 6) & 1) == o) & (((col & 7) >> 1) == i) & ((col >> 8) == c)
                 row = o * 512 + i * 128 + c * 64
                 out_ref[row : row + 64, :] = jnp.where(keep, wide, 0.0).astype(BF)
-
-
-def prepare_kernel(w1_ref, w2_ref, wh_ref, conv1_ref, conv2_ref, head_ref):
-    fill_conv1(conv1_ref, w1_ref)
-    fill_conv2(conv2_ref, w2_ref)
-    fill_head(head_ref, wh_ref)
-
-
-def prepare(w1, w2, wh):
-    shapes = [(1024, 256), (1536, 256), (1024, 512)]
-    return pl.pallas_call(
-        prepare_kernel, name="prepare", out_shape=[jax.ShapeDtypeStruct(x, BF) for x in shapes]
-    )(w1, w2, wh)
 
 
 def up3(a, e, put, wu_ref, bias, mean, size, factor=None):
@@ -735,17 +742,6 @@
             h = (part + e[2 * j + ro].astype(F32)).astype(BF)
             u = activate(h.astype(F32), bias, mean)
             put(2 * j + ro, h, u if factor is None else u * factor)
-
-
-def conv_rows(rows, reach, w_ref):
-    count, size, _ = rows[0].shape
-    lhs = [
-        jnp.concatenate(
-            [r[:, :, q * 256 : q * 256 + reach].reshape(count * size, reach) for r in rows], axis=1
-        )
-        for q in range(2)
-    ]
-    return dotf(jnp.concatenate(lhs, axis=0), w_ref[...])
 
 
 def up2(prior, acc, e, put, wu_ref, bias, mean, size):
@@ -765,7 +761,7 @@
             put(2 * j + ro, h, activate(h.astype(F32), bias, mean))
 
 
-def up1(prior, acc, e, put, wu_ref, bias, mean, size):
+def up1(prior, acc, e, put, wu_ref, size):
     count = prior.shape[0]
     flat = count * size
     g = []
@@ -780,7 +776,7 @@
                 spread[p * flat + j * size : p * flat + (j + 1) * size, ro * 128 : (ro + 1) * 128] for p in range(4)
             ]
             h = (jnp.concatenate(part, axis=1) + e(j, ro).astype(F32)).astype(BF)
-            put(j, ro, h, activate(h.astype(F32), bias, mean))
+            put(j, ro, h)
 
 
 def decoder_own_kernel(
@@ -855,18 +851,18 @@
         out_specs=[ANYWHERE] * 4,
         out_shape=[
             jax.ShapeDtypeStruct((inner, size, 512), BF),
-            jax.ShapeDtypeStruct((inner, size, 768), BF),
+            jax.ShapeDtypeStruct((inner, 6, size, 128), BF),
             jax.ShapeDtypeStruct((2, size, 512), BF),
-            jax.ShapeDtypeStruct((4, size, 1024), BF),
+            jax.ShapeDtypeStruct((4, 8, size, 128), BF),
         ],
         scratch_shapes=[
             out((rows3, size, 512), BF),
-            out((rows3, size, 1024), BF),
+            out((rows3, 8, size, 128), BF),
             out(w3.shape, BF),
             out(wu2.shape, BF),
             out((2 * rows3 - 4, size, 512), BF),
             out((inner, size, 512), BF),
-            out((inner, size, 768), BF),
+            out((inner, 6, size, 128), BF),
             pltpu.SemaphoreType.DMA((7,)),
             pltpu.SemaphoreType.DMA(((rows3 - 2) // divisor(rows3 - 2, 7), 2)),
         ],
@@ -874,16 +870,17 @@
 
 
 def decoder_kernel(
-    flags, factors, bias_ref, top_ref, bot_ref, edge_h_ref, edge_taps_ref, wu1_ref, wu3_ref,
-    h2_own_ref, taps2_own_ref, e2_in, w3_in, wu2_in, e1_edge_in, conv2_in, e1_own_in, conv1_in, head_in, noisy_ref, noise_ref,
+    factors, bias_ref, top_ref, bot_ref, edge_h_ref, edge_taps_ref, wu1_ref, wu3_ref, w2_ref, w1_ref, wh_ref,
+    h2_own_ref, taps2_own_ref, e2_in, w3_in, wu2_in, e1_edge_in, e1_own_in, noisy_ref, noise_ref,
     out_ref,
     h3_ref, taps3_ref, h2_ref, taps2_ref, h1_ref, taps1_ref, turn_ref,
-    e2_ref, w3_ref, wu2_ref, e1_edge_ref, conv2_ref, e1_own_ref, conv1_ref, head_ref, sems,
-    *, n, size, rows1,
+    e2_ref, w3_ref, wu2_ref, e1_edge_ref, e1_own_ref, conv2_ref, conv1_ref, head_ref, g_ref, sems,
+    *, n, size, rows1, lat,
 ):
     rows2 = rows1 // 2
     inner = rows2 - 4
     step = pl.program_id(0)
+    last = pl.num_programs(0) - 2
 
     def prepare():
         fetch = Fetch(
@@ -894,12 +891,13 @@
             wu2=(wu2_in, wu2_ref),
             h2=(h2_own_ref, h2_ref.at[pl.ds(4, inner)]),
             taps2=(taps2_own_ref, taps2_ref.at[pl.ds(4, inner)]),
-            conv2=(conv2_in, conv2_ref),
             e1_edge=(e1_edge_in, e1_edge_ref),
             e1_own=(e1_own_in, e1_own_ref),
-            conv1=(conv1_in, conv1_ref),
-            head=(head_in, head_ref),
         )
+        flags = ends(lat)
+        fill_conv1(conv1_ref, w1_ref)
+        fill_conv2(conv2_ref, w2_ref)
+        fill_head(head_ref, wh_ref)
         mean1, mean2, mean3 = mean_matrix(64), mean_matrix(128), mean_matrix(256)
         bias3, bias2, bias1 = bias_ref[4:5, :], bias_ref[5:6, :], bias_ref[6:7, :]
 
@@ -931,51 +929,53 @@
 
         fetch.wait("w3", "wu2", "e2a", "e2b")
         up2(h3_ref[...], conv_rows(rows, 768, w3_ref), lambda j: e2_ref[j], put2, wu2_ref, bias2, mean2, size)
-        fetch.wait("h2", "taps2", "conv2", "e1_edge")
+        fetch.wait("h2", "taps2", "e1_edge")
 
         rows = [jnp.concatenate([taps2_ref[a : a + 2], taps2_ref[rows2 + a : rows2 + a + 2]], axis=0) for a in range(3)]
         prior = jnp.concatenate([h2_ref[1:3], h2_ref[rows2 + 1 : rows2 + 3]], axis=0)
 
-        def put1(j, ro, h, u):
-            k = j if j < 2 else rows2 + j - 2
-            if j == 0:
-                u = u * flags[0]
-            if j == 3:
-                u = u * flags[1]
-            h1_ref[ro, k] = h
-            put_taps1(taps1_ref, ro, k, u)
+        def lay(ro, k, factor=None):
+            u = activate(h1_ref[ro, k].astype(F32), bias1, mean1)
+            put_taps1(taps1_ref, ro, k, u if factor is None else u * factor)
+
+        def put1(j, ro, h):
+            h1_ref[ro, j if j < 2 else rows2 + j - 2] = h
 
         acc = conv_rows(rows, 512, conv2_ref)
-        up1(prior, acc, lambda j, ro: e1_edge_ref[ro, j], put1, wu1_ref, bias1, mean1, size)
+        up1(prior, acc, lambda j, ro: e1_edge_ref[ro, j], put1, wu1_ref, size)
 
         def first(i, count):
-            o = i + 2
-
-            def put(j, ro, h, u):
-                h1_ref[ro, o + j] = h
-                put_taps1(taps1_ref, ro, o + j, u)
-
-            acc = conv(taps2_ref, o, count, 512, conv2_ref)
-            up1(h2_ref[pl.ds(o + 1, count)], acc, lambda j, ro: e1_own_ref[ro, i + j], put, wu1_ref, bias1, mean1, size)
-
+            def put(j, ro, h):
+                h1_ref[ro, i + 2 + j] = h
+
+            acc = conv(taps2_ref, i + 2, count, 512, conv2_ref)
+            up1(h2_ref[pl.ds(i + 3, count)], acc, lambda j, ro: e1_own_ref[ro, i + j], put, wu1_ref, size)
+
+        def behind(i, count):
+            for j in range(count):
+                for ro in range(2):
+                    lay(ro, i + 2 + j)
+
+        chunk = divisor(rows2 - 2, 6)
+        steps = (rows2 - 2) // chunk
         fetch.wait("e1_own")
-        loop_chunks(rows2 - 2, 6, first)
-        fetch.wait("conv1", "head")
+        for ro in range(2):
+            lay(ro, 0, flags[0])
+            lay(ro, 1)
+            lay(ro, rows2)
+            lay(ro, rows2 + 1, flags[1])
+        first(0, chunk)
+
+        def both(c):
+            behind((c - 1) * chunk, chunk)
+            first(c * chunk, chunk)
+
+        loop(steps - 1, lambda c: both(c + 1))
+        behind((steps - 1) * chunk, chunk)
 
     pl.when(step == 0)(prepare)
 
-    i = step * 4
-    acc = conv1(taps1_ref, i, 4, conv1_ref)
-    flat = 4 * size
-    g = []
-    for p in range(4):
-        halves = []
-        for ro in range(2):
-            prior = h1_ref[ro, pl.ds(i + 1, 4), :, p * 128 : (p + 1) * 128].reshape(flat, 128).astype(F32)
-            halves.append((prior + acc[p * flat : (p + 1) * flat, ro * 128 : (ro + 1) * 128]).astype(BF))
-        both = jnp.concatenate(halves, axis=1)
-        g.append(jnp.concatenate([both[j * size : (j + 1) * size] for j in range(4)], axis=1))
-    spread = dotf(jnp.concatenate(g, axis=0), head_ref[...])
+    spread = dotf(g_ref[...], head_ref[...])
     for p in range(4):
         for s in range(4):
             turn_ref[pl.ds(4 * p + s, n, stride=16), :] = spread[p * size : p * size + n, s * 128 : (s + 1) * 128]
@@ -986,38 +986,51 @@
         rows = slice(o * 8, (o + 1) * 8)
         out_ref[:, rows, :] = factors[0] * noisy_ref[:, rows, :] - factors[1] * part + factors[2] * noise_ref[:, rows, :]
 
-
-def decoder(flags, factors, biases, top, bot, edge_h, edge_taps, e2, e1_own, e1_edge, weights, h2, taps2, noisy, step_noise, n, size):
+    i = jnp.minimum(step, last) * 4
+    acc = conv1(taps1_ref, i, 4, conv1_ref)
+    flat = 4 * size
+    for p in range(4):
+        halves = []
+        for ro in range(2):
+            prior = h1_ref[ro, pl.ds(i + 1, 4), :, p * 128 : (p + 1) * 128].reshape(flat, 128).astype(F32)
+            halves.append((prior + acc[p * flat : (p + 1) * flat, ro * 128 : (ro + 1) * 128]).astype(BF))
+        both = jnp.concatenate(halves, axis=1)
+        for j in range(4):
+            g_ref[p * size : (p + 1) * size, j * 256 : (j + 1) * 256] = both[j * size : (j + 1) * size]
+
+
+def decoder(lat_count, factors, biases, top, bot, edge_h, edge_taps, e2, e1_own, e1_edge, weights, h2, taps2, noisy, step_noise, n, size):
     nvars, lat, cols = noisy.shape
     rows1 = lat // 2
     rows2 = rows1 // 2
-    field = pl.BlockSpec((nvars, 16, cols), lambda k: (0, k, 0))
+    field = pl.BlockSpec((nvars, 16, cols), lambda k: (0, jnp.maximum(k - 1, 0), 0))
     smem = pl.BlockSpec(memory_space=pltpu.SMEM)
     inside = pl.BlockSpec(memory_space=pltpu.VMEM)
     vmem = pltpu.VMEM
-    wu3, w3, wu2, conv2_w, wu1, conv1_w, head_w = weights
-    late = [w3, wu2, e1_edge, conv2_w, e1_own, conv1_w, head_w]
+    wu3, w3, wu2, w2, wu1, w1, wh = weights
+    late = [w3, wu2, e1_edge, e1_own]
     return pl.pallas_call(
-        functools.partial(decoder_kernel, n=n, size=size, rows1=rows1),
+        functools.partial(decoder_kernel, n=n, size=size, rows1=rows1, lat=lat_count),
         name="decoder",
-        grid=(rows1 // 8,),
-        in_specs=[smem, smem] + [inside] * 7 + [ANYWHERE] * 10 + [field, field],
+        grid=(rows1 // 8 + 1,),
+        in_specs=[smem] + [inside] * 10 + [ANYWHERE] * 7 + [field, field],
         out_specs=field,
         out_shape=jax.ShapeDtypeStruct(noisy.shape, F32),
         scratch_shapes=[
             vmem((4, size, 512), BF),
-            vmem((8, size, 1024), BF),
+            vmem((8, 8, size, 128), BF),
             vmem((rows2 + 4, size, 512), BF),
-            vmem((rows2 + 4, size, 768), BF),
+            vmem((rows2 + 4, 6, size, 128), BF),
             vmem((2, rows2 + 2, size, 512), BF),
-            vmem((2, rows2 + 2, size, 1024), BF),
+            vmem((2, rows2 + 2, 8, size, 128), BF),
             vmem((cols, 128), F32),
             vmem((8, size, 512), BF),
         ]
         + [vmem(x.shape, BF) for x in late]
-        + [pltpu.SemaphoreType.DMA((11,))],
+        + [vmem((1536, 256), BF), vmem((1024, 256), BF), vmem((1024, 512), BF), vmem((4 * size, 1024), BF)]
+        + [pltpu.SemaphoreType.DMA((8,))],
     )(
-        flags, factors, biases, near(top), near(bot), edge_h, edge_taps, wu1, wu3,
+        factors, biases, near(top), near(bot), edge_h, edge_taps, wu1, wu3, w2, w1.T, wh.T,
         h2, taps2, e2, *late, noisy, step_noise,
     )
 
@@ -1041,8 +1054,7 @@
     rows1 = lat // 2
     rows4 = lat // 16
     groups = lax.axis_size("lon")
-    lat_at, lat_count = lax.axis_index("lat"), lax.axis_size("lat")
-    flags = jnp.stack([lat_at > 0, lat_at < lat_count - 1]).astype(F32)
+    lat_count = lax.axis_size("lat")
 
     wide, left, right = embed_strips(noisy, coarse, w_embed)
     rhalo = shift(left, "lon", -1, True)
@@ -1053,7 +1065,9 @@
     factors = update_factors(timestep)
     widths = [w_enc1.shape[1], w_enc2.shape[1], w_enc3.shape[1], w_qkv.shape[0], w_dec3.shape[1], w_dec2.shape[1], w_dec1.shape[1]]
     starts = [sum(widths[:i]) for i in range(7)]
-    biases = jnp.stack([jnp.tile(temb[s : s + w], 512 // w) for s, w in zip(starts, widths)])
+    biases = jnp.stack(
+        [jnp.tile(temb[s : s + w], 512 // w) * (1.0 if i == 3 else 0.5) for i, (s, w) in enumerate(zip(starts, widths))]
+    )
 
     top, bot = embed_edges(noisy, coarse, wide, lhalo, rhalo)
     from_top = shift(bot, "lat", 1, False)
@@ -1064,14 +1078,12 @@
 
     copies = max(1, groups // rows4)
     each = max(1, rows4 // groups)
-    lon_at = lax.axis_index("lon")
-    sides = jnp.stack([(lon_at - 1) % groups, (lon_at + 1) % groups]).astype(jnp.int32)
     e1_edge, e2, e3, sent = encoder(
-        flags, sides, biases, from_top, from_bot, edge_h, edge_taps,
+        lat_count, biases, from_top, from_bot, edge_h, edge_taps,
         (conv1_w, w_down1, conv2_w, w_down2, w_enc3, w_down3), d1, taps2, n, size, rows1, (groups, each, copies),
     )
     got = lax.all_to_all(sent, "lon", split_axis=0, concat_axis=0, tiled=True)
-    out, e3 = attention(sides, got, biases, e3, w_qkv, w_attn_out, n, size, each)
+    out, e3 = attention(got, biases, e3, w_qkv, w_attn_out, n, size, each)
     a4 = lax.all_to_all(out.reshape(groups, each * size, 512), "lon", split_axis=0, concat_axis=0, tiled=True)
     a4 = a4.reshape(groups * each, size, 512)
     if copies > 1:
@@ -1080,10 +1092,9 @@
     top = shift(jnp.concatenate([a4[-1:], e3[-2:]]), "lat", 1, False)
     bot = shift(jnp.concatenate([a4[:1], e3[:2]]), "lat", -1, False)
     h2, taps2, edge_h, edge_taps = decoder_own(biases, a4, e3, e2, w_up3, w_dec3, w_up2, size)
-    conv1_w, conv2_w, head_w = prepare(w_dec1, w_dec2, w_head)
     return decoder(
-        flags, factors, biases, top, bot, edge_h, edge_taps, e2, e1_own, e1_edge,
-        (w_up3, w_dec3, w_up2, conv2_w, w_up1, conv1_w, head_w), h2, taps2, noisy, step_noise, n, size,
+        lat_count, factors, biases, top, bot, edge_h, edge_taps, e2, e1_own, e1_edge,
+        (w_up3, w_dec3, w_up2, w_dec2, w_up1, w_dec1, w_head), h2, taps2, noisy, step_noise, n, size,
     )
 
 

time: 121 us -> 114 us (0.942)
  Pallas kernels: 75 us -> 67.7 us
  waiting for transfers between devices: 3.69 us -> 8.05 us
  local copies, waits for them, and re-layouts: 4.26 us -> 1.78 us
    all_to_all x1, waiting for transfers between devices: 3.68 us -> 8.03 us  [body(): lax.all_to_all(out.reshape(groups, each * size, 512), 'lon', split_axis=0...]
    pallas_call x1 -> x0, Pallas kernels: 2.87 us -> none  [prepare(): pl.pallas_call(prepare_kernel, name='prepare', out_shape=[jax.ShapeDtypeS...]
    pallas_call x1, Pallas kernels: 23.8 us -> 21.3 us  [decoder(): pl.pallas_call(functools.partial(decoder_kernel, n=n, size=size, rows1=ro...]
    unnamed x15 -> x6, local copies, waits for them, and re-layouts: 2.28 us -> 0.02 us
    pallas_call x1, Pallas kernels: 11.8 us -> 10 us  [encoder_own(): pl.pallas_call(functools.partial(encoder_own_kernel, n=n, size=size), nam...]
  transfers between devices with their start and end apart: 7 -> 7, of which waited for: 1 -> 1; matrix products, arithmetic and copies ran while one was open for 5% -> 3% of each run, Pallas kernels for 25% -> 22%
where the time goes in v2:
time: 114 us; the launch traced here: 113 us
  Pallas kernels  67.7 us (59%)
  starting transfers between devices  19.8 us (17%)
  blocking collectives  12.6 us (11%)
  waiting for transfers between devices  8.05 us (7%)
  local copies, waits for them, and re-layouts  1.78 us (2%)
  between operations  1.36 us (1%)
    pallas_call x1, Pallas kernels, decoder(): pl.pallas_call(functools.partial(decoder_kernel, n=n, size=size, rows1=ro...  21.3 us
    ppermute x6, starting transfers between devices, shift(): return lax.ppermute(array, axis, pairs)  16.4 us
    all_to_all x1, blocking collectives, body(): got = lax.all_to_all(sent, 'lon', split_axis=0, concat_axis=0, tiled=True)  12.6 us
    pallas_call x1, Pallas kernels, encoder(): pl.pallas_call(functools.partial(encoder_kernel, n=n, size=size, rows1=ro...  12 us
    pallas_call x1, Pallas kernels, encoder_own(): pl.pallas_call(functools.partial(encoder_own_kernel, n=n, size=size), nam...  10 us
    pallas_call x1, Pallas kernels, decoder_own(): pl.pallas_call(functools.partial(decoder_own_kernel, size=size), name='de...  8.62 us
    all_to_all x1, waiting for transfers between devices, body(): lax.all_to_all(out.reshape(groups, each * size, 512), 'lon', split_axis=0...  8.03 us
    pallas_call x1, Pallas kernels, embed_middle(): pl.pallas_call(embed_mid_kernel, name='embed_middle', grid=(steps,), in_s...  6.04 us
  transfers between devices with their start and end apart: 7, of which 1 were waited for; matrix products, arithmetic and copies ran while one was open for 3% of the time, Pallas kernels for 22%

profile of v2, /device:TPU:1, one launch (start us, length us, event | category | flops | bytes accessed | tf_op | source)
XLA Modules:
  0.0 112.9 jit_solution(16498316385209186103)
XLA Ops:
  0.0 3.0 %embed_strips.1 = (bf16[512,512]{1,0:T(8,128)(2,1)}, bf16[64,512]{1,0:T(8,128)(2,1)}, bf16[64,512]{1,0:T(8,128)(2,1)}) custom-call(bf16[64,64]{1,0:T(8,128)(2,1)} %w_ref.1, f32[8,128,384]{2,1,0:T(8,128)} %noisy_ref.5, f32[8,128,384]{2,1,0:T(8,128)} %coarse_ref.3, f32[8,128,384]{2,1,0:T(8,128)} %noisy_ref.5, f32[8,128,384]{2,1,0:T(8,128)} %coarse_ref.3), custom_call_target="tpu_custom_call" | custom-call | tf_op jit(solution)/shard_map/embed_strips/pallas_call | solution.py:286
  3.0 2.0 %collective-permute-start = (bf16[64,512]{1,0:T(8,128)(2,1)}, bf16[64,512]{1,0:T(8,128)(2,1)S(1)}, u32[]{:S(2)}, u32[]{:S(2)}) collective-permute-start(bf16[64,512]{1,0:T(8,128)(2,1)} %get-tuple-element.28), channel_id=1, source_target_pairs={{0,1},{1,2},{2,3},{3,4},{4,5},{5,6},{6,7},{7,0},{8,9},{9,10},{10,1... | collective-permute-start | bytes 196616 | tf_op jit(solution)/shard_map/ppermute | solution.py:1044
  5.0 3.0 %collective-permute-start.1 = (bf16[64,512]{1,0:T(8,128)(2,1)}, bf16[64,512]{1,0:T(8,128)(2,1)S(1)}, u32[]{:S(2)}, u32[]{:S(2)}) collective-permute-start(bf16[64,512]{1,0:T(8,128)(2,1)} %get-tuple-element.29), channel_id=1, source_target_pairs={{0,7},{1,0},{2,1},{3,2},{4,3},{5,4},{6,5},{7,6},{8,15},{9,8},{10,9... | collective-permute-start | bytes 196616 | tf_op jit(solution)/shard_map/ppermute | solution.py:1044
  8.8 0.5 convolution_reduce_fusion
  9.3 0.1 slice_multiply_fusion
  9.6 0.1 mul.158
  9.6 0.1 mul.143
  9.7 6.0 %embed_middle.1.mid_ref = bf16[1152,512]{1,0:T(8,128)(2,1)} custom-call(bf16[512,512]{1,0:T(8,128)(2,1)} %get-tuple-element.27.wide_ref, f32[8,128,384]{2,1,0:T(8,128)} %noisy_ref.5, f32[8,128,384]{2,1,0:T(8,128)} %coarse_ref.3), custom_call_target="tpu_custom_call" | custom-call | tf_op jit(solution)/shard_map/embed_middle/pallas_call | solution.py:319
  15.8 3.0 %embed_edges.1 = (bf16[208,512]{1,0:T(8,128)(2,1)}, bf16[208,512]{1,0:T(8,128)(2,1)}) custom-call(bf16[512,512]{1,0:T(8,128)(2,1)} %get-tuple-element.27.wide_ref, bf16[64,512]{1,0:T(8,128)(2,1)S(1)} %collective-permute-done.left_ref.lhalo_ref, bf16[64,512]{1,0:T(8,128)(2,1)S(1)} %collective-permute-done.1.right_ref.rhalo_ref, f32[8,128,384]{2,1,0:T(8,128)} %noisy_ref.5, ...), custom_call_target="tpu_custom_call" | custom-call | tf_op jit(solution)/shard_map/embed_edges/pallas_call | solution.py:303
  18.7 4.2 %collective-permute-start.2 = (bf16[208,512]{1,0:T(8,128)(2,1)}, bf16[208,512]{1,0:T(8,128)(2,1)S(1)}, u32[]{:S(2)}, u32[]{:S(2)}) collective-permute-start(bf16[208,512]{1,0:T(8,128)(2,1)} %get-tuple-element.30.bot_ref), channel_id=1, source_target_pairs={{0,8},{8,16},{16,24},{1,9},{9,17},{17,25},{2,10},{10,18},{18,26},{... | collective-permute-start | bytes 638984 | tf_op jit(solution)/shard_map/ppermute | solution.py:1044
  22.9 1.9 %collective-permute-start.3 = (bf16[208,512]{1,0:T(8,128)(2,1)}, bf16[208,512]{1,0:T(8,128)(2,1)S(1)}, u32[]{:S(2)}, u32[]{:S(2)}) collective-permute-start(bf16[208,512]{1,0:T(8,128)(2,1)} %get-tuple-element.31.top_ref), channel_id=1, source_target_pairs={{8,0},{16,8},{24,16},{9,1},{17,9},{25,17},{10,2},{18,10},{26,18},{... | collective-permute-start | bytes 638984 | tf_op jit(solution)/shard_map/ppermute | solution.py:1044
  24.9 0.6 stack.25.bias_ref
  25.5 10.0 %encoder_own.1 = (bf16[2,30,32,512]{3,2,1,0:T(8,128)(2,1)}, bf16[30,32,512]{2,1,0:T(8,128)(2,1)}, bf16[30,6,32,128]{3,2,1,0:T(8,128)(2,1)}, bf16[2,4,32,512]{3,2...) custom-call(f32[7,512]{1,0:T(8,128)} %stack.25.bias_ref, ...), custom_call_target="tpu_custom_call" | custom-call | tf_op jit(solution)/shard_map/encoder_own/pallas_call | solution.py:451
  35.6 12.0 %encoder.1 = (bf16[2,4,32,512]{3,2,1,0:T(8,128)(2,1)}, bf16[36,32,512]{2,1,0:T(8,128)(2,1)}, bf16[16,32,512]{2,1,0:T(8,128)(2,1)}, bf16[8,40,512]{2,1,0:T(8,128)(2,1)}) custom-call(f32[7,512]{1,0:T(8,128)} %stack.25.bias_ref, bf16[208,512]{1,0:T(8,128)(2,1)S(1)} %collective-permute-done.2.top_ref, bf16[208,512]{1,0:T(8,128)(2,1)S(1)} %collective-permute-done.3.bot_ref, ...), custom_call_target="tpu_custom_call" | custom-call | tf_op jit(solution)/shard_map/encoder/pallas_call | solution.py:612
  47.6 12.6 %all_to_all.10.x_ref = bf16[8,40,512]{2,1,0:T(8,128)(2,1)S(1)} all-to-all(bf16[8,40,512]{2,1,0:T(8,128)(2,1)} %get-tuple-element.38), channel_id=1, replica_groups=mesh['lat'=4,'lon'=8] {'lon'}, dimensions={0} | all-to-all | bytes 655360 | tf_op jit(solution)/shard_map/all_to_all | solution.py:1085
  60.2 3.8 %attention.1 = (bf16[8,1,32,512]{3,2,1,0:T(8,128)(2,1)}, bf16[16,32,512]{2,1,0:T(8,128)(2,1)}) custom-call(bf16[8,40,512]{2,1,0:T(8,128)(2,1)S(1)} %all_to_all.10.x_ref, f32[7,512]{1,0:T(8,128)} %stack.25.bias_ref, bf16[512,1536]{1,0:T(8,128)(2,1)} %wqkv_ref.1, bf16[16,32,512]{2,1,0:T(8,128)(2,1)} %get-tuple-element.39.e3_in, bf16[512,512]{1,0:T(8,128)(2,1)} %wout_in.1), custom_call_target="tpu_custom_call" | custom-call | tf_op jit(solution)/shard_map/attention/pallas_call | solution.py:704
  64.0 3.4 %all-to-all-start.1 = ((bf16[8,32,512]{2,1,0:T(8,128)(2,1)}), bf16[8,32,512]{2,1,0:T(8,128)(2,1)S(1)}, u32[]{:S(2)}, u32[]{:S(2)}) async-start(bf16[8,32,512]{2,1,0:T(8,128)(2,1)} %bitcast.35), calls=%async_computation.1 | async-start | bytes 524288 | tf_op jit(solution)/shard_map/all_to_all | solution.py:1087
  67.8 0.9 fusion.9
  68.7 8.0 %all-to-all-done.1.a4_ref = bf16[8,32,512]{2,1,0:T(8,128)(2,1)S(1)} async-done(((bf16[8,32,512]{2,1,0:T(8,128)(2,1)}), bf16[8,32,512]{2,1,0:T(8,128)(2,1)S(1)}, u32[]{:S(2)}, u32[]{:S(2)}) %all-to-all-start.1) | async-done | bytes 262176 | tf_op jit(solution)/shard_map/all_to_all | solution.py:1087
  76.8 3.4 %collective-permute-start.4 = (bf16[3,32,512]{2,1,0:T(8,128)(2,1)S(1)}, bf16[3,32,512]{2,1,0:T(8,128)(2,1)S(1)}, u32[]{:S(2)}, u32[]{:S(2)}) collective-permute-start(bf16[3,32,512]{2,1,0:T(8,128)(2,1)S(1)} %pad_maximum_fusion), channel_id=1, source_target_pairs={{0,8},{8,16},{16,24},{1,9},{9,17},{17,25},{2,10},{10,18},{18,26},{... | collective-permute-start | bytes 294920 | tf_op jit(solution)/shard_map/ppermute | solution.py:1044
  80.2 1.9 %collective-permute-start.5 = (bf16[3,32,512]{2,1,0:T(8,128)(2,1)S(1)}, bf16[3,32,512]{2,1,0:T(8,128)(2,1)S(1)}, u32[]{:S(2)}, u32[]{:S(2)}) collective-permute-start(bf16[3,32,512]{2,1,0:T(8,128)(2,1)S(1)} %pad_maximum_fusion.1), channel_id=1, source_target_pairs={{8,0},{16,8},{24,16},{9,1},{17,9},{25,17},{10,2},{18,10},{26,18},{... | collective-permute-start | bytes 294920 | tf_op jit(solution)/shard_map/ppermute | solution.py:1044
  82.1 0.7 pad_maximum_fusion.2.factors
  82.7 8.6 %decoder_own.1 = (bf16[28,32,512]{2,1,0:T(8,128)(2,1)}, bf16[28,6,32,128]{3,2,1,0:T(8,128)(2,1)}, bf16[2,32,512]{2,1,0:T(8,128)(2,1)}, bf16[4,8,32,128]{3,2,1,0:T(8,128)(2,1)}) custom-call(f32[7,512]{1,0:T(8,128)} %stack.25.bias_ref, bf16[8,32,512]{2,1,0:T(8,128)(2,1)S(1)} %all-to-all-done.1.a4_ref, bf16[16,32,512]{2,1,0:T(8,128)(2,1)} %get-tuple-element.41.e3_ref, ...), custom_call_target="tpu_custom_call" | custom-call | tf_op jit(solution)/shard_map/decoder_own/pallas_call | solution.py:847
  91.4 21.3 %decoder.1 = f32[8,128,384]{2,1,0:T(8,128)} custom-call(f32[3]{0:T(128)} %pad_maximum_fusion.2.factors, f32[7,512]{1,0:T(8,128)} %stack.25.bias_ref, bf16[3,32,512]{2,1,0:T(8,128)(2,1)S(1)} %collective-permute-done.4.top_ref, bf16[3,32,512]{2,1,0:T(8,128)(2,1)S(1)} %collective-permute-done.5.bot_ref, bf16[2,32,512]{2,1,0:T(8,128)(2,1)} %get-tuple-element.43.edge_h_ref, ...), custom_call_target="tpu_custom_call" | custom-call | tf_op jit(solution)/shard_map/decoder/pallas_call | solution.py:1012
  (25 shorter events, 0.4 us)
Async XLA Ops:
  0.0 8.8 %copy-start = (f32[128,1408]{1,0:T(8,128)S(1)}, f32[128,1408]{1,0:T(8,128)}, u32[]{:S(2)}) copy-start(f32[128,1408]{1,0:T(8,128)} %param.25) | copy-start | bytes 2162692
  3.0 12.8 %collective-permute-start = (bf16[64,512]{1,0:T(8,128)(2,1)}, bf16[64,512]{1,0:T(8,128)(2,1)S(1)}, u32[]{:S(2)}, u32[]{:S(2)}) collective-permute-start(bf16[64,512]{1,0:T(8,128)(2,1)} %get-tuple-element.28), channel_id=1, source_target_pairs={{0,1},{1,2},{2,3},{3,4},{4,5},{5,6},{6,7},{7,0},{8,9},{9,10},{10,1... | collective-permute-start | bytes 196616 | tf_op jit(solution)/shard_map/ppermute | solution.py:1044
  5.0 10.7 %collective-permute-start.1 = (bf16[64,512]{1,0:T(8,128)(2,1)}, bf16[64,512]{1,0:T(8,128)(2,1)S(1)}, u32[]{:S(2)}, u32[]{:S(2)}) collective-permute-start(bf16[64,512]{1,0:T(8,128)(2,1)} %get-tuple-element.29), channel_id=1, source_target_pairs={{0,7},{1,0},{2,1},{3,2},{4,3},{5,4},{6,5},{7,6},{8,15},{9,8},{10,9... | collective-permute-start | bytes 196616 | tf_op jit(solution)/shard_map/ppermute | solution.py:1044
  18.7 16.9 %collective-permute-start.2 = (bf16[208,512]{1,0:T(8,128)(2,1)}, bf16[208,512]{1,0:T(8,128)(2,1)S(1)}, u32[]{:S(2)}, u32[]{:S(2)}) collective-permute-start(bf16[208,512]{1,0:T(8,128)(2,1)} %get-tuple-element.30.bot_ref), channel_id=1, source_target_pairs={{0,8},{8,16},{16,24},{1,9},{9,17},{17,25},{2,10},{10,18},{18,26},{... | collective-permute-start | bytes 638984 | tf_op jit(solution)/shard_map/ppermute | solution.py:1044
  22.9 12.7 %collective-permute-start.3 = (bf16[208,512]{1,0:T(8,128)(2,1)}, bf16[208,512]{1,0:T(8,128)(2,1)S(1)}, u32[]{:S(2)}, u32[]{:S(2)}) collective-permute-start(bf16[208,512]{1,0:T(8,128)(2,1)} %get-tuple-element.31.top_ref), channel_id=1, source_target_pairs={{8,0},{16,8},{24,16},{9,1},{17,9},{25,17},{10,2},{18,10},{26,18},{... | collective-permute-start | bytes 638984 | tf_op jit(solution)/shard_map/ppermute | solution.py:1044
  64.0 12.7 %all-to-all-start.1 = ((bf16[8,32,512]{2,1,0:T(8,128)(2,1)}), bf16[8,32,512]{2,1,0:T(8,128)(2,1)S(1)}, u32[]{:S(2)}, u32[]{:S(2)}) async-start(bf16[8,32,512]{2,1,0:T(8,128)(2,1)} %bitcast.35), calls=%async_computation.1 | async-start | bytes 524288 | tf_op jit(solution)/shard_map/all_to_all | solution.py:1087
  76.8 14.6 %collective-permute-start.4 = (bf16[3,32,512]{2,1,0:T(8,128)(2,1)S(1)}, bf16[3,32,512]{2,1,0:T(8,128)(2,1)S(1)}, u32[]{:S(2)}, u32[]{:S(2)}) collective-permute-start(bf16[3,32,512]{2,1,0:T(8,128)(2,1)S(1)} %pad_maximum_fusion), channel_id=1, source_target_pairs={{0,8},{8,16},{16,24},{1,9},{9,17},{17,25},{2,10},{10,18},{18,26},{... | collective-permute-start | bytes 294920 | tf_op jit(solution)/shard_map/ppermute | solution.py:1044
  80.2 11.2 %collective-permute-start.5 = (bf16[3,32,512]{2,1,0:T(8,128)(2,1)S(1)}, bf16[3,32,512]{2,1,0:T(8,128)(2,1)S(1)}, u32[]{:S(2)}, u32[]{:S(2)}) collective-permute-start(bf16[3,32,512]{2,1,0:T(8,128)(2,1)S(1)} %pad_maximum_fusion.1), channel_id=1, source_target_pairs={{8,0},{16,8},{24,16},{9,1},{17,9},{25,17},{10,2},{18,10},{26,18},{... | collective-permute-start | bytes 294920 | tf_op jit(solution)/shard_map/ppermute | solution.py:1044

commit v3 on v2

--- a/solution.py
+++ b/solution.py
@@ -186,26 +186,18 @@
         out_ref[:, i * 128 : (i + 1) * 128] = jnp.where(keep, wide, 0.0).astype(BF)
 
 
-def embed_rows(noisy_ref, coarse_ref, w_ref, turn_ref):
-    cols = noisy_ref.shape[2]
-    n = cols // 16
-    out = []
-    for o in range(2):
-        block = jnp.concatenate(
-            [noisy_ref[:, o * 8 : (o + 1) * 8, :].reshape(64, cols), coarse_ref[:, o * 8 : (o + 1) * 8, :].reshape(64, cols)],
-            axis=0,
-        )
-        turn_ref[o] = block.T
-        lhs = [
-            jnp.concatenate([turn_ref[o, pl.ds(4 * p + s, n, stride=16), :] for s in range(4)], axis=1)
-            for p in range(4)
-        ]
-        res = dotf(jnp.concatenate(lhs, axis=0).astype(BF), w_ref[...])
-        for i in range(4):
-            out.append(
-                jnp.concatenate([res[p * n : (p + 1) * n, i * 128 : (i + 1) * 128] for p in range(4)], axis=1)
-            )
-    return out
+def embed_rows(fields, w_ref, turn_ref, slot):
+    n = fields[0].shape[1] // 16
+    turn_ref[slot] = jnp.concatenate(fields, axis=0).T
+    lhs = [
+        jnp.concatenate([turn_ref[slot, pl.ds(4 * p + s, n, stride=16), :] for s in range(4)], axis=1)
+        for p in range(4)
+    ]
+    res = dotf(jnp.concatenate(lhs, axis=0).astype(BF), w_ref[...])
+    return [
+        jnp.concatenate([res[p * n : (p + 1) * n, i * 128 : (i + 1) * 128] for p in range(4)], axis=1)
+        for i in range(4)
+    ]
 
 
 def strips_kernel(w_ref, nl_ref, cl_ref, nr_ref, cr_ref, wide_ref, left_ref, right_ref, turn_ref, strip_ref):
@@ -238,23 +230,63 @@
             out_ref[:, p * 128 : (p + 1) * 128] = strip_ref[p].astype(BF)
 
 
-def embed_mid_kernel(wide_ref, noisy_ref, coarse_ref, mid_ref, turn_ref):
-    mid_ref[...] = jnp.concatenate(embed_rows(noisy_ref, coarse_ref, wide_ref, turn_ref), axis=0).astype(BF)
-
-
-def embed_edge_kernel(wide_ref, left_ref, right_ref, noisy_ref, coarse_ref, top_ref, bot_ref, turn_ref):
-    rows = embed_rows(noisy_ref, coarse_ref, wide_ref, turn_ref)
-    n = rows[0].shape[0]
+def embed_kernel(wide_ref, noisy_in, coarse_in, top_out, mid_out, bot_out, x_ref, turn_ref, e0_ref, sems, out_sems):
+    _, nvars, rows, cols = x_ref.shape
+    n = cols // 16
+    chunks = rows // 16
+
+    def reads(c):
+        part = pl.ds(pl.multiple_of(16 * c, 16), 16)
+        return [
+            pltpu.make_async_copy(source.at[:, part, :], x_ref.at[t, :, part, :], sems.at[c, t])
+            for t, source in enumerate((noisy_in, coarse_in))
+        ]
+
+    def write(c, out, place):
+        part = pl.ds(pl.multiple_of(c * 8 * n, 8 * n), 8 * n)
+        to = pl.ds(pl.multiple_of(place * 8 * n, 8 * n), 8 * n)
+        return pltpu.make_async_copy(e0_ref.at[part], out.at[to], out_sems.at[c])
+
+    def writes(c):
+        return write(c, top_out, 0) if c == 0 else write(c, bot_out, 0) if c == chunks - 1 else write(c, mid_out, c - 1)
+
+    for c in range(chunks):
+        for copy in reads(c):
+            copy.start()
+
+    def chunk(c):
+        for copy in reads(c):
+            copy.wait()
+        out = []
+        for o in range(2):
+            at = pl.ds(pl.multiple_of(16 * c + 8 * o, 8), 8)
+            fields = [x_ref[t, :, at, :].reshape(8 * nvars, cols) for t in range(2)]
+            out += embed_rows(fields, wide_ref, turn_ref, o)
+        e0_ref[pl.ds(pl.multiple_of(c * 8 * n, 8 * n), 8 * n), :] = jnp.concatenate(out, axis=0).astype(BF)
+
+        @pl.when((c > 0) & (c < chunks - 1))
+        def _():
+            write(c, mid_out, c - 1).start()
+
+    loop(chunks, chunk)
+    for c in (0, chunks - 1):
+        writes(c).start()
+    for c in range(chunks):
+        writes(c).wait()
+
+
+def rims_kernel(left_ref, right_ref, top_in, bot_in, top_out, bot_out, rim_ref, sems):
     count = left_ref.shape[0]
-    for k, ref in ((0, top_ref), (1, bot_ref)):
-
-        @pl.when(pl.program_id(0) == k)
-        def _(k=k, ref=ref):
-            ref[0 : 8 * n, :] = jnp.concatenate(rows, axis=0).astype(BF)
-            at = slice(0, 16) if k == 0 else slice(count - 16, count)
-            pick = slice(0, 8) if k == 0 else slice(8, 16)
-            rims = [r[at, :].astype(F32)[pick] for r in (left_ref, right_ref)]
-            ref[8 * n :, :] = jnp.concatenate(rims, axis=0).astype(BF)
+    at = top_out.shape[0] - 16
+    copies = []
+    for k, out in ((0, top_out), (1, bot_out)):
+        rows = slice(0, 16) if k == 0 else slice(count - 16, count)
+        pick = slice(0, 8) if k == 0 else slice(8, 16)
+        rim_ref[k] = jnp.concatenate([r[rows, :].astype(F32)[pick] for r in (left_ref, right_ref)], axis=0).astype(BF)
+        copies.append(pltpu.make_async_copy(rim_ref.at[k], out.at[pl.ds(at, 16)], sems.at[k]))
+        copies[-1].start()
+    for copy in copies:
+        copy.wait()
 
 
 def near(array):
@@ -294,37 +326,37 @@
     )(w_embed, noisy, coarse, noisy, coarse)
 
 
-def embed_edges(noisy, coarse, wide, left, right):
+def embed(noisy, coarse, wide):
     nvars, rows, cols = noisy.shape
     n = cols // 16
-    last = rows // 16 - 1
-    field = pl.BlockSpec((nvars, 16, cols), lambda k: (0, k * last, 0))
     pay = jax.ShapeDtypeStruct((8 * n + 16, 512), BF)
     return pl.pallas_call(
-        embed_edge_kernel,
-        name="embed_edges",
-        grid=(2,),
-        in_specs=[whole(wide.shape), whole(left.shape), whole(right.shape), field, field],
-        out_specs=[whole(pay.shape)] * 2,
-        out_shape=[pay, pay],
-        scratch_shapes=[pltpu.VMEM((2, cols, 128), F32)],
-    )(wide, near(left), near(right), noisy, coarse)
-
-
-def embed_middle(noisy, coarse, wide):
-    nvars, rows, cols = noisy.shape
-    n = cols // 16
-    steps = rows // 16 - 2
-    field = pl.BlockSpec((nvars, 16, cols), lambda k: (0, k + 1, 0))
+        embed_kernel,
+        name="embed",
+        in_specs=[pl.BlockSpec(memory_space=pltpu.VMEM), ANYWHERE, ANYWHERE],
+        out_specs=[ANYWHERE] * 3,
+        out_shape=[pay, jax.ShapeDtypeStruct(((rows // 2 - 16) * n, 512), BF), pay],
+        scratch_shapes=[
+            pltpu.VMEM((2, nvars, rows, cols), F32),
+            pltpu.VMEM((2, cols, 128), F32),
+            pltpu.VMEM((rows // 2 * n, 512), BF),
+            pltpu.SemaphoreType.DMA((rows // 16, 2)),
+            pltpu.SemaphoreType.DMA((rows // 16,)),
+        ],
+    )(wide, noisy, coarse)
+
+
+def add_rims(left, right, top, bot):
+    inside = pl.BlockSpec(memory_space=pltpu.VMEM)
     return pl.pallas_call(
-        embed_mid_kernel,
-        name="embed_middle",
-        grid=(steps,),
-        in_specs=[whole(wide.shape), field, field],
-        out_specs=pl.BlockSpec((8 * n, 512), lambda k: (k, 0)),
-        out_shape=jax.ShapeDtypeStruct((8 * steps * n, 512), BF),
-        scratch_shapes=[pltpu.VMEM((2, cols, 128), F32)],
-    )(wide, noisy, coarse)
+        rims_kernel,
+        name="rims",
+        in_specs=[inside, inside, ANYWHERE, ANYWHERE],
+        out_specs=[ANYWHERE] * 2,
+        out_shape=[jax.ShapeDtypeStruct(top.shape, BF)] * 2,
+        scratch_shapes=[pltpu.VMEM((2, 16, 512), BF), pltpu.SemaphoreType.DMA((2,))],
+        input_output_aliases={2: 0, 3: 1},
+    )(near(left), near(right), top, bot)
 
 
 def full_rows(x, left, right, n, size):
@@ -871,10 +903,10 @@
 
 def decoder_kernel(
     factors, bias_ref, top_ref, bot_ref, edge_h_ref, edge_taps_ref, wu1_ref, wu3_ref, w2_ref, w1_ref, wh_ref,
-    h2_own_ref, taps2_own_ref, e2_in, w3_in, wu2_in, e1_edge_in, e1_own_in, noisy_ref, noise_ref,
+    h2_own_ref, taps2_own_ref, e2_in, w3_in, wu2_in, e1_edge_in, e1_own_in, noisy_in, noise_in,
     out_ref,
     h3_ref, taps3_ref, h2_ref, taps2_ref, h1_ref, taps1_ref, turn_ref,
-    e2_ref, w3_ref, wu2_ref, e1_edge_ref, e1_own_ref, conv2_ref, conv1_ref, head_ref, g_ref, sems,
+    e2_ref, w3_ref, wu2_ref, e1_edge_ref, e1_own_ref, conv2_ref, conv1_ref, head_ref, g_ref, noisy_ref, noise_ref, sems,
     *, n, size, rows1, lat,
 ):
     rows2 = rows1 // 2
@@ -893,6 +925,8 @@
             taps2=(taps2_own_ref, taps2_ref.at[pl.ds(4, inner)]),
             e1_edge=(e1_edge_in, e1_edge_ref),
             e1_own=(e1_own_in, e1_own_ref),
+            noisy=(noisy_in, noisy_ref),
+            noise=(noise_in, noise_ref),
         )
         flags = ends(lat)
         fill_conv1(conv1_ref, w1_ref)
@@ -958,20 +992,26 @@
 
         chunk = divisor(rows2 - 2, 6)
         steps = (rows2 - 2) // chunk
+        inner_chunk = steps // 2
+
+        def order(c):
+            return jnp.where(c == 0, inner_chunk, jnp.where(c <= inner_chunk, c - 1, c))
+
         fetch.wait("e1_own")
+        first(inner_chunk * chunk, chunk)
         for ro in range(2):
             lay(ro, 0, flags[0])
             lay(ro, 1)
             lay(ro, rows2)
             lay(ro, rows2 + 1, flags[1])
-        first(0, chunk)
 
         def both(c):
-            behind((c - 1) * chunk, chunk)
-            first(c * chunk, chunk)
+            behind(order(c - 1) * chunk, chunk)
+            first(order(c) * chunk, chunk)
 
         loop(steps - 1, lambda c: both(c + 1))
-        behind((steps - 1) * chunk, chunk)
+        behind(order(steps - 1) * chunk, chunk)
+        fetch.wait("noisy", "noise")
 
     pl.when(step == 0)(prepare)
 
@@ -983,8 +1023,9 @@
     nvars, _, cols = noisy_ref.shape
     for o in range(2):
         part = eps[o * 64 : (o + 1) * 64].reshape(nvars, 8, cols)
-        rows = slice(o * 8, (o + 1) * 8)
-        out_ref[:, rows, :] = factors[0] * noisy_ref[:, rows, :] - factors[1] * part + factors[2] * noise_ref[:, rows, :]
+        rows = pl.ds(pl.multiple_of(jnp.maximum(step - 1, 0) * 16 + o * 8, 8), 8)
+        new = factors[0] * noisy_ref[:, rows, :] - factors[1] * part + factors[2] * noise_ref[:, rows, :]
+        out_ref[:, o * 8 : (o + 1) * 8, :] = new
 
     i = jnp.minimum(step, last) * 4
     acc = conv1(taps1_ref, i, 4, conv1_ref)
@@ -1013,7 +1054,7 @@
         functools.partial(decoder_kernel, n=n, size=size, rows1=rows1, lat=lat_count),
         name="decoder",
         grid=(rows1 // 8 + 1,),
-        in_specs=[smem] + [inside] * 10 + [ANYWHERE] * 7 + [field, field],
+        in_specs=[smem] + [inside] * 10 + [ANYWHERE] * 9,
         out_specs=field,
         out_shape=jax.ShapeDtypeStruct(noisy.shape, F32),
         scratch_shapes=[
@@ -1028,7 +1069,7 @@
         ]
         + [vmem(x.shape, BF) for x in late]
         + [vmem((1536, 256), BF), vmem((1024, 256), BF), vmem((1024, 512), BF), vmem((4 * size, 1024), BF)]
-        + [pltpu.SemaphoreType.DMA((8,))],
+        + [vmem(noisy.shape, F32), vmem(noisy.shape, F32), pltpu.SemaphoreType.DMA((10,))],
     )(
         factors, biases, near(top), near(bot), edge_h, edge_taps, wu1, wu3, w2, w1.T, wh.T,
         h2, taps2, e2, *late, noisy, step_noise,
@@ -1059,7 +1100,7 @@
     wide, left, right = embed_strips(noisy, coarse, w_embed)
     rhalo = shift(left, "lon", -1, True)
     lhalo = shift(right, "lon", 1, True)
-    mid = embed_middle(noisy, coarse, wide)
+    top, mid, bot = embed(noisy, coarse, wide)
 
     temb = time_embed(timestep, w_time)
     factors = update_factors(timestep)
@@ -1069,7 +1110,7 @@
         [jnp.tile(temb[s : s + w], 512 // w) * (1.0 if i == 3 else 0.5) for i, (s, w) in enumerate(zip(starts, widths))]
     )
 
-    top, bot = embed_edges(noisy, coarse, wide, lhalo, rhalo)
+    top, bot = add_rims(lhalo, rhalo, top, bot)
     from_top = shift(bot, "lat", 1, False)
     from_bot = shift(top, "lat", -1, False)
     e1_own, d1, taps2, edge_h, edge_taps, conv1_w, conv2_w = encoder_own(

time: 114 us -> 110 us (0.965)
  Pallas kernels: 67.7 us -> 64.4 us
    pallas_call x2, Pallas kernels: 9 us -> 7.02 us  [the longest x1 6.39 us: embed(): pl.pallas_call(embed_kernel, name='embed', in_specs=[pl.BlockSpec(memory_...]
    pallas_call x1, Pallas kernels: 21.3 us -> 19.9 us  [decoder(): pl.pallas_call(functools.partial(decoder_kernel, n=n, size=size, rows1=ro...]
  transfers between devices with their start and end apart: 7 -> 7, of which waited for: 1 -> 1; matrix products, arithmetic and copies ran while one was open for 3% -> 3% of each run, Pallas kernels for 22% -> 23%
where the time goes in v3:
time: 110 us; the launch traced here: 109 us
  Pallas kernels  64.4 us (59%)
  starting transfers between devices  19.9 us (18%)
  blocking collectives  12.6 us (11%)
  waiting for transfers between devices  8.05 us (7%)
  local copies, waits for them, and re-layouts  1.78 us (2%)
  between operations  1.39 us (1%)
    pallas_call x1, Pallas kernels, decoder(): pl.pallas_call(functools.partial(decoder_kernel, n=n, size=size, rows1=ro...  19.9 us
    ppermute x6, starting transfers between devices, shift(): return lax.ppermute(array, axis, pairs)  16.4 us
    all_to_all x1, blocking collectives, body(): got = lax.all_to_all(sent, 'lon', split_axis=0, concat_axis=0, tiled=True)  12.6 us
    pallas_call x1, Pallas kernels, encoder(): pl.pallas_call(functools.partial(encoder_kernel, n=n, size=size, rows1=ro...  12 us
    pallas_call x1, Pallas kernels, encoder_own(): pl.pallas_call(functools.partial(encoder_own_kernel, n=n, size=size), nam...  10 us
    pallas_call x1, Pallas kernels, decoder_own(): pl.pallas_call(functools.partial(decoder_own_kernel, size=size), name='de...  8.62 us
    all_to_all x1, waiting for transfers between devices, body(): lax.all_to_all(out.reshape(groups, each * size, 512), 'lon', split_axis=0...  8.03 us
    pallas_call x1, Pallas kernels, embed(): pl.pallas_call(embed_kernel, name='embed', in_specs=[pl.BlockSpec(memory_...  6.39 us
  transfers between devices with their start and end apart: 7, of which 1 were waited for; matrix products, arithmetic and copies ran while one was open for 3% of the time, Pallas kernels for 23%

profile of v3, /device:TPU:1, one launch (start us, length us, event | category | flops | bytes accessed | tf_op | source)
XLA Modules:
  0.0 109.4 jit_solution(6779847758964307012)
XLA Ops:
  0.0 3.0 %embed_strips.1 = (bf16[512,512]{1,0:T(8,128)(2,1)}, bf16[64,512]{1,0:T(8,128)(2,1)}, bf16[64,512]{1,0:T(8,128)(2,1)}) custom-call(bf16[64,64]{1,0:T(8,128)(2,1)} %w_ref.1, f32[8,128,384]{2,1,0:T(8,128)} %noisy_in.3, f32[8,128,384]{2,1,0:T(8,128)} %coarse_in.1, f32[8,128,384]{2,1,0:T(8,128)} %noisy_in.3, f32[8,128,384]{2,1,0:T(8,128)} %coarse_in.1), custom_call_target="tpu_custom_call" | custom-call | tf_op jit(solution)/shard_map/embed_strips/pallas_call | solution.py:318
  3.0 2.0 %collective-permute-start = (bf16[64,512]{1,0:T(8,128)(2,1)}, bf16[64,512]{1,0:T(8,128)(2,1)S(1)}, u32[]{:S(2)}, u32[]{:S(2)}) collective-permute-start(bf16[64,512]{1,0:T(8,128)(2,1)} %get-tuple-element.30), channel_id=1, source_target_pairs={{0,1},{1,2},{2,3},{3,4},{4,5},{5,6},{6,7},{7,0},{8,9},{9,10},{10,1... | collective-permute-start | bytes 196616 | tf_op jit(solution)/shard_map/ppermute | solution.py:1085
  5.0 3.0 %collective-permute-start.1 = (bf16[64,512]{1,0:T(8,128)(2,1)}, bf16[64,512]{1,0:T(8,128)(2,1)S(1)}, u32[]{:S(2)}, u32[]{:S(2)}) collective-permute-start(bf16[64,512]{1,0:T(8,128)(2,1)} %get-tuple-element.31), channel_id=1, source_target_pairs={{0,7},{1,0},{2,1},{3,2},{4,3},{5,4},{6,5},{7,6},{8,15},{9,8},{10,9... | collective-permute-start | bytes 196616 | tf_op jit(solution)/shard_map/ppermute | solution.py:1085
  8.8 0.5 convolution_reduce_fusion
  9.3 0.1 slice_multiply_fusion
  9.6 0.1 mul.158
  9.6 0.1 mul.143
  9.7 6.4 %embed.1 = (bf16[208,512]{1,0:T(8,128)(2,1)}, bf16[1152,512]{1,0:T(8,128)(2,1)}, bf16[208,512]{1,0:T(8,128)(2,1)}) custom-call(bf16[512,512]{1,0:T(8,128)(2,1)} %get-tuple-element.32.wide_ref, f32[8,128,384]{2,1,0:T(8,128)} %noisy_in.3, f32[8,128,384]{2,1,0:T(8,128)} %coarse_in.1), custom_call_target="tpu_custom_call" | custom-call | tf_op jit(solution)/shard_map/embed/pallas_call | solution.py:333
  16.1 0.6 rims.1
  16.8 4.2 %collective-permute-start.2 = (bf16[208,512]{1,0:T(8,128)(2,1)}, bf16[208,512]{1,0:T(8,128)(2,1)S(1)}, u32[]{:S(2)}, u32[]{:S(2)}) collective-permute-start(bf16[208,512]{1,0:T(8,128)(2,1)} %get-tuple-element.35.bot_ref), channel_id=1, source_target_pairs={{0,8},{8,16},{16,24},{1,9},{9,17},{17,25},{2,10},{10,18},{18,26},{... | collective-permute-start | bytes 638984 | tf_op jit(solution)/shard_map/ppermute | solution.py:1085
  21.0 1.9 %collective-permute-start.3 = (bf16[208,512]{1,0:T(8,128)(2,1)}, bf16[208,512]{1,0:T(8,128)(2,1)S(1)}, u32[]{:S(2)}, u32[]{:S(2)}) collective-permute-start(bf16[208,512]{1,0:T(8,128)(2,1)} %get-tuple-element.36.top_ref), channel_id=1, source_target_pairs={{8,0},{16,8},{24,16},{9,1},{17,9},{25,17},{10,2},{18,10},{26,18},{... | collective-permute-start | bytes 638984 | tf_op jit(solution)/shard_map/ppermute | solution.py:1085
  23.0 0.6 stack.25.bias_ref
  23.6 10.0 %encoder_own.1 = (bf16[2,30,32,512]{3,2,1,0:T(8,128)(2,1)}, bf16[30,32,512]{2,1,0:T(8,128)(2,1)}, bf16[30,6,32,128]{3,2,1,0:T(8,128)(2,1)}, bf16[2,4,32,512]{3,2...) custom-call(f32[7,512]{1,0:T(8,128)} %stack.25.bias_ref, ...), custom_call_target="tpu_custom_call" | custom-call | tf_op jit(solution)/shard_map/encoder_own/pallas_call | solution.py:483
  33.7 12.0 %encoder.1 = (bf16[2,4,32,512]{3,2,1,0:T(8,128)(2,1)}, bf16[36,32,512]{2,1,0:T(8,128)(2,1)}, bf16[16,32,512]{2,1,0:T(8,128)(2,1)}, bf16[8,40,512]{2,1,0:T(8,128)(2,1)}) custom-call(f32[7,512]{1,0:T(8,128)} %stack.25.bias_ref, bf16[208,512]{1,0:T(8,128)(2,1)S(1)} %collective-permute-done.2.top_ref, bf16[208,512]{1,0:T(8,128)(2,1)S(1)} %collective-permute-done.3.bot_ref, ...), custom_call_target="tpu_custom_call" | custom-call | tf_op jit(solution)/shard_map/encoder/pallas_call | solution.py:644
  45.6 12.6 %all_to_all.10.x_ref = bf16[8,40,512]{2,1,0:T(8,128)(2,1)S(1)} all-to-all(bf16[8,40,512]{2,1,0:T(8,128)(2,1)} %get-tuple-element.44), channel_id=1, replica_groups=mesh['lat'=4,'lon'=8] {'lon'}, dimensions={0} | all-to-all | bytes 655360 | tf_op jit(solution)/shard_map/all_to_all | solution.py:1126
  58.3 3.8 %attention.1 = (bf16[8,1,32,512]{3,2,1,0:T(8,128)(2,1)}, bf16[16,32,512]{2,1,0:T(8,128)(2,1)}) custom-call(bf16[8,40,512]{2,1,0:T(8,128)(2,1)S(1)} %all_to_all.10.x_ref, f32[7,512]{1,0:T(8,128)} %stack.25.bias_ref, bf16[512,1536]{1,0:T(8,128)(2,1)} %wqkv_ref.1, bf16[16,32,512]{2,1,0:T(8,128)(2,1)} %get-tuple-element.45.e3_in, bf16[512,512]{1,0:T(8,128)(2,1)} %wout_in.1), custom_call_target="tpu_custom_call" | custom-call | tf_op jit(solution)/shard_map/attention/pallas_call | solution.py:736
  62.1 3.4 %all-to-all-start.1 = ((bf16[8,32,512]{2,1,0:T(8,128)(2,1)}), bf16[8,32,512]{2,1,0:T(8,128)(2,1)S(1)}, u32[]{:S(2)}, u32[]{:S(2)}) async-start(bf16[8,32,512]{2,1,0:T(8,128)(2,1)} %bitcast.35), calls=%async_computation.1 | async-start | bytes 524288 | tf_op jit(solution)/shard_map/all_to_all | solution.py:1128
  65.9 0.9 fusion.9
  66.8 8.0 %all-to-all-done.1.a4_ref = bf16[8,32,512]{2,1,0:T(8,128)(2,1)S(1)} async-done(((bf16[8,32,512]{2,1,0:T(8,128)(2,1)}), bf16[8,32,512]{2,1,0:T(8,128)(2,1)S(1)}, u32[]{:S(2)}, u32[]{:S(2)}) %all-to-all-start.1) | async-done | bytes 262176 | tf_op jit(solution)/shard_map/all_to_all | solution.py:1128
  74.8 3.4 %collective-permute-start.4 = (bf16[3,32,512]{2,1,0:T(8,128)(2,1)S(1)}, bf16[3,32,512]{2,1,0:T(8,128)(2,1)S(1)}, u32[]{:S(2)}, u32[]{:S(2)}) collective-permute-start(bf16[3,32,512]{2,1,0:T(8,128)(2,1)S(1)} %pad_maximum_fusion), channel_id=1, source_target_pairs={{0,8},{8,16},{16,24},{1,9},{9,17},{17,25},{2,10},{10,18},{18,26},{... | collective-permute-start | bytes 294920 | tf_op jit(solution)/shard_map/ppermute | solution.py:1085
  78.2 1.9 %collective-permute-start.5 = (bf16[3,32,512]{2,1,0:T(8,128)(2,1)S(1)}, bf16[3,32,512]{2,1,0:T(8,128)(2,1)S(1)}, u32[]{:S(2)}, u32[]{:S(2)}) collective-permute-start(bf16[3,32,512]{2,1,0:T(8,128)(2,1)S(1)} %pad_maximum_fusion.1), channel_id=1, source_target_pairs={{8,0},{16,8},{24,16},{9,1},{17,9},{25,17},{10,2},{18,10},{26,18},{... | collective-permute-start | bytes 294920 | tf_op jit(solution)/shard_map/ppermute | solution.py:1085
  80.2 0.6 pad_maximum_fusion.2.factors
  80.7 8.6 %decoder_own.1 = (bf16[28,32,512]{2,1,0:T(8,128)(2,1)}, bf16[28,6,32,128]{3,2,1,0:T(8,128)(2,1)}, bf16[2,32,512]{2,1,0:T(8,128)(2,1)}, bf16[4,8,32,128]{3,2,1,0:T(8,128)(2,1)}) custom-call(f32[7,512]{1,0:T(8,128)} %stack.25.bias_ref, bf16[8,32,512]{2,1,0:T(8,128)(2,1)S(1)} %all-to-all-done.1.a4_ref, bf16[16,32,512]{2,1,0:T(8,128)(2,1)} %get-tuple-element.47.e3_ref, ...), custom_call_target="tpu_custom_call" | custom-call | tf_op jit(solution)/shard_map/decoder_own/pallas_call | solution.py:879
  89.4 19.9 %decoder.1 = f32[8,128,384]{2,1,0:T(8,128)} custom-call(f32[3]{0:T(128)} %pad_maximum_fusion.2.factors, f32[7,512]{1,0:T(8,128)} %stack.25.bias_ref, bf16[3,32,512]{2,1,0:T(8,128)(2,1)S(1)} %collective-permute-done.4.top_ref, bf16[3,32,512]{2,1,0:T(8,128)(2,1)S(1)} %collective-permute-done.5.bot_ref, bf16[2,32,512]{2,1,0:T(8,128)(2,1)} %get-tuple-element.49.edge_h_ref, ...), custom_call_target="tpu_custom_call" | custom-call | tf_op jit(solution)/shard_map/decoder/pallas_call | solution.py:1053
  (25 shorter events, 0.4 us)
Async XLA Ops:
  0.0 8.8 %copy-start = (f32[128,1408]{1,0:T(8,128)S(1)}, f32[128,1408]{1,0:T(8,128)}, u32[]{:S(2)}) copy-start(f32[128,1408]{1,0:T(8,128)} %param.25) | copy-start | bytes 2162692
  3.0 13.1 %collective-permute-start = (bf16[64,512]{1,0:T(8,128)(2,1)}, bf16[64,512]{1,0:T(8,128)(2,1)S(1)}, u32[]{:S(2)}, u32[]{:S(2)}) collective-permute-start(bf16[64,512]{1,0:T(8,128)(2,1)} %get-tuple-element.30), channel_id=1, source_target_pairs={{0,1},{1,2},{2,3},{3,4},{4,5},{5,6},{6,7},{7,0},{8,9},{9,10},{10,1... | collective-permute-start | bytes 196616 | tf_op jit(solution)/shard_map/ppermute | solution.py:1085
  5.0 11.1 %collective-permute-start.1 = (bf16[64,512]{1,0:T(8,128)(2,1)}, bf16[64,512]{1,0:T(8,128)(2,1)S(1)}, u32[]{:S(2)}, u32[]{:S(2)}) collective-permute-start(bf16[64,512]{1,0:T(8,128)(2,1)} %get-tuple-element.31), channel_id=1, source_target_pairs={{0,7},{1,0},{2,1},{3,2},{4,3},{5,4},{6,5},{7,6},{8,15},{9,8},{10,9... | collective-permute-start | bytes 196616 | tf_op jit(solution)/shard_map/ppermute | solution.py:1085
  16.8 16.9 %collective-permute-start.2 = (bf16[208,512]{1,0:T(8,128)(2,1)}, bf16[208,512]{1,0:T(8,128)(2,1)S(1)}, u32[]{:S(2)}, u32[]{:S(2)}) collective-permute-start(bf16[208,512]{1,0:T(8,128)(2,1)} %get-tuple-element.35.bot_ref), channel_id=1, source_target_pairs={{0,8},{8,16},{16,24},{1,9},{9,17},{17,25},{2,10},{10,18},{18,26},{... | collective-permute-start | bytes 638984 | tf_op jit(solution)/shard_map/ppermute | solution.py:1085
  21.0 12.7 %collective-permute-start.3 = (bf16[208,512]{1,0:T(8,128)(2,1)}, bf16[208,512]{1,0:T(8,128)(2,1)S(1)}, u32[]{:S(2)}, u32[]{:S(2)}) collective-permute-start(bf16[208,512]{1,0:T(8,128)(2,1)} %get-tuple-element.36.top_ref), channel_id=1, source_target_pairs={{8,0},{16,8},{24,16},{9,1},{17,9},{25,17},{10,2},{18,10},{26,18},{... | collective-permute-start | bytes 638984 | tf_op jit(solution)/shard_map/ppermute | solution.py:1085
  62.1 12.7 %all-to-all-start.1 = ((bf16[8,32,512]{2,1,0:T(8,128)(2,1)}), bf16[8,32,512]{2,1,0:T(8,128)(2,1)S(1)}, u32[]{:S(2)}, u32[]{:S(2)}) async-start(bf16[8,32,512]{2,1,0:T(8,128)(2,1)} %bitcast.35), calls=%async_computation.1 | async-start | bytes 524288 | tf_op jit(solution)/shard_map/all_to_all | solution.py:1128
  74.8 14.5 %collective-permute-start.4 = (bf16[3,32,512]{2,1,0:T(8,128)(2,1)S(1)}, bf16[3,32,512]{2,1,0:T(8,128)(2,1)S(1)}, u32[]{:S(2)}, u32[]{:S(2)}) collective-permute-start(bf16[3,32,512]{2,1,0:T(8,128)(2,1)S(1)} %pad_maximum_fusion), channel_id=1, source_target_pairs={{0,8},{8,16},{16,24},{1,9},{9,17},{17,25},{2,10},{10,18},{18,26},{... | collective-permute-start | bytes 294920 | tf_op jit(solution)/shard_map/ppermute | solution.py:1085
  78.2 11.1 %collective-permute-start.5 = (bf16[3,32,512]{2,1,0:T(8,128)(2,1)S(1)}, bf16[3,32,512]{2,1,0:T(8,128)(2,1)S(1)}, u32[]{:S(2)}, u32[]{:S(2)}) collective-permute-start(bf16[3,32,512]{2,1,0:T(8,128)(2,1)S(1)} %pad_maximum_fusion.1), channel_id=1, source_target_pairs={{8,0},{16,8},{24,16},{9,1},{17,9},{25,17},{10,2},{18,10},{26,18},{... | collective-permute-start | bytes 294920 | tf_op jit(solution)/shard_map/ppermute | solution.py:1085

commit v4 on v3

--- a/solution.py
+++ b/solution.py
@@ -437,7 +437,7 @@
         for copy in leave(i):
             copy.start()
 
-    chunk = divisor(rows1 // 2 - 2, 6)
+    chunk = divisor(rows1 // 2 - 2, 10)
     steps = (rows1 // 2 - 2) // chunk
 
     def leave(i):
@@ -504,7 +504,7 @@
             vmem((inner, 6, size, 128), BF),
             vmem((1024, 256), BF),
             vmem((1536, 256), BF),
-            pltpu.SemaphoreType.DMA((inner // divisor(inner, 6), 4)),
+            pltpu.SemaphoreType.DMA((inner // divisor(inner, 10), 4)),
             pltpu.SemaphoreType.DMA((10,)),
         ],
     )(biases, mid, top, bot, near(lhalo), near(rhalo), w1.T, wd1, w2)
@@ -568,7 +568,7 @@
             put_taps(taps2_ref, at + j, part if inside else part * flags[side], 128)
 
     fetch.wait("conv2", "d1", "taps2", "wd2")
-    chunk2, chunk3 = divisor(rows3 + 2, 6), divisor(rows3 // 2, 4)
+    chunk2, chunk3 = divisor(rows3 + 2, 9), divisor(rows3 // 2, 4)
 
     def leave2(i):
         part = pl.ds(2 * i, 2 * chunk2)
@@ -669,7 +669,7 @@
             vmem((rows2 + 4, size, 512), BF),
             vmem((rows3, size, 512), BF),
             pltpu.SemaphoreType.DMA((15,)),
-            pltpu.SemaphoreType.DMA(((rows3 + 2) // divisor(rows3 + 2, 6),)),
+            pltpu.SemaphoreType.DMA(((rows3 + 2) // divisor(rows3 + 2, 9),)),
             pltpu.SemaphoreType.DMA((rows3 // 2 // divisor(rows3 // 2, 4),)),
         ],
     )(
@@ -902,11 +902,11 @@
 
 
 def decoder_kernel(
-    factors, bias_ref, top_ref, bot_ref, edge_h_ref, edge_taps_ref, wu1_ref, wu3_ref, w2_ref, w1_ref, wh_ref,
-    h2_own_ref, taps2_own_ref, e2_in, w3_in, wu2_in, e1_edge_in, e1_own_in, noisy_in, noise_in,
+    factors, bias_ref, top_ref, bot_ref, edge_h_ref, edge_taps_ref, wu1_ref, w2_ref, w1_ref, wh_ref,
+    wu3_in, h2_own_ref, taps2_own_ref, e2_in, w3_in, wu2_in, e1_edge_in, e1_own_in, noisy_in, noise_in,
     out_ref,
     h3_ref, taps3_ref, h2_ref, taps2_ref, h1_ref, taps1_ref, turn_ref,
-    e2_ref, w3_ref, wu2_ref, e1_edge_ref, e1_own_ref, conv2_ref, conv1_ref, head_ref, g_ref, noisy_ref, noise_ref, sems,
+    wu3_ref, e2_ref, w3_ref, wu2_ref, e1_edge_ref, e1_own_ref, conv2_ref, conv1_ref, head_ref, g_ref, noisy_ref, noise_ref, sems,
     *, n, size, rows1, lat,
 ):
     rows2 = rows1 // 2
@@ -917,6 +917,7 @@
     def prepare():
         fetch = Fetch(
             sems,
+            wu3=(wu3_in, wu3_ref),
             w3=(w3_in, w3_ref),
             e2a=(e2_in.at[pl.ds(0, 4)], e2_ref.at[pl.ds(0, 4)]),
             e2b=(e2_in.at[pl.ds(rows2, 4)], e2_ref.at[pl.ds(4, 4)]),
@@ -932,6 +933,7 @@
         fill_conv1(conv1_ref, w1_ref)
         fill_conv2(conv2_ref, w2_ref)
         fill_head(head_ref, wh_ref)
+        fetch.wait("wu3")
         mean1, mean2, mean3 = mean_matrix(64), mean_matrix(128), mean_matrix(256)
         bias3, bias2, bias1 = bias_ref[4:5, :], bias_ref[5:6, :], bias_ref[6:7, :]
 
@@ -990,7 +992,7 @@
                 for ro in range(2):
                     lay(ro, i + 2 + j)
 
-        chunk = divisor(rows2 - 2, 6)
+        chunk = divisor(rows2 - 2, 10)
         steps = (rows2 - 2) // chunk
         inner_chunk = steps // 2
 
@@ -1054,7 +1056,7 @@
         functools.partial(decoder_kernel, n=n, size=size, rows1=rows1, lat=lat_count),
         name="decoder",
         grid=(rows1 // 8 + 1,),
-        in_specs=[smem] + [inside] * 10 + [ANYWHERE] * 9,
+        in_specs=[smem] + [inside] * 9 + [ANYWHERE] * 10,
         out_specs=field,
         out_shape=jax.ShapeDtypeStruct(noisy.shape, F32),
         scratch_shapes=[
@@ -1065,13 +1067,14 @@
             vmem((2, rows2 + 2, size, 512), BF),
             vmem((2, rows2 + 2, 8, size, 128), BF),
             vmem((cols, 128), F32),
+            vmem(wu3.shape, BF),
             vmem((8, size, 512), BF),
         ]
         + [vmem(x.shape, BF) for x in late]
         + [vmem((1536, 256), BF), vmem((1024, 256), BF), vmem((1024, 512), BF), vmem((4 * size, 1024), BF)]
-        + [vmem(noisy.shape, F32), vmem(noisy.shape, F32), pltpu.SemaphoreType.DMA((10,))],
+        + [vmem(noisy.shape, F32), vmem(noisy.shape, F32), pltpu.SemaphoreType.DMA((11,))],
     )(
-        factors, biases, near(top), near(bot), edge_h, edge_taps, wu1, wu3, w2, w1.T, wh.T,
+        factors, biases, near(top), near(bot), edge_h, edge_taps, wu1, w2, w1.T, wh.T, wu3,
         h2, taps2, e2, *late, noisy, step_noise,
     )
 

time: 110 us -> 109 us (level)
  Pallas kernels: 64.4 us -> 63.1 us
where the time goes in v4:
time: 109 us; the launch traced here: 108 us
  Pallas kernels  63.1 us (58%)
  starting transfers between devices  20.1 us (18%)
  blocking collectives  12.6 us (12%)
  waiting for transfers between devices  8.05 us (7%)
  local copies, waits for them, and re-layouts  1.78 us (2%)
  between operations  1.39 us (1%)
    pallas_call x1, Pallas kernels, decoder(): pl.pallas_call(functools.partial(decoder_kernel, n=n, size=size, rows1=ro...  19.3 us
    ppermute x6, starting transfers between devices, shift(): return lax.ppermute(array, axis, pairs)  16.7 us
    all_to_all x1, blocking collectives, body(): got = lax.all_to_all(sent, 'lon', split_axis=0, concat_axis=0, tiled=True)  12.6 us
    pallas_call x1, Pallas kernels, encoder(): pl.pallas_call(functools.partial(encoder_kernel, n=n, size=size, rows1=ro...  11.6 us
    pallas_call x1, Pallas kernels, encoder_own(): pl.pallas_call(functools.partial(encoder_own_kernel, n=n, size=size), nam...  9.84 us
    pallas_call x1, Pallas kernels, decoder_own(): pl.pallas_call(functools.partial(decoder_own_kernel, size=size), name='de...  8.62 us
    all_to_all x1, waiting for transfers between devices, body(): lax.all_to_all(out.reshape(groups, each * size, 512), 'lon', split_axis=0...  8.03 us
    pallas_call x1, Pallas kernels, embed(): pl.pallas_call(embed_kernel, name='embed', in_specs=[pl.BlockSpec(memory_...  6.39 us
  transfers between devices with their start and end apart: 7, of which 1 were waited for; matrix products, arithmetic and copies ran while one was open for 3% of the time, Pallas kernels for 23%

profile of v4, /device:TPU:1, one launch (start us, length us, event | category | flops | bytes accessed | tf_op | source)
XLA Modules:
  0.0 108.4 jit_solution(12879354708960713059)
XLA Ops:
  0.0 3.0 %embed_strips.1 = (bf16[512,512]{1,0:T(8,128)(2,1)}, bf16[64,512]{1,0:T(8,128)(2,1)}, bf16[64,512]{1,0:T(8,128)(2,1)}) custom-call(bf16[64,64]{1,0:T(8,128)(2,1)} %w_ref.1, f32[8,128,384]{2,1,0:T(8,128)} %noisy_in.3, f32[8,128,384]{2,1,0:T(8,128)} %coarse_in.1, f32[8,128,384]{2,1,0:T(8,128)} %noisy_in.3, f32[8,128,384]{2,1,0:T(8,128)} %coarse_in.1), custom_call_target="tpu_custom_call" | custom-call | tf_op jit(solution)/shard_map/embed_strips/pallas_call | solution.py:318
  3.0 2.0 %collective-permute-start = (bf16[64,512]{1,0:T(8,128)(2,1)}, bf16[64,512]{1,0:T(8,128)(2,1)S(1)}, u32[]{:S(2)}, u32[]{:S(2)}) collective-permute-start(bf16[64,512]{1,0:T(8,128)(2,1)} %get-tuple-element.30), channel_id=1, source_target_pairs={{0,1},{1,2},{2,3},{3,4},{4,5},{5,6},{6,7},{7,0},{8,9},{9,10},{10,1... | collective-permute-start | bytes 196616 | tf_op jit(solution)/shard_map/ppermute | solution.py:1088
  5.0 3.0 %collective-permute-start.1 = (bf16[64,512]{1,0:T(8,128)(2,1)}, bf16[64,512]{1,0:T(8,128)(2,1)S(1)}, u32[]{:S(2)}, u32[]{:S(2)}) collective-permute-start(bf16[64,512]{1,0:T(8,128)(2,1)} %get-tuple-element.31), channel_id=1, source_target_pairs={{0,7},{1,0},{2,1},{3,2},{4,3},{5,4},{6,5},{7,6},{8,15},{9,8},{10,9... | collective-permute-start | bytes 196616 | tf_op jit(solution)/shard_map/ppermute | solution.py:1088
  8.8 0.5 convolution_reduce_fusion
  9.3 0.1 slice_multiply_fusion
  9.6 0.1 mul.158
  9.6 0.1 mul.143
  9.7 6.4 %embed.1 = (bf16[208,512]{1,0:T(8,128)(2,1)}, bf16[1152,512]{1,0:T(8,128)(2,1)}, bf16[208,512]{1,0:T(8,128)(2,1)}) custom-call(bf16[512,512]{1,0:T(8,128)(2,1)} %get-tuple-element.32.wide_ref, f32[8,128,384]{2,1,0:T(8,128)} %noisy_in.3, f32[8,128,384]{2,1,0:T(8,128)} %coarse_in.1), custom_call_target="tpu_custom_call" | custom-call | tf_op jit(solution)/shard_map/embed/pallas_call | solution.py:333
  16.1 0.6 rims.1
  16.8 4.2 %collective-permute-start.2 = (bf16[208,512]{1,0:T(8,128)(2,1)}, bf16[208,512]{1,0:T(8,128)(2,1)S(1)}, u32[]{:S(2)}, u32[]{:S(2)}) collective-permute-start(bf16[208,512]{1,0:T(8,128)(2,1)} %get-tuple-element.35.bot_ref), channel_id=1, source_target_pairs={{0,8},{8,16},{16,24},{1,9},{9,17},{17,25},{2,10},{10,18},{18,26},{... | collective-permute-start | bytes 638984 | tf_op jit(solution)/shard_map/ppermute | solution.py:1088
  21.0 1.9 %collective-permute-start.3 = (bf16[208,512]{1,0:T(8,128)(2,1)}, bf16[208,512]{1,0:T(8,128)(2,1)S(1)}, u32[]{:S(2)}, u32[]{:S(2)}) collective-permute-start(bf16[208,512]{1,0:T(8,128)(2,1)} %get-tuple-element.36.top_ref), channel_id=1, source_target_pairs={{8,0},{16,8},{24,16},{9,1},{17,9},{25,17},{10,2},{18,10},{26,18},{... | collective-permute-start | bytes 638984 | tf_op jit(solution)/shard_map/ppermute | solution.py:1088
  23.0 0.6 stack.25.bias_ref
  23.6 9.8 %encoder_own.1 = (bf16[2,30,32,512]{3,2,1,0:T(8,128)(2,1)}, bf16[30,32,512]{2,1,0:T(8,128)(2,1)}, bf16[30,6,32,128]{3,2,1,0:T(8,128)(2,1)}, bf16[2,4,32,512]{3,2...) custom-call(f32[7,512]{1,0:T(8,128)} %stack.25.bias_ref, ...), custom_call_target="tpu_custom_call" | custom-call | tf_op jit(solution)/shard_map/encoder_own/pallas_call | solution.py:483
  33.5 11.6 %encoder.1 = (bf16[2,4,32,512]{3,2,1,0:T(8,128)(2,1)}, bf16[36,32,512]{2,1,0:T(8,128)(2,1)}, bf16[16,32,512]{2,1,0:T(8,128)(2,1)}, bf16[8,40,512]{2,1,0:T(8,128)(2,1)}) custom-call(f32[7,512]{1,0:T(8,128)} %stack.25.bias_ref, bf16[208,512]{1,0:T(8,128)(2,1)S(1)} %collective-permute-done.2.top_ref, bf16[208,512]{1,0:T(8,128)(2,1)S(1)} %collective-permute-done.3.bot_ref, ...), custom_call_target="tpu_custom_call" | custom-call | tf_op jit(solution)/shard_map/encoder/pallas_call | solution.py:644
  45.1 12.6 %all_to_all.10.x_ref = bf16[8,40,512]{2,1,0:T(8,128)(2,1)S(1)} all-to-all(bf16[8,40,512]{2,1,0:T(8,128)(2,1)} %get-tuple-element.44), channel_id=1, replica_groups=mesh['lat'=4,'lon'=8] {'lon'}, dimensions={0} | all-to-all | bytes 655360 | tf_op jit(solution)/shard_map/all_to_all | solution.py:1129
  57.7 3.8 %attention.1 = (bf16[8,1,32,512]{3,2,1,0:T(8,128)(2,1)}, bf16[16,32,512]{2,1,0:T(8,128)(2,1)}) custom-call(bf16[8,40,512]{2,1,0:T(8,128)(2,1)S(1)} %all_to_all.10.x_ref, f32[7,512]{1,0:T(8,128)} %stack.25.bias_ref, bf16[512,1536]{1,0:T(8,128)(2,1)} %wqkv_ref.1, bf16[16,32,512]{2,1,0:T(8,128)(2,1)} %get-tuple-element.45.e3_in, bf16[512,512]{1,0:T(8,128)(2,1)} %wout_in.1), custom_call_target="tpu_custom_call" | custom-call | tf_op jit(solution)/shard_map/attention/pallas_call | solution.py:736
  61.5 3.4 %all-to-all-start.1 = ((bf16[8,32,512]{2,1,0:T(8,128)(2,1)}), bf16[8,32,512]{2,1,0:T(8,128)(2,1)S(1)}, u32[]{:S(2)}, u32[]{:S(2)}) async-start(bf16[8,32,512]{2,1,0:T(8,128)(2,1)} %bitcast.35), calls=%async_computation.1 | async-start | bytes 524288 | tf_op jit(solution)/shard_map/all_to_all | solution.py:1131
  65.3 0.9 fusion.9
  66.2 8.0 %all-to-all-done.1.a4_ref = bf16[8,32,512]{2,1,0:T(8,128)(2,1)S(1)} async-done(((bf16[8,32,512]{2,1,0:T(8,128)(2,1)}), bf16[8,32,512]{2,1,0:T(8,128)(2,1)S(1)}, u32[]{:S(2)}, u32[]{:S(2)}) %all-to-all-start.1) | async-done | bytes 262176 | tf_op jit(solution)/shard_map/all_to_all | solution.py:1131
  74.3 3.4 %collective-permute-start.4 = (bf16[3,32,512]{2,1,0:T(8,128)(2,1)S(1)}, bf16[3,32,512]{2,1,0:T(8,128)(2,1)S(1)}, u32[]{:S(2)}, u32[]{:S(2)}) collective-permute-start(bf16[3,32,512]{2,1,0:T(8,128)(2,1)S(1)} %pad_maximum_fusion), channel_id=1, source_target_pairs={{0,8},{8,16},{16,24},{1,9},{9,17},{17,25},{2,10},{10,18},{18,26},{... | collective-permute-start | bytes 294920 | tf_op jit(solution)/shard_map/ppermute | solution.py:1088
  77.7 2.1 %collective-permute-start.5 = (bf16[3,32,512]{2,1,0:T(8,128)(2,1)S(1)}, bf16[3,32,512]{2,1,0:T(8,128)(2,1)S(1)}, u32[]{:S(2)}, u32[]{:S(2)}) collective-permute-start(bf16[3,32,512]{2,1,0:T(8,128)(2,1)S(1)} %pad_maximum_fusion.1), channel_id=1, source_target_pairs={{8,0},{16,8},{24,16},{9,1},{17,9},{25,17},{10,2},{18,10},{26,18},{... | collective-permute-start | bytes 294920 | tf_op jit(solution)/shard_map/ppermute | solution.py:1088
  79.8 0.6 pad_maximum_fusion.2.factors
  80.4 8.6 %decoder_own.1 = (bf16[28,32,512]{2,1,0:T(8,128)(2,1)}, bf16[28,6,32,128]{3,2,1,0:T(8,128)(2,1)}, bf16[2,32,512]{2,1,0:T(8,128)(2,1)}, bf16[4,8,32,128]{3,2,1,0:T(8,128)(2,1)}) custom-call(f32[7,512]{1,0:T(8,128)} %stack.25.bias_ref, bf16[8,32,512]{2,1,0:T(8,128)(2,1)S(1)} %all-to-all-done.1.a4_ref, bf16[16,32,512]{2,1,0:T(8,128)(2,1)} %get-tuple-element.47.e3_ref, ...), custom_call_target="tpu_custom_call" | custom-call | tf_op jit(solution)/shard_map/decoder_own/pallas_call | solution.py:879
  89.0 19.3 %decoder.1 = f32[8,128,384]{2,1,0:T(8,128)} custom-call(f32[3]{0:T(128)} %pad_maximum_fusion.2.factors, f32[7,512]{1,0:T(8,128)} %stack.25.bias_ref, bf16[3,32,512]{2,1,0:T(8,128)(2,1)S(1)} %collective-permute-done.4.top_ref, bf16[3,32,512]{2,1,0:T(8,128)(2,1)S(1)} %collective-permute-done.5.bot_ref, bf16[2,32,512]{2,1,0:T(8,128)(2,1)} %get-tuple-element.49.edge_h_ref, ...), custom_call_target="tpu_custom_call" | custom-call | tf_op jit(solution)/shard_map/decoder/pallas_call | solution.py:1055
  (25 shorter events, 0.4 us)
Async XLA Ops:
  0.0 8.8 %copy-start = (f32[128,1408]{1,0:T(8,128)S(1)}, f32[128,1408]{1,0:T(8,128)}, u32[]{:S(2)}) copy-start(f32[128,1408]{1,0:T(8,128)} %param.25) | copy-start | bytes 2162692
  3.0 13.1 %collective-permute-start = (bf16[64,512]{1,0:T(8,128)(2,1)}, bf16[64,512]{1,0:T(8,128)(2,1)S(1)}, u32[]{:S(2)}, u32[]{:S(2)}) collective-permute-start(bf16[64,512]{1,0:T(8,128)(2,1)} %get-tuple-element.30), channel_id=1, source_target_pairs={{0,1},{1,2},{2,3},{3,4},{4,5},{5,6},{6,7},{7,0},{8,9},{9,10},{10,1... | collective-permute-start | bytes 196616 | tf_op jit(solution)/shard_map/ppermute | solution.py:1088
  5.0 11.1 %collective-permute-start.1 = (bf16[64,512]{1,0:T(8,128)(2,1)}, bf16[64,512]{1,0:T(8,128)(2,1)S(1)}, u32[]{:S(2)}, u32[]{:S(2)}) collective-permute-start(bf16[64,512]{1,0:T(8,128)(2,1)} %get-tuple-element.31), channel_id=1, source_target_pairs={{0,7},{1,0},{2,1},{3,2},{4,3},{5,4},{6,5},{7,6},{8,15},{9,8},{10,9... | collective-permute-start | bytes 196616 | tf_op jit(solution)/shard_map/ppermute | solution.py:1088
  16.8 16.7 %collective-permute-start.2 = (bf16[208,512]{1,0:T(8,128)(2,1)}, bf16[208,512]{1,0:T(8,128)(2,1)S(1)}, u32[]{:S(2)}, u32[]{:S(2)}) collective-permute-start(bf16[208,512]{1,0:T(8,128)(2,1)} %get-tuple-element.35.bot_ref), channel_id=1, source_target_pairs={{0,8},{8,16},{16,24},{1,9},{9,17},{17,25},{2,10},{10,18},{18,26},{... | collective-permute-start | bytes 638984 | tf_op jit(solution)/shard_map/ppermute | solution.py:1088
  21.0 12.5 %collective-permute-start.3 = (bf16[208,512]{1,0:T(8,128)(2,1)}, bf16[208,512]{1,0:T(8,128)(2,1)S(1)}, u32[]{:S(2)}, u32[]{:S(2)}) collective-permute-start(bf16[208,512]{1,0:T(8,128)(2,1)} %get-tuple-element.36.top_ref), channel_id=1, source_target_pairs={{8,0},{16,8},{24,16},{9,1},{17,9},{25,17},{10,2},{18,10},{26,18},{... | collective-permute-start | bytes 638984 | tf_op jit(solution)/shard_map/ppermute | solution.py:1088
  61.5 12.7 %all-to-all-start.1 = ((bf16[8,32,512]{2,1,0:T(8,128)(2,1)}), bf16[8,32,512]{2,1,0:T(8,128)(2,1)S(1)}, u32[]{:S(2)}, u32[]{:S(2)}) async-start(bf16[8,32,512]{2,1,0:T(8,128)(2,1)} %bitcast.35), calls=%async_computation.1 | async-start | bytes 524288 | tf_op jit(solution)/shard_map/all_to_all | solution.py:1131
  74.3 14.7 %collective-permute-start.4 = (bf16[3,32,512]{2,1,0:T(8,128)(2,1)S(1)}, bf16[3,32,512]{2,1,0:T(8,128)(2,1)S(1)}, u32[]{:S(2)}, u32[]{:S(2)}) collective-permute-start(bf16[3,32,512]{2,1,0:T(8,128)(2,1)S(1)} %pad_maximum_fusion), channel_id=1, source_target_pairs={{0,8},{8,16},{16,24},{1,9},{9,17},{17,25},{2,10},{10,18},{18,26},{... | collective-permute-start | bytes 294920 | tf_op jit(solution)/shard_map/ppermute | solution.py:1088
  77.7 11.3 %collective-permute-start.5 = (bf16[3,32,512]{2,1,0:T(8,128)(2,1)S(1)}, bf16[3,32,512]{2,1,0:T(8,128)(2,1)S(1)}, u32[]{:S(2)}, u32[]{:S(2)}) collective-permute-start(bf16[3,32,512]{2,1,0:T(8,128)(2,1)S(1)} %pad_maximum_fusion.1), channel_id=1, source_target_pairs={{8,0},{16,8},{24,16},{9,1},{17,9},{25,17},{10,2},{18,10},{26,18},{... | collective-permute-start | bytes 294920 | tf_op jit(solution)/shard_map/ppermute | solution.py:1088

commit v5 on v4

--- a/solution.py
+++ b/solution.py
@@ -568,7 +568,7 @@
             put_taps(taps2_ref, at + j, part if inside else part * flags[side], 128)
 
     fetch.wait("conv2", "d1", "taps2", "wd2")
-    chunk2, chunk3 = divisor(rows3 + 2, 9), divisor(rows3 // 2, 4)
+    chunk2, chunk3 = divisor(rows3 + 2, 9), divisor(rows3 // 2, 8)
 
     def leave2(i):
         part = pl.ds(2 * i, 2 * chunk2)
@@ -670,7 +670,7 @@
             vmem((rows3, size, 512), BF),
             pltpu.SemaphoreType.DMA((15,)),
             pltpu.SemaphoreType.DMA(((rows3 + 2) // divisor(rows3 + 2, 9),)),
-            pltpu.SemaphoreType.DMA((rows3 // 2 // divisor(rows3 // 2, 4),)),
+            pltpu.SemaphoreType.DMA((rows3 // 2 // divisor(rows3 // 2, 8),)),
         ],
     )(
         biases, near(top), near(bot), wd1,

time: 109 us -> 109 us (level)
  no operation moved by 1% of the time
where the time goes in v5:
time: 109 us; the launch traced here: 108 us
  Pallas kernels  62.7 us (58%)
  starting transfers between devices  20.2 us (19%)
  blocking collectives  12.6 us (12%)
  waiting for transfers between devices  7.85 us (7%)
  local copies, waits for them, and re-layouts  1.78 us (2%)
  between operations  1.39 us (1%)
    pallas_call x1, Pallas kernels, decoder(): pl.pallas_call(functools.partial(decoder_kernel, n=n, size=size, rows1=ro...  19.2 us
    ppermute x6, starting transfers between devices, shift(): return lax.ppermute(array, axis, pairs)  16.6 us
    all_to_all x1, blocking collectives, body(): got = lax.all_to_all(sent, 'lon', split_axis=0, concat_axis=0, tiled=True)  12.6 us
    pallas_call x1, Pallas kernels, encoder(): pl.pallas_call(functools.partial(encoder_kernel, n=n, size=size, rows1=ro...  11.2 us
    pallas_call x1, Pallas kernels, encoder_own(): pl.pallas_call(functools.partial(encoder_own_kernel, n=n, size=size), nam...  9.84 us
    pallas_call x1, Pallas kernels, decoder_own(): pl.pallas_call(functools.partial(decoder_own_kernel, size=size), name='de...  8.62 us
    all_to_all x1, waiting for transfers between devices, body(): lax.all_to_all(out.reshape(groups, each * size, 512), 'lon', split_axis=0...  7.84 us
    pallas_call x1, Pallas kernels, embed(): pl.pallas_call(embed_kernel, name='embed', in_specs=[pl.BlockSpec(memory_...  6.39 us
  transfers between devices with their start and end apart: 7, of which 1 were waited for; matrix products, arithmetic and copies ran while one was open for 3% of the time, Pallas kernels for 23%

profile of v5, /device:TPU:1, one launch (start us, length us, event | category | flops | bytes accessed | tf_op | source)
XLA Modules:
  0.0 108.0 jit_solution(12937814441720879985)
XLA Ops:
  0.0 3.0 %embed_strips.1 = (bf16[512,512]{1,0:T(8,128)(2,1)}, bf16[64,512]{1,0:T(8,128)(2,1)}, bf16[64,512]{1,0:T(8,128)(2,1)}) custom-call(bf16[64,64]{1,0:T(8,128)(2,1)} %w_ref.1, f32[8,128,384]{2,1,0:T(8,128)} %noisy_in.3, f32[8,128,384]{2,1,0:T(8,128)} %coarse_in.1, f32[8,128,384]{2,1,0:T(8,128)} %noisy_in.3, f32[8,128,384]{2,1,0:T(8,128)} %coarse_in.1), custom_call_target="tpu_custom_call" | custom-call | tf_op jit(solution)/shard_map/embed_strips/pallas_call | solution.py:318
  3.0 2.0 %collective-permute-start = (bf16[64,512]{1,0:T(8,128)(2,1)}, bf16[64,512]{1,0:T(8,128)(2,1)S(1)}, u32[]{:S(2)}, u32[]{:S(2)}) collective-permute-start(bf16[64,512]{1,0:T(8,128)(2,1)} %get-tuple-element.30), channel_id=1, source_target_pairs={{0,1},{1,2},{2,3},{3,4},{4,5},{5,6},{6,7},{7,0},{8,9},{9,10},{10,1... | collective-permute-start | bytes 196616 | tf_op jit(solution)/shard_map/ppermute | solution.py:1088
  5.0 3.0 %collective-permute-start.1 = (bf16[64,512]{1,0:T(8,128)(2,1)}, bf16[64,512]{1,0:T(8,128)(2,1)S(1)}, u32[]{:S(2)}, u32[]{:S(2)}) collective-permute-start(bf16[64,512]{1,0:T(8,128)(2,1)} %get-tuple-element.31), channel_id=1, source_target_pairs={{0,7},{1,0},{2,1},{3,2},{4,3},{5,4},{6,5},{7,6},{8,15},{9,8},{10,9... | collective-permute-start | bytes 196616 | tf_op jit(solution)/shard_map/ppermute | solution.py:1088
  8.8 0.5 convolution_reduce_fusion
  9.3 0.1 slice_multiply_fusion
  9.6 0.1 mul.158
  9.6 0.1 mul.143
  9.7 6.4 %embed.1 = (bf16[208,512]{1,0:T(8,128)(2,1)}, bf16[1152,512]{1,0:T(8,128)(2,1)}, bf16[208,512]{1,0:T(8,128)(2,1)}) custom-call(bf16[512,512]{1,0:T(8,128)(2,1)} %get-tuple-element.32.wide_ref, f32[8,128,384]{2,1,0:T(8,128)} %noisy_in.3, f32[8,128,384]{2,1,0:T(8,128)} %coarse_in.1), custom_call_target="tpu_custom_call" | custom-call | tf_op jit(solution)/shard_map/embed/pallas_call | solution.py:333
  16.1 0.6 rims.1
  16.8 4.2 %collective-permute-start.2 = (bf16[208,512]{1,0:T(8,128)(2,1)}, bf16[208,512]{1,0:T(8,128)(2,1)S(1)}, u32[]{:S(2)}, u32[]{:S(2)}) collective-permute-start(bf16[208,512]{1,0:T(8,128)(2,1)} %get-tuple-element.35.bot_ref), channel_id=1, source_target_pairs={{0,8},{8,16},{16,24},{1,9},{9,17},{17,25},{2,10},{10,18},{18,26},{... | collective-permute-start | bytes 638984 | tf_op jit(solution)/shard_map/ppermute | solution.py:1088
  21.0 1.9 %collective-permute-start.3 = (bf16[208,512]{1,0:T(8,128)(2,1)}, bf16[208,512]{1,0:T(8,128)(2,1)S(1)}, u32[]{:S(2)}, u32[]{:S(2)}) collective-permute-start(bf16[208,512]{1,0:T(8,128)(2,1)} %get-tuple-element.36.top_ref), channel_id=1, source_target_pairs={{8,0},{16,8},{24,16},{9,1},{17,9},{25,17},{10,2},{18,10},{26,18},{... | collective-permute-start | bytes 638984 | tf_op jit(solution)/shard_map/ppermute | solution.py:1088
  23.0 0.6 stack.25.bias_ref
  23.6 9.8 %encoder_own.1 = (bf16[2,30,32,512]{3,2,1,0:T(8,128)(2,1)}, bf16[30,32,512]{2,1,0:T(8,128)(2,1)}, bf16[30,6,32,128]{3,2,1,0:T(8,128)(2,1)}, bf16[2,4,32,512]{3,2...) custom-call(f32[7,512]{1,0:T(8,128)} %stack.25.bias_ref, ...), custom_call_target="tpu_custom_call" | custom-call | tf_op jit(solution)/shard_map/encoder_own/pallas_call | solution.py:483
  33.5 11.2 %encoder.1 = (bf16[2,4,32,512]{3,2,1,0:T(8,128)(2,1)}, bf16[36,32,512]{2,1,0:T(8,128)(2,1)}, bf16[16,32,512]{2,1,0:T(8,128)(2,1)}, bf16[8,40,512]{2,1,0:T(8,128)(2,1)}) custom-call(f32[7,512]{1,0:T(8,128)} %stack.25.bias_ref, bf16[208,512]{1,0:T(8,128)(2,1)S(1)} %collective-permute-done.2.top_ref, bf16[208,512]{1,0:T(8,128)(2,1)S(1)} %collective-permute-done.3.bot_ref, ...), custom_call_target="tpu_custom_call" | custom-call | tf_op jit(solution)/shard_map/encoder/pallas_call | solution.py:644
  44.7 12.6 %all_to_all.10.x_ref = bf16[8,40,512]{2,1,0:T(8,128)(2,1)S(1)} all-to-all(bf16[8,40,512]{2,1,0:T(8,128)(2,1)} %get-tuple-element.44), channel_id=1, replica_groups=mesh['lat'=4,'lon'=8] {'lon'}, dimensions={0} | all-to-all | bytes 655360 | tf_op jit(solution)/shard_map/all_to_all | solution.py:1129
  57.3 3.8 %attention.1 = (bf16[8,1,32,512]{3,2,1,0:T(8,128)(2,1)}, bf16[16,32,512]{2,1,0:T(8,128)(2,1)}) custom-call(bf16[8,40,512]{2,1,0:T(8,128)(2,1)S(1)} %all_to_all.10.x_ref, f32[7,512]{1,0:T(8,128)} %stack.25.bias_ref, bf16[512,1536]{1,0:T(8,128)(2,1)} %wqkv_ref.1, bf16[16,32,512]{2,1,0:T(8,128)(2,1)} %get-tuple-element.45.e3_in, bf16[512,512]{1,0:T(8,128)(2,1)} %wout_in.1), custom_call_target="tpu_custom_call" | custom-call | tf_op jit(solution)/shard_map/attention/pallas_call | solution.py:736
  61.1 3.6 %all-to-all-start.1 = ((bf16[8,32,512]{2,1,0:T(8,128)(2,1)}), bf16[8,32,512]{2,1,0:T(8,128)(2,1)S(1)}, u32[]{:S(2)}, u32[]{:S(2)}) async-start(bf16[8,32,512]{2,1,0:T(8,128)(2,1)} %bitcast.35), calls=%async_computation.1 | async-start | bytes 524288 | tf_op jit(solution)/shard_map/all_to_all | solution.py:1131
  65.1 0.9 fusion.9
  66.0 7.8 %all-to-all-done.1.a4_ref = bf16[8,32,512]{2,1,0:T(8,128)(2,1)S(1)} async-done(((bf16[8,32,512]{2,1,0:T(8,128)(2,1)}), bf16[8,32,512]{2,1,0:T(8,128)(2,1)S(1)}, u32[]{:S(2)}, u32[]{:S(2)}) %all-to-all-start.1) | async-done | bytes 262176 | tf_op jit(solution)/shard_map/all_to_all | solution.py:1131
  73.9 3.5 %collective-permute-start.4 = (bf16[3,32,512]{2,1,0:T(8,128)(2,1)S(1)}, bf16[3,32,512]{2,1,0:T(8,128)(2,1)S(1)}, u32[]{:S(2)}, u32[]{:S(2)}) collective-permute-start(bf16[3,32,512]{2,1,0:T(8,128)(2,1)S(1)} %pad_maximum_fusion), channel_id=1, source_target_pairs={{0,8},{8,16},{16,24},{1,9},{9,17},{17,25},{2,10},{10,18},{18,26},{... | collective-permute-start | bytes 294920 | tf_op jit(solution)/shard_map/ppermute | solution.py:1088
  77.4 1.9 %collective-permute-start.5 = (bf16[3,32,512]{2,1,0:T(8,128)(2,1)S(1)}, bf16[3,32,512]{2,1,0:T(8,128)(2,1)S(1)}, u32[]{:S(2)}, u32[]{:S(2)}) collective-permute-start(bf16[3,32,512]{2,1,0:T(8,128)(2,1)S(1)} %pad_maximum_fusion.1), channel_id=1, source_target_pairs={{8,0},{16,8},{24,16},{9,1},{17,9},{25,17},{10,2},{18,10},{26,18},{... | collective-permute-start | bytes 294920 | tf_op jit(solution)/shard_map/ppermute | solution.py:1088
  79.4 0.6 pad_maximum_fusion.2.factors
  79.9 8.6 %decoder_own.1 = (bf16[28,32,512]{2,1,0:T(8,128)(2,1)}, bf16[28,6,32,128]{3,2,1,0:T(8,128)(2,1)}, bf16[2,32,512]{2,1,0:T(8,128)(2,1)}, bf16[4,8,32,128]{3,2,1,0:T(8,128)(2,1)}) custom-call(f32[7,512]{1,0:T(8,128)} %stack.25.bias_ref, bf16[8,32,512]{2,1,0:T(8,128)(2,1)S(1)} %all-to-all-done.1.a4_ref, bf16[16,32,512]{2,1,0:T(8,128)(2,1)} %get-tuple-element.47.e3_ref, ...), custom_call_target="tpu_custom_call" | custom-call | tf_op jit(solution)/shard_map/decoder_own/pallas_call | solution.py:879
  88.6 19.2 %decoder.1 = f32[8,128,384]{2,1,0:T(8,128)} custom-call(f32[3]{0:T(128)} %pad_maximum_fusion.2.factors, f32[7,512]{1,0:T(8,128)} %stack.25.bias_ref, bf16[3,32,512]{2,1,0:T(8,128)(2,1)S(1)} %collective-permute-done.4.top_ref, bf16[3,32,512]{2,1,0:T(8,128)(2,1)S(1)} %collective-permute-done.5.bot_ref, bf16[2,32,512]{2,1,0:T(8,128)(2,1)} %get-tuple-element.49.edge_h_ref, ...), custom_call_target="tpu_custom_call" | custom-call | tf_op jit(solution)/shard_map/decoder/pallas_call | solution.py:1055
  (25 shorter events, 0.4 us)
Async XLA Ops:
  0.0 8.8 %copy-start = (f32[128,1408]{1,0:T(8,128)S(1)}, f32[128,1408]{1,0:T(8,128)}, u32[]{:S(2)}) copy-start(f32[128,1408]{1,0:T(8,128)} %param.25) | copy-start | bytes 2162692
  3.0 13.1 %collective-permute-start = (bf16[64,512]{1,0:T(8,128)(2,1)}, bf16[64,512]{1,0:T(8,128)(2,1)S(1)}, u32[]{:S(2)}, u32[]{:S(2)}) collective-permute-start(bf16[64,512]{1,0:T(8,128)(2,1)} %get-tuple-element.30), channel_id=1, source_target_pairs={{0,1},{1,2},{2,3},{3,4},{4,5},{5,6},{6,7},{7,0},{8,9},{9,10},{10,1... | collective-permute-start | bytes 196616 | tf_op jit(solution)/shard_map/ppermute | solution.py:1088
  5.0 11.1 %collective-permute-start.1 = (bf16[64,512]{1,0:T(8,128)(2,1)}, bf16[64,512]{1,0:T(8,128)(2,1)S(1)}, u32[]{:S(2)}, u32[]{:S(2)}) collective-permute-start(bf16[64,512]{1,0:T(8,128)(2,1)} %get-tuple-element.31), channel_id=1, source_target_pairs={{0,7},{1,0},{2,1},{3,2},{4,3},{5,4},{6,5},{7,6},{8,15},{9,8},{10,9... | collective-permute-start | bytes 196616 | tf_op jit(solution)/shard_map/ppermute | solution.py:1088
  16.8 16.7 %collective-permute-start.2 = (bf16[208,512]{1,0:T(8,128)(2,1)}, bf16[208,512]{1,0:T(8,128)(2,1)S(1)}, u32[]{:S(2)}, u32[]{:S(2)}) collective-permute-start(bf16[208,512]{1,0:T(8,128)(2,1)} %get-tuple-element.35.bot_ref), channel_id=1, source_target_pairs={{0,8},{8,16},{16,24},{1,9},{9,17},{17,25},{2,10},{10,18},{18,26},{... | collective-permute-start | bytes 638984 | tf_op jit(solution)/shard_map/ppermute | solution.py:1088
  21.0 12.5 %collective-permute-start.3 = (bf16[208,512]{1,0:T(8,128)(2,1)}, bf16[208,512]{1,0:T(8,128)(2,1)S(1)}, u32[]{:S(2)}, u32[]{:S(2)}) collective-permute-start(bf16[208,512]{1,0:T(8,128)(2,1)} %get-tuple-element.36.top_ref), channel_id=1, source_target_pairs={{8,0},{16,8},{24,16},{9,1},{17,9},{25,17},{10,2},{18,10},{26,18},{... | collective-permute-start | bytes 638984 | tf_op jit(solution)/shard_map/ppermute | solution.py:1088
  61.1 12.7 %all-to-all-start.1 = ((bf16[8,32,512]{2,1,0:T(8,128)(2,1)}), bf16[8,32,512]{2,1,0:T(8,128)(2,1)S(1)}, u32[]{:S(2)}, u32[]{:S(2)}) async-start(bf16[8,32,512]{2,1,0:T(8,128)(2,1)} %bitcast.35), calls=%async_computation.1 | async-start | bytes 524288 | tf_op jit(solution)/shard_map/all_to_all | solution.py:1131
  73.9 14.7 %collective-permute-start.4 = (bf16[3,32,512]{2,1,0:T(8,128)(2,1)S(1)}, bf16[3,32,512]{2,1,0:T(8,128)(2,1)S(1)}, u32[]{:S(2)}, u32[]{:S(2)}) collective-permute-start(bf16[3,32,512]{2,1,0:T(8,128)(2,1)S(1)} %pad_maximum_fusion), channel_id=1, source_target_pairs={{0,8},{8,16},{16,24},{1,9},{9,17},{17,25},{2,10},{10,18},{18,26},{... | collective-permute-start | bytes 294920 | tf_op jit(solution)/shard_map/ppermute | solution.py:1088
  77.4 11.1 %collective-permute-start.5 = (bf16[3,32,512]{2,1,0:T(8,128)(2,1)S(1)}, bf16[3,32,512]{2,1,0:T(8,128)(2,1)S(1)}, u32[]{:S(2)}, u32[]{:S(2)}) collective-permute-start(bf16[3,32,512]{2,1,0:T(8,128)(2,1)S(1)} %pad_maximum_fusion.1), channel_id=1, source_target_pairs={{8,0},{16,8},{24,16},{9,1},{17,9},{25,17},{10,2},{18,10},{26,18},{... | collective-permute-start | bytes 294920 | tf_op jit(solution)/shard_map/ppermute | solution.py:1088
